TPU v7x, 32 devices: a whole 2x2x4 slice. The times are simulated.
32 devices in a mesh: batch: 2 (over x), seq: 16 (over z, y, core).
Axes of the slice: x: 2, y: 2, z: 4, core: 2. Of those that a mesh axis runs over, the one named last changes fastest.
Arguments:
- tokens: bfloat16 [4, 1024, 1024], P('batch', 'seq'), may hold values from -6 to 6
- segments: int32 [4, 1024], P('batch', 'seq'), may hold values from 0 to 3, never falling along the last dimension, each value on 1 to 512 neighbouring positions
- norm1_gain: float32 [1024], replicated, may hold values from 0.5 to 1.5
- norm1_bias: float32 [1024], replicated, may hold values from -3 to 3
- decay_log: float32 [1024, 64], replicated, may hold values from -1 to 0.5
- decay_freq: float32 [1024, 64], replicated, may hold values from 0 to 192
- input_re: float32 [1024, 64], replicated, may hold values from -6 to 6
- input_im: float32 [1024, 64], replicated, may hold values from -6 to 6
- output_re: float32 [1024, 64], replicated, may hold values from -6 to 6
- output_im: float32 [1024, 64], replicated, may hold values from -6 to 6
- step_log: float32 [1024], replicated, may hold values from -9.2 to -2.3
- skip_gain: float32 [1024], replicated, may hold values from -6 to 6
- glu_weight: bfloat16 [1024, 2048], replicated, may hold values from -0.1875 to 0.1875
- glu_bias: float32 [2048], replicated, may hold values from -3 to 3
- norm2_gain: float32 [1024], replicated, may hold values from 0.5 to 1.5
- norm2_bias: float32 [1024], replicated, may hold values from -3 to 3
- ffn_in: bfloat16 [1024, 4096], replicated, may hold values from -0.1875 to 0.1875
- ffn_in_bias: float32 [4096], replicated, may hold values from -3 to 3
- ffn_out: bfloat16 [4096, 1024], replicated, may hold values from -0.09375 to 0.09375
- ffn_out_bias: float32 [1024], replicated, may hold values from -3 to 3
- cotangent: bfloat16 [4, 1024, 1024], P('batch', 'seq'), may hold values from -6 to 6
Outputs:
- result: bfloat16 [4, 1024, 1024], P('batch', 'seq')
- grad_tokens: bfloat16 [4, 1024, 1024], P('batch', 'seq')
- grad_norm1_gain: float32 [1024], replicated
- grad_norm1_bias: float32 [1024], replicated
- grad_decay_log: float32 [1024, 64], replicated
- grad_decay_freq: float32 [1024, 64], replicated
- grad_input_re: float32 [1024, 64], replicated
- grad_input_im: float32 [1024, 64], replicated
- grad_output_re: float32 [1024, 64], replicated
- grad_output_im: float32 [1024, 64], replicated
- grad_step_log: float32 [1024], replicated
- grad_skip_gain: float32 [1024], replicated
- grad_glu_weight: float32 [1024, 2048], P('seq')
- grad_glu_bias: float32 [2048], replicated
- grad_norm2_gain: float32 [1024], replicated
- grad_norm2_bias: float32 [1024], replicated
- grad_ffn_in: float32 [1024, 4096], P('seq')
- grad_ffn_in_bias: float32 [4096], replicated
- grad_ffn_out: float32 [4096, 1024], P('seq')
- grad_ffn_out_bias: float32 [1024], replicated
Inputs may be any that keep to these rules, and one draw needn't show every extreme that they name: `segments`: within each context the document numbers start at 0 and never fall from one position to the next; a document holds at most min(512, 1021) positions.
All inputs are finite; a program needn't handle non-finite values.
Results may differ from a plain program's by a relative error of at most 0.0061.
Values sent between devices are 32-bit elements; how exact they have to be, the bound alone decides.
No kernel may reach another device: no remote copies, remote signals or barrier semaphores. Data moves between devices by JAX's collectives and lax.ppermute only.
A program may use at most 640 MiB of HBM per device.

v0:
```python
import jax
import jax.numpy as jnp
from jax import lax
from jax.sharding import PartitionSpec as P

SUB = 64


EPSILON = 1e-05


def passed_along(block, axis, distance):
    devices = range(lax.axis_size(axis))
    route = [(i - distance, i) for i in devices if i - distance in devices]
    return lax.ppermute(block, axis, route)


def carried_in(value, axis, join, neutral, backward):
    count, mine = (lax.axis_size(axis), lax.axis_index(axis))
    pieces = jax.tree.map(lambda part: lax.all_gather(part, axis), value)
    if backward:
        pieces = jax.tree.map(lambda part: part[::-1], pieces)
        mine = count - 1 - mine
    total = jax.tree.map(
        lambda part, zero: jnp.full_like(part, 0) + jnp.asarray(zero, part.dtype), value, neutral
    )

    def turn(position, total):
        longer = join(total, jax.tree.map(lambda part: part[position], pieces))
        return jax.tree.map(lambda new, old: jnp.where(position < mine, new, old), longer, total)

    return lax.fori_loop(0, count - 1, turn, total)


def mode_power(delta_re, delta_im, exponent):
    magnitude = jnp.exp(exponent * delta_re)
    phase_angle = exponent * delta_im
    return (magnitude * jnp.cos(phase_angle), magnitude * jnp.sin(phase_angle))


def mode_tables(params, span_len):
    decay_log, decay_freq, input_re, input_im, output_re, output_im, step_log = params
    step_size = jnp.exp(step_log)[:, None]
    real_part = -jnp.exp(decay_log)
    delta_re = step_size * real_part
    delta_im = step_size * decay_freq
    lam_re, lam_im = mode_power(delta_re, delta_im, 1.0)
    denominator = real_part * real_part + decay_freq * decay_freq
    num_re = lam_re - 1.0
    rat_re = (num_re * real_part + lam_im * decay_freq) / denominator
    rat_im = (lam_im * real_part - num_re * decay_freq) / denominator
    bbar_re = rat_re * input_re - rat_im * input_im
    bbar_im = rat_re * input_im + rat_im * input_re
    prod_re = output_re * bbar_re - output_im * bbar_im
    prod_im = output_re * bbar_im + output_im * bbar_re
    power_steps = jnp.arange(span_len, dtype=jnp.float32)[:, None, None]
    pow_re, pow_im = mode_power(delta_re, delta_im, power_steps)
    kernel = 2.0 * jnp.sum(prod_re * pow_re - prod_im * pow_im, axis=2)
    next_re, next_im = mode_power(delta_re, delta_im, power_steps + 1.0)
    cl_re = output_re * next_re - output_im * next_im
    cl_im = output_re * next_im + output_im * next_re
    back_re, back_im = mode_power(delta_re, delta_im, span_len - 1.0 - power_steps)
    lb_re = back_re * bbar_re - back_im * bbar_im
    lb_im = back_re * bbar_im + back_im * bbar_re
    lag_index = jnp.arange(span_len)
    onehot = (
        lag_index[:, None, None] == lag_index[None, :, None] - lag_index[None, None, :]
    ).astype(jnp.float32)
    toeplitz = jnp.einsum("ktj,kh->tjh", onehot, kernel, precision=lax.Precision.HIGHEST)
    return (toeplitz, cl_re, cl_im, lb_re, lb_im, delta_re, delta_im)


def block_step(consts, state_re, state_im, previous, block_in, block_seg):
    toeplitz, cl_re, cl_im, lb_re, lb_im, delta_re, delta_im = consts
    span_len = block_seg.shape[1]
    lag_index = jnp.arange(span_len)
    causal = lag_index[:, None] >= lag_index[None, :]
    same_doc = ((block_seg[:, :, None] == block_seg[:, None, :]) & causal[None]).astype(jnp.float32)
    weights = toeplitz[None] * same_doc[:, :, :, None]
    local_sum = jnp.einsum("ctjh,cjh->cth", weights, block_in, precision=lax.Precision.HIGHEST)
    carried = (block_seg == previous[:, None]).astype(jnp.float32)
    injected = 2.0 * (
        jnp.einsum("thn,chn->cth", cl_re, state_re, precision=lax.Precision.HIGHEST)
        - jnp.einsum("thn,chn->cth", cl_im, state_im, precision=lax.Precision.HIGHEST)
    )
    outcome = local_sum + carried[:, :, None] * injected
    tail_mask = (block_seg == block_seg[:, -1:]).astype(jnp.float32)
    masked = block_in * tail_mask[:, :, None]
    new_re = jnp.einsum("jhn,cjh->chn", lb_re, masked, precision=lax.Precision.HIGHEST)
    new_im = jnp.einsum("jhn,cjh->chn", lb_im, masked, precision=lax.Precision.HIGHEST)
    keep_state = carried[:, -1][:, None, None]
    full_re, full_im = mode_power(delta_re, delta_im, float(span_len))
    new_re = new_re + keep_state * (full_re * state_re - full_im * state_im)
    new_im = new_im + keep_state * (full_re * state_im + full_im * state_re)
    return (outcome, new_re, new_im, block_seg[:, -1])


def piece_local(consts, mixin, segments):
    contexts = mixin.shape[0]
    state_re = jnp.zeros((contexts,) + consts[1].shape[1:], jnp.float32)
    state_im = jnp.zeros((contexts,) + consts[1].shape[1:], jnp.float32)
    previous = -jnp.ones((contexts,), jnp.int32)
    outcome, state_re, state_im, previous = block_step(
        consts, state_re, state_im, previous, mixin, segments
    )
    pieces = [outcome]
    return (jnp.concatenate(pieces, axis=1), state_re, state_im)


def piece_inject(consts, enter_re, enter_im, carried, through):
    toeplitz, cl_re, cl_im, lb_re, lb_im, delta_re, delta_im = consts
    piece_len = carried.shape[1]
    shift_re, shift_im = mode_power(delta_re, delta_im, float(0))
    cur_re = shift_re * enter_re - shift_im * enter_im
    cur_im = shift_re * enter_im + shift_im * enter_re
    pieces = [
        2.0
        * (
            jnp.einsum("thn,chn->cth", cl_re, cur_re, precision=lax.Precision.HIGHEST)
            - jnp.einsum("thn,chn->cth", cl_im, cur_im, precision=lax.Precision.HIGHEST)
        )
    ]
    injected = jnp.concatenate(pieces, axis=1) * carried[:, :, None]
    total_re, total_im = mode_power(delta_re, delta_im, float(piece_len))
    gate_open = through[:, None, None]
    pass_re = gate_open * (total_re * enter_re - total_im * enter_im)
    pass_im = gate_open * (total_re * enter_im + total_im * enter_re)
    return (injected, pass_re, pass_im)


def layer_norm(values, norm_gain, norm_shift):
    centre = values - jnp.mean(values, axis=-1, keepdims=True)
    spread = jnp.mean(centre * centre, axis=-1, keepdims=True)
    return centre * lax.rsqrt(spread + EPSILON) * norm_gain + norm_shift


def gelu_exact(values):
    return jax.nn.gelu(values, approximate=False)


def gated_unit(values):
    middle = values.shape[-1] // 2
    return values[..., :middle] * jax.nn.sigmoid(values[..., middle:])


def inner_rows(left, right):
    return lax.dot_general(
        left, right, (((0,), (0,)), ((), ())), preferred_element_type=jnp.float32
    )


def outer_cols(left, right):
    return lax.dot_general(
        left, right, (((1,), (1,)), ((), ())), preferred_element_type=jnp.float32
    )


def on_device(
    tokens,
    segments,
    norm1_gain,
    norm1_bias,
    decay_log,
    decay_freq,
    input_re,
    input_im,
    output_re,
    output_im,
    step_log,
    skip_gain,
    glu_weight,
    glu_bias,
    norm2_gain,
    norm2_bias,
    ffn_in,
    ffn_in_bias,
    ffn_out,
    ffn_out_bias,
    cotangent,
):
    contexts, piece_len, feature_count = tokens.shape
    row_count = contexts * piece_len
    params = (decay_log, decay_freq, input_re, input_im, output_re, output_im, step_log)
    floats = tokens.astype(jnp.float32)
    normed, norm1_pull = jax.vjp(layer_norm, floats, norm1_gain, norm1_bias)
    before = passed_along(segments[:, -1] + 1, "seq", 1) - 1
    through = (segments[:, -1] == before).astype(jnp.float32)
    carried = (segments == before[:, None]).astype(jnp.float32)
    consts, modes_pull = jax.vjp(lambda packed: mode_tables(packed, SUB), params)
    delta_re, delta_im = (consts[5], consts[6])

    def local_part(const_in, mixin):
        return piece_local(const_in, mixin, segments)

    def inject_part(const_in, enter_re, enter_im):
        return piece_inject(const_in, enter_re, enter_im, carried, through)

    def carry_combine(earlier, following):
        fac_re, fac_im = mode_power(delta_re, delta_im, piece_len * following[3][:, None, None])
        gate_open = following[2][:, None, None]
        return (
            following[0] + gate_open * (fac_re * earlier[0] - fac_im * earlier[1]),
            following[1] + gate_open * (fac_re * earlier[1] + fac_im * earlier[0]),
            earlier[2] * following[2],
            earlier[3] + following[3],
        )

    def adjoint_combine(earlier, following):
        fac_re, fac_im = mode_power(delta_re, -delta_im, piece_len * following[3][:, None, None])
        gate_open = following[2][:, None, None]
        return (
            following[0] + gate_open * (fac_re * earlier[0] - fac_im * earlier[1]),
            following[1] + gate_open * (fac_re * earlier[1] + fac_im * earlier[0]),
            earlier[2] * following[2],
            earlier[3] + following[3],
        )

    local_vals = local_part(consts, normed)
    local_out, loc_re, loc_im = local_vals
    zero_state = jnp.zeros_like(loc_re)
    unit_flags = jnp.ones_like(through)
    identity = (zero_state, zero_state, unit_flags, jnp.zeros_like(through))
    entering = carried_in(
        (loc_re, loc_im, through, unit_flags), "seq", carry_combine, identity, False
    )
    inject_vals, inject_pull = jax.vjp(inject_part, consts, entering[0], entering[1])
    mixed_out = local_out + inject_vals[0] + skip_gain * normed
    activation, gelu1_pull = jax.vjp(gelu_exact, mixed_out)
    flat_act = activation.astype(jnp.bfloat16).reshape(row_count, feature_count)
    glu_pre = jnp.dot(flat_act, glu_weight, preferred_element_type=jnp.float32) + glu_bias
    glu_out, glu_pull = jax.vjp(gated_unit, glu_pre)
    hidden = floats + glu_out.reshape(contexts, piece_len, feature_count)
    normed_two, norm2_pull = jax.vjp(layer_norm, hidden, norm2_gain, norm2_bias)
    norm2_low = normed_two.astype(jnp.bfloat16).reshape(row_count, feature_count)
    ffn_pre = jnp.dot(norm2_low, ffn_in, preferred_element_type=jnp.float32) + ffn_in_bias
    ffn_act, gelu2_pull = jax.vjp(gelu_exact, ffn_pre)
    ffn_low = ffn_act.astype(jnp.bfloat16)
    ffn_res = jnp.dot(ffn_low, ffn_out, preferred_element_type=jnp.float32) + ffn_out_bias
    result = (hidden + ffn_res.reshape(contexts, piece_len, feature_count)).astype(jnp.bfloat16)
    upstream = cotangent.astype(jnp.float32)
    up_low = cotangent.reshape(row_count, feature_count)
    grad_ffn_low = outer_cols(up_low, ffn_out)
    term_out = inner_rows(ffn_low, up_low)
    bias_out = jnp.sum(upstream, axis=(0, 1))
    pre_low = gelu2_pull(grad_ffn_low)[0].astype(jnp.bfloat16)
    grad_normed_two = outer_cols(pre_low, ffn_in)
    term_in = inner_rows(norm2_low, pre_low)
    bias_in = jnp.sum(pre_low.astype(jnp.float32), axis=0)
    hidden_part, grad_g2, grad_b2 = norm2_pull(
        grad_normed_two.reshape(contexts, piece_len, feature_count)
    )
    grad_hidden = upstream + hidden_part
    glu_low = glu_pull(grad_hidden.reshape(row_count, feature_count))[0].astype(jnp.bfloat16)
    grad_act = outer_cols(glu_low, glu_weight)
    term_glu = inner_rows(flat_act, glu_low)
    bias_glu = jnp.sum(glu_low.astype(jnp.float32), axis=0)
    grad_mixed = gelu1_pull(grad_act.reshape(contexts, piece_len, feature_count))[0]
    const_inject, adjoint_re, adjoint_im = inject_pull((grad_mixed, zero_state, zero_state))
    leaving = carried_in(
        (adjoint_re, adjoint_im, through, unit_flags), "seq", adjoint_combine, identity, True
    )
    const_pass = inject_pull((jnp.zeros_like(grad_mixed), leaving[0], leaving[1]))[0]
    const_local, grad_normed = jax.vjp(local_part, consts, normed)[1](
        (grad_mixed, leaving[0], leaving[1])
    )
    grad_normed = grad_normed + skip_gain * grad_mixed
    grad_skip = jnp.sum(grad_mixed * normed, axis=(0, 1))
    const_total = jax.tree.map(
        lambda part_one, part_two, part_three: part_one + part_two + part_three,
        const_inject,
        const_pass,
        const_local,
    )
    grad_params = modes_pull(const_total)[0]
    token_part, grad_g1, grad_b1 = norm1_pull(grad_normed)
    grad_tokens = (grad_hidden + token_part).astype(jnp.bfloat16)
    small = lax.psum(
        (
            grad_g1,
            grad_b1,
            grad_params[0],
            grad_params[1],
            grad_params[2],
            grad_params[3],
            grad_params[4],
            grad_params[5],
            grad_params[6],
            grad_skip,
            bias_glu,
            grad_g2,
            grad_b2,
            bias_in,
            bias_out,
        ),
        ("batch", "seq"),
    )
    row_sums = (
        lax.psum_scatter(term_glu, "seq", scatter_dimension=0, tiled=True),
        lax.psum_scatter(term_in, "seq", scatter_dimension=0, tiled=True),
        lax.psum_scatter(term_out, "seq", scatter_dimension=0, tiled=True),
    )
    weight_grads = lax.psum((row_sums[0], row_sums[1], row_sums[2]), "batch")
    return (
        result,
        grad_tokens,
        small[0],
        small[1],
        small[2],
        small[3],
        small[4],
        small[5],
        small[6],
        small[7],
        small[8],
        small[9],
        weight_grads[0],
        small[10],
        small[11],
        small[12],
        weight_grads[1],
        small[13],
        weight_grads[2],
        small[14],
    )


def solution(mesh):
    in_specs = (
        P("batch", "seq", None),
        P("batch", "seq"),
        P(),
        P(),
        P(),
        P(),
        P(),
        P(),
        P(),
        P(),
        P(),
        P(),
        P(),
        P(),
        P(),
        P(),
        P(),
        P(),
        P(),
        P(),
        P("batch", "seq", None),
    )
    out_specs = (
        P("batch", "seq", None),
        P("batch", "seq", None),
        P(),
        P(),
        P(),
        P(),
        P(),
        P(),
        P(),
        P(),
        P(),
        P(),
        P("seq", None),
        P(),
        P(),
        P(),
        P("seq", None),
        P(),
        P("seq", None),
        P(),
    )
    return jax.shard_map(
        on_device, mesh=mesh, in_specs=in_specs, out_specs=out_specs, check_vma=False
    )
```

profile of v0, /device:TPU:0, one launch (start us, length us, event | category | flops | bytes accessed | tf_op | source)
XLA Modules:
  0.0 3829.2 jit_solution(5729478146738589993)
XLA Ops:
  29.2 156.2 %fusion.63 = f32[1024,2,64]{2,1,0:T(2,128)} fusion(f32[2,64,1024]{1,0,2:T(2,128)S(1)} %copy.332, f32[1024,64]{1,0:T(8,128)} %copy.331, f32[1024,64]{1,0:T(8,128)} %copy.330, f32[64]{0:T(128)S(1)} %get-tuple-element.828, f32[1024,64]{1,0:T(8,128)} %copy.320, f32[1024,64]{1,0:T(8,128)S(1)} %copy.319), kind=kOutput, calls=%fused_computation.117 | convolution fusion | flops 130023424 | bytes 2097408 | tf_op jit(solution)/shard_map/jhn,cjh->chn/dot_general | solution.py:90
  185.4 155.8 %fusion.61 = f32[1024,2,64]{2,1,0:T(2,128)} fusion(f32[2,64,1024]{1,0,2:T(2,128)S(1)} %copy.332, f32[1024,64]{1,0:T(8,128)S(1)} %copy-done.56, f32[1024,64]{1,0:T(8,128)S(1)} %copy-done.58, f32[64]{0:T(128)S(1)} %get-tuple-element.828, f32[1024,64]{1,0:T(8,128)} %copy.320, f32[1024,64]{1,0:T(8,128)S(1)} %copy.319), kind=kOutput, calls=%fused_computation.115 | convolution fusion | flops 130023424 | bytes 2097408 | tf_op jit(solution)/shard_map/jhn,cjh->chn/dot_general | solution.py:89
  350.2 131.5 %subtract_reduce_fusion = f32[64,1024]{0,1:T(8,128)S(1)} fusion(f32[1024,64]{1,0:T(8,128)S(1)} %copy.321, f32[1024,64]{1,0:T(8,128)} %copy.320, f32[1024,64]{1,0:T(8,128)S(1)} %copy.319, f32[1024,64]{1,0:T(8,128)S(1)} %copy.318), kind=kLoop, calls=%fused_computation.107 | loop fusion | flops 33488896 | bytes 1310720 | tf_op jit(solution)/shard_map/jvp()/reduce_sum | solution.py:58
  481.9 176.8 %fusion.89 = f32[1024,2,64]{2,1,0:T(2,128)S(1)} fusion(f32[1024,64]{1,0:T(8,128)} %copy.325, f32[64]{0:T(128)S(1)} %get-tuple-element.829, f32[1024,64]{1,0:T(8,128)} %copy.324, f32[1024,64]{1,0:T(8,128)} %copy.320, f32[1024,64]{1,0:T(8,128)S(1)} %copy.319), kind=kOutput, calls=%fused_computation.143 | convolution fusion | flops 130023424 | bytes 1573120 | tf_op jit(solution)/shard_map/thn,chn->cth/dot_general | solution.py:83
  660.0 176.8 %fusion.93 = f32[1024,2,64]{2,1,0:T(2,128)S(1)} fusion(f32[1024,64]{1,0:T(8,128)S(1)} %copy-done.60, f32[64]{0:T(128)S(1)} %get-tuple-element.829, f32[1024,64]{1,0:T(8,128)S(1)} %copy-done.59, f32[1024,64]{1,0:T(8,128)} %copy.320, f32[1024,64]{1,0:T(8,128)S(1)} %copy.319), kind=kOutput, calls=%fused_computation.147 | convolution fusion | flops 130023424 | bytes 1573120 | tf_op jit(solution)/shard_map/thn,chn->cth/dot_general | solution.py:84
  838.0 154.1 %fusion.86 = f32[1024,2,64]{2,1,0:T(2,128)S(1)} fusion(f32[1024,64]{1,0:T(8,128)} %copy.325, f32[64]{0:T(128)S(1)} %get-tuple-element.829, f32[1024,64]{1,0:T(8,128)S(1)} %copy-done.59, f32[1024,64]{1,0:T(8,128)} %copy.320, f32[1024,64]{1,0:T(8,128)S(1)} %copy.319), kind=kOutput, calls=%fused_computation.140 | convolution fusion | flops 130023424 | bytes 1573120 | tf_op jit(solution)/shard_map/transpose(jvp(thn,chn->cth))/dot_general | solution.py:119
  1053.7 128.7 %while.34 = (s32[]{:T(128)}, f32[2,1024,64]{2,1,0:T(8,128)}, f32[2,1024,64]{2,1,0:T(8,128)}, s32[]{:T(128)}, f32[16,2,1024,64]{2,3,1,0:T(8,128)}, /*index=5*/f32...) while((s32[]{:T(128)}, f32[2,1024,64]{2,1,0:T(8,128)}, ...), condition=%wide.region_4.5_spmd.clone, body=%wide.region_3.4_spmd.clone.sunk | while | flops 2097156 | bytes 8913065 | solution.py:32
  1189.0 178.5 %fusion.88 = f32[1024,2,64]{2,1,0:T(2,128)} fusion(f32[2,1024,64]{2,0,1:T(2,128)} %copy.342, f32[1024,64]{1,0:T(8,128)} %copy.325, f32[64]{0:T(128)S(1)} %get-tuple-element.829, f32[1024,64]{1,0:T(8,128)} %copy.324, f32[1024,64]{1,0:T(8,128)} %copy.320, f32[1024,64]{1,0:T(8,128)S(1)} %get-tuple-element.1075), kind=kOutput, calls=%fused_computation.142 | convolution fusion | flops 130023424 | bytes 2097408 | tf_op jit(solution)/shard_map/jvp(thn,chn->cth)/dot_general | solution.py:119
  1369.8 178.4 %fusion.92 = f32[1024,2,64]{2,1,0:T(2,128)} fusion(f32[2,1024,64]{2,0,1:T(2,128)S(1)} %copy.345, f32[1024,64]{1,0:T(8,128)} %copy.325, f32[64]{0:T(128)S(1)} %get-tuple-element.829, f32[1024,64]{1,0:T(8,128)} %copy.324, f32[1024,64]{1,0:T(8,128)} %copy.320, f32[1024,64]{1,0:T(8,128)S(1)} %get-tuple-element.1075), kind=kOutput, calls=%fused_computation.146 | convolution fusion | flops 130023424 | bytes 2097408 | tf_op jit(solution)/shard_map/jvp(thn,chn->cth)/dot_general | solution.py:120
  1591.5 156.2 %fusion.87 = f32[1024,2,64]{2,1,0:T(2,128)} fusion(f32[1024,2,64]{2,1,0:T(2,128)} %copy.350, f32[1024,64]{1,0:T(8,128)} %copy.325, f32[64]{0:T(128)S(1)} %get-tuple-element.829, f32[1024,64]{1,0:T(8,128)} %copy.324, f32[1024,64]{1,0:T(8,128)} %copy.320, f32[1024,64]{1,0:T(8,128)S(1)} %get-tuple-element.1075), kind=kOutput, calls=%fused_computation.141 | convolution fusion | flops 130023424 | bytes 2097408 | tf_op jit(solution)/shard_map/transpose(jvp(thn,chn->cth))/dot_general | solution.py:119
  1749.9 155.7 %fusion.91 = f32[1024,2,64]{2,1,0:T(2,128)} fusion(f32[1024,2,64]{2,1,0:T(2,128)S(1)} %copy.348, f32[1024,64]{1,0:T(8,128)} %copy.325, f32[64]{0:T(128)S(1)} %get-tuple-element.829, f32[1024,64]{1,0:T(8,128)} %copy.324, f32[1024,64]{1,0:T(8,128)} %copy.320, f32[1024,64]{1,0:T(8,128)S(1)} %get-tuple-element.1075), kind=kOutput, calls=%fused_computation.145 | convolution fusion | flops 130023424 | bytes 2097408 | tf_op jit(solution)/shard_map/transpose(jvp(thn,chn->cth))/dot_general | solution.py:120
  1931.9 156.6 %fusion.109 = (f32[1024,64]{1,0:T(8,128)}, f32[1024,64]{1,0:T(8,128)}) fusion(f32[2,1024,64]{2,1,0:T(8,128)S(1)} %copy-done.4, f32[2,1024,64]{2,1,0:T(8,128)S(1)} %copy-done.2, f32[1024,64]{1,0:T(8,128)} %copy.325, f32[64]{0:T(128)S(1)} %get-tuple-element.829, f32[1024,64]{1,0:T(8,128)} %copy.324, f32[1024,64]{1,0:T(8,128)} %copy.320, ...), kind=kOutput, calls=%fused_computation.177 | convolution fusion | flops 130416640 | bytes 2621696 | tf_op jit(solution)/shard_map/transpose(jvp(thn,chn->cth))/dot_general | solution.py:120
  2196.4 56.2 %fusion.210 = f32[1024,64,64]{2,1,0:T(8,128)} fusion(f32[1024,2,64]{2,1,0:T(2,128)S(1)} %copy-done.31, f32[2,1024,64]{2,0,1:T(2,128)S(1)} %copy-done.16), kind=kOutput, calls=%fused_computation.396 | convolution fusion | flops 100663296 | bytes 17825792 | tf_op jit(solution)/shard_map/transpose(jvp(thn,chn->cth))/dot_general | solution.py:120
  2252.7 56.6 %fusion.211 = f32[1024,64,64]{2,1,0:T(8,128)} fusion(f32[1024,2,64]{2,1,0:T(2,128)S(1)} %copy-done.32, f32[2,1024,64]{2,0,1:T(2,128)S(1)} %copy-done.17), kind=kOutput, calls=%fused_computation.397 | convolution fusion | flops 100663296 | bytes 17825792 | tf_op jit(solution)/shard_map/transpose(jvp(thn,chn->cth))/dot_general | solution.py:119
  2309.4 60.2 %add_add_fusion.1 = f32[1024,64,64]{2,1,0:T(8,128)} fusion(f32[1024,64,64]{2,1,0:T(8,128)} %fusion.210, f32[1024,64,64]{2,1,0:T(8,128)} %fusion.157, f32[1024,2,64]{2,1,0:T(2,128)S(1)} %copy-done.29), kind=kOutput, calls=%fused_computation.96 | convolution fusion | flops 109051904 | bytes 50855936 | tf_op jit(solution)/shard_map/transpose(jvp(thn,chn->cth))/dot_general | solution.py:84
  2418.6 78.9 %while.35 = (s32[]{:T(128)}, f32[2,1024,64]{2,1,0:T(8,128)S(1)}, f32[2,1024,64]{2,1,0:T(8,128)S(1)}, s32[]{:T(128)}, f32[16,2,1024,64]{3,2,1,0:T(8,128)}, /*inde...) while((s32[]{:T(128)}, f32[2,1024,64]{2,1,0:T(8,128)S(1)}, ...), condition=%wide.region_10.11_spmd.clone, body=%wide.region_9.10_spmd.clone.sunk | while | flops 2097156 | bytes 4718761 | solution.py:32
  2498.6 178.4 %fusion.62 = f32[1024,2,64]{2,1,0:T(2,128)} fusion(f32[1024,64]{1,0:T(8,128)} %copy.331, f32[1024,64]{1,0:T(8,128)} %copy.330, f32[64]{0:T(128)S(1)} %copy-done.119, f32[1024,64]{1,0:T(8,128)} %copy.320, f32[1024,64]{1,0:T(8,128)S(1)} %get-tuple-element.1076, f32[1024,2,64]{2,0,1:T(8,128)S(1)} %bitcast.288), kind=kOutput, calls=%fused_computation.116 | convolution fusion | flops 130023424 | bytes 2097408 | tf_op jit(solution)/shard_map/transpose(jvp(jhn,cjh->chn))/dot_general | solution.py:90
  2677.0 56.7 %fusion.115 = f32[1024,64,64]{1,2,0:T(8,128)} fusion(f32[2,64,1024]{1,0,2:T(2,128)S(1)} %copy-done.19, f32[1024,2,64]{2,0,1:T(8,128)S(1)} %bitcast.289), kind=kOutput, calls=%fused_computation.190 | convolution fusion | flops 100663296 | bytes 17825792 | tf_op jit(solution)/shard_map/transpose(jvp(jhn,cjh->chn))/dot_general | solution.py:90
  2734.8 178.2 %fusion.60 = f32[1024,2,64]{2,1,0:T(2,128)} fusion(f32[1024,64]{1,0:T(8,128)S(1)} %copy-done.57, f32[1024,64]{1,0:T(8,128)} %copy.330, f32[64]{0:T(128)S(1)} %copy-done.119, f32[1024,64]{1,0:T(8,128)} %copy.320, f32[1024,64]{1,0:T(8,128)S(1)} %get-tuple-element.1076, f32[1024,2,64]{2,0,1:T(8,128)S(1)} %bitcast.290), kind=kOutput, calls=%fused_computation.114 | convolution fusion | flops 130023424 | bytes 2097408 | tf_op jit(solution)/shard_map/transpose(jvp(jhn,cjh->chn))/dot_general | solution.py:89
  2913.2 56.6 %fusion.112 = f32[1024,64,64]{1,2,0:T(8,128)} fusion(f32[2,64,1024]{1,0,2:T(2,128)S(1)} %copy-done.20, f32[1024,2,64]{2,0,1:T(8,128)S(1)} %bitcast.291), kind=kOutput, calls=%fused_computation.187 | convolution fusion | flops 100663296 | bytes 17825792 | tf_op jit(solution)/shard_map/transpose(jvp(jhn,cjh->chn))/dot_general | solution.py:89
  2988.3 560.1 %multiply_reduce_fusion = (f32[1024,64]{1,0:T(8,128)}, f32[1024,64]{1,0:T(8,128)}, f32[1024,64]{1,0:T(8,128)}, f32[1024,64]{1,0:T(8,128)}, f32[1024,64]{1,0:T(8,...) fusion(f32[64]{0:T(128)S(1)} %copy-done.121, ...), kind=kOutput, calls=%fused_computation.94 | convolution fusion | flops 485490688 | bytes 91226624 | tf_op jit(solution)/shard_map/transpose(jvp(thn,chn->cth))/dot_general | solution.py:83
  3600.4 38.7 %all-reduce.3 = (f32[1024]{0:T(1024)}, f32[1024]{0:T(1024)}, f32[1024]{0:T(1024)}, f32[1024]{0:T(1024)}, f32[2048]{0:T(1024)}, /*index=5*/f32[1024]{0:T(1024)}, f32[1024]{0:T(1024)}, f32[4096]{0:T(1024)}, f32[1024]{0:T(1024)}) all-reduce(f32[1024]{0:T(1024)S(1)} %copy-done.87, ...), channel_id=1, replica_groups=mesh['batch'=2,'seq'=16] {'batch','seq'}, use_global_device_ids=true, to_apply=%region_14.15 | all-reduce | flops 13312 | bytes 106496 | tf_op jit(solution)/shard_map/psum | solution.py:277
  3640.1 89.8 %all-reduce.9.cloned.1.call-done = (f32[1024,64]{0,1:T(8,128)}, f32[1024,64]{0,1:T(8,128)}, f32[1024,64]{0,1:T(8,128)}, f32[1024,64]{0,1:T(8,128)}, f32[1024,64]{0,1:T(8,128)}, /*index=5*/f32[1024,64]{0,1:T(8,128)}) async-done(((f32[1024,64]{0,1:T(8,128)}, f32[1024,64]{0,1:T(8,128)}, f32[1024,64]{0,1:T(8,128)}, f32[1024,64]{0,1:T(8,128)}, f32[1024,64]{0,1:T(8,128)}, /*index=5*/f32[1024,64]{0,1:T(8,128)}), ...) | async-done | bytes 1572880 | tf_op jit(solution)/shard_map/psum | solution.py:277
  3729.9 76.0 %all-reduce.11.cloned.1.call-done = (f32[64,2048]{1,0:T(8,128)}, f32[64,4096]{1,0:T(8,128)}, f32[256,1024]{1,0:T(8,128)}) async-done(((f32[64,2048]{1,0:T(8,128)}, f32[64,4096]{1,0:T(8,128)}, f32[256,1024]{1,0:T(8,128)}), (f32[64,2048]{1,0:T(8,128)}, f32[64,4096]{1,0:T(8,128)}, f32[256,1024]{1,0:T(8,128)})) %all-reduce.11.cloned.1.call-update) | async-done | bytes 2621456 | tf_op jit(solution)/shard_map/psum | solution.py:302
  (566 shorter events, 627.5 us)
Async XLA Ops:
  7.2 1046.5 %all-gather.12.cloned.1.call-start = ((), (), s32[]{:S(2)}) async-start(), calls=%async_computation.7 | async-start | bytes 8912896 | tf_op jit(solution)/shard_map/all_gather | solution.py:20
  8.1 16.0 collective-permute-start
  10.5 1921.4 %copy-start.120 = (f32[64]{0:T(128)}, f32[64]{0:T(128)S(1)}, u32[]{:S(2)}) copy-start(f32[64]{0:T(128)S(1)} %get-tuple-element.829) | copy-start | bytes 772
  21.8 326.8 %copy-start.45 = (f32[1024,64]{0,1:T(8,128)}, f32[1024,64]{0,1:T(8,128)S(1)}, u32[]{:S(2)}) copy-start(f32[1024,64]{0,1:T(8,128)S(1)} %get-tuple-element.808) | copy-start | bytes 786436
  21.8 326.8 %copy-start.46 = (f32[1024,64]{0,1:T(8,128)}, f32[1024,64]{0,1:T(8,128)S(1)}, u32[]{:S(2)}) copy-start(f32[1024,64]{0,1:T(8,128)S(1)} %get-tuple-element.809) | copy-start | bytes 786436
  24.1 320.3 %copy-start.49 = (f32[1024,64]{0,1:T(8,128)}, f32[1024,64]{0,1:T(8,128)S(1)}, u32[]{:S(2)}) copy-start(f32[1024,64]{0,1:T(8,128)S(1)} %get-tuple-element.803) | copy-start | bytes 786436
  26.0 315.3 %copy-start.97 = (f32[2,64]{1,0:T(2,128)}, f32[2,64]{1,0:T(2,128)S(1)}, u32[]{:S(2)}) copy-start(f32[2,64]{1,0:T(2,128)S(1)} %get-tuple-element.818) | copy-start | bytes 1540
  341.4 317.3 %copy-start.113 = (f32[2]{0:T(128)}, f32[2]{0:T(128)S(1)}, u32[]{:S(2)}) copy-start(f32[2]{0:T(128)S(1)} %slice_reduce_fusion) | copy-start | bytes 28
  345.5 708.2 %all-gather.10.cloned.1.call-start = ((), (), s32[]{:S(2)}) async-start(), calls=%async_computation.6 | async-start | bytes 8912896 | tf_op jit(solution)/shard_map/all_gather | solution.py:20
  346.3 2023.3 %all-gather.16.cloned.1.call-start = ((), (), s32[]{:S(2)}) async-start(), calls=%async_computation.9 | async-start | bytes 8912896 | tf_op jit(solution)/shard_map/all_gather | solution.py:20
  838.0 201.6 %copy-start.33 = (f32[2,1024,64]{1,2,0:T(8,128)S(1)}, f32[2,1024,64]{1,2,0:T(8,128)}, u32[]{:S(2)}) copy-start(f32[2,1024,64]{1,2,0:T(8,128)} %get-tuple-element.805) | copy-start | bytes 1572868
  1586.5 506.0 %copy-start.13 = (f32[2,64,1024]{2,1,0:T(8,128)}, f32[2,64,1024]{2,1,0:T(8,128)S(1)}, u32[]{:S(2)}) copy-start(f32[2,64,1024]{2,1,0:T(8,128)S(1)} %get-tuple-element.752) | copy-start | bytes 1572868
  1913.0 481.7 %all-gather.14.cloned.1.call-start = ((), (), s32[]{:S(2)}) async-start(), calls=%async_computation.8 | async-start | bytes 8912896 | tf_op jit(solution)/shard_map/all_gather | solution.py:20
  1913.5 1684.0 %reduce-scatter.4.cloned.1.call-start = ((), (), s32[]{:S(2)}) async-start(), calls=%async_computation.3 | async-start | bytes 8912896 | tf_op jit(solution)/shard_map/reduce_scatter | solution.py:298
  1919.5 1678.0 %reduce-scatter.6.cloned.1.call-start = ((), (), s32[]{:S(2)}) async-start(), calls=%async_computation.4 | async-start | bytes 17825792 | tf_op jit(solution)/shard_map/reduce_scatter | solution.py:299
  1928.9 1668.7 %reduce-scatter.8.cloned.1.call-start = ((), (), s32[]{:S(2)}) async-start(), calls=%async_computation.5 | async-start | bytes 17825792 | tf_op jit(solution)/shard_map/reduce_scatter | solution.py:300
  2309.3 1420.6 %all-reduce.9.cloned.1.call-start = ((), (), s32[]{:S(2)}) async-start(), calls=%async_computation.10 | async-start | bytes 3145728 | tf_op jit(solution)/shard_map/psum | solution.py:277
  2988.2 591.3 %copy-start.114 = (f32[2]{0:T(128)S(1)}, f32[2]{0:T(128)}, u32[]{:S(2)}) copy-start(f32[2]{0:T(128)} %copy-done.113) | copy-start | bytes 28
  2988.2 598.1 %copy-start.22 = (f32[1024,64]{0,1:T(8,128)S(1)}, f32[1024,64]{0,1:T(8,128)}, u32[]{:S(2)}) copy-start(f32[1024,64]{0,1:T(8,128)} %copy-done.21) | copy-start | bytes 786436
  2988.3 598.1 %copy-start.27 = (f32[1024,64]{0,1:T(8,128)S(1)}, f32[1024,64]{0,1:T(8,128)}, u32[]{:S(2)}) copy-start(f32[1024,64]{0,1:T(8,128)} %param.30) | copy-start | bytes 786436
  2988.3 598.1 %copy-start.28 = (f32[1024,64]{0,1:T(8,128)S(1)}, f32[1024,64]{0,1:T(8,128)}, u32[]{:S(2)}) copy-start(f32[1024,64]{0,1:T(8,128)} %param.29) | copy-start | bytes 786436
  2988.3 598.1 %copy-start.41 = (f32[1024,64]{0,1:T(8,128)S(1)}, f32[1024,64]{0,1:T(8,128)}, u32[]{:S(2)}) copy-start(f32[1024,64]{0,1:T(8,128)} %copy-done.40) | copy-start | bytes 786436
  2988.3 598.1 %copy-start.69 = (f32[1024]{0:T(1024)S(1)}, f32[1024]{0:T(1024)}, u32[]{:S(2)}) copy-start(f32[1024]{0:T(1024)} %copy-done.68) | copy-start | bytes 12292
  3597.4 208.5 %all-reduce.11.cloned.1.call-start = ((), (), s32[]{:S(2)}) async-start(), calls=%async_computation.11 | async-start | bytes 5242880 | tf_op jit(solution)/shard_map/psum | solution.py:302
  (112 other events, 8934.4 us)
Sparse Core Ops, SparseCore 0:
  345.6 77.6 all-gather.11
  425.4 73.3 all-gather.9
  1913.1 72.1 all-gather.15
  1987.3 73.2 all-gather.13
  2064.5 102.9 reduce-scatter.3
  2171.5 178.3 reduce-scatter.5
  2354.0 177.5 reduce-scatter.7
  3597.6 132.3 all-reduce.8
  3732.4 73.5 all-reduce.10
where the time goes:
time: 3840 us; the launch traced here: 3830 us
  matrix products  2990 us (78%)
  other arithmetic  384 us (10%)
  local copies, waits for them, and re-layouts  198 us (5%)
  waiting for transfers between devices  168 us (4%)
  blocking collectives  72.6 us (2%)
    dot_general x2, matrix products, block_step(): jnp.einsum('thn,chn->cth', cl_re, state_re, precision=lax.Precision.HIGHEST)  737 us
    dot_general x5, matrix products, piece_inject(): jnp.einsum('thn,chn->cth', cl_im, cur_im, precision=lax.Precision.HIGHEST)  585 us
    dot_general x5, matrix products, piece_inject(): jnp.einsum('thn,chn->cth', cl_re, cur_re, precision=lax.Precision.HIGHEST)  577 us
    dot_general x3, matrix products, block_step(): jnp.einsum('jhn,cjh->chn', lb_im, masked, precision=lax.Precision.HIGHEST)  391 us
    dot_general x3, matrix products, block_step(): jnp.einsum('jhn,cjh->chn', lb_re, masked, precision=lax.Precision.HIGHEST)  391 us
    dot_general x2, matrix products, block_step(): jnp.einsum('thn,chn->cth', cl_im, state_im, precision=lax.Precision.HIGHEST)  237 us
    reduce_sum x1, other arithmetic, mode_tables(): kernel = 2.0 * jnp.sum(prod_re * pow_re - prod_im * pow_im, axis=2)  132 us
    psum x1, waiting for transfers between devices, on_device(): lax.psum((grad_g1, grad_b1, grad_params[0], grad_params[1], grad_params[2...  89.8 us
  transfers between devices with their start and end apart: 10, of which 2 were waited for; matrix products, arithmetic and copies ran while one was open for 62% of the time, Pallas kernels for 0%

commit v1 on v0

v1 whole, which is shorter than its diff:
```python
import jax, jax.numpy as jnp
from jax import lax
from jax.sharding import PartitionSpec as P
from jax.experimental import pallas as pl
from jax.experimental.pallas import tpu as pltpu
F32, BF16 = jnp.float32, jnp.bfloat16
LANES = 128
HALF = 64
FORWARD_UNROLL = 4
BACKWARD_UNROLL = 2
NN = (((1,), (0,)), ((), ()))
NT = (((1,), (1,)), ((), ()))
TN = (((0,), (0,)), ((), ()))


def halves(value):
    high = value.astype(BF16)
    return high, (value - high.astype(F32)).astype(BF16)


def mm(left, right, dims):
    out = lax.dot_general(left[0], right[0], dims, preferred_element_type=F32)
    out = out + lax.dot_general(left[1], right[0], dims, preferred_element_type=F32)
    return out + lax.dot_general(left[0], right[1], dims, preferred_element_type=F32)


def swap(value):
    return pltpu.roll(value, HALF, value.ndim - 1)


def low_lanes(shape):
    return lax.broadcasted_iota(jnp.int32, shape, len(shape) - 1) < HALF


def as_factor(value):
    turned = swap(value)
    low = low_lanes(value.shape)
    return jnp.where(low, value, turned), jnp.where(low, -turned, value)


def times(value, factor):
    return value * factor[0] + swap(value) * factor[1]


def power_setup(lam, base_ref, fre_ref, fim_ref, steps, channels):
    one = jnp.where(low_lanes(lam.shape), 1.0, 0.0)
    factor = as_factor(lam)
    row = one
    for k in range(8):
        base_ref[pl.ds(k * channels, channels), :] = row
        row = times(row, factor)
    eight = as_factor(row)
    row = one
    for i in range(16):
        fre, fim = as_factor(row)
        fre_ref[pl.ds(i * channels, channels), :] = fre
        fim_ref[pl.ds(i * channels, channels), :] = fim
        row = times(row, eight)
    for s in range(steps):
        fre, fim = as_factor(row)
        fre_ref[pl.ds((16 + s) * channels, channels), :] = fre
        fim_ref[pl.ds((16 + s) * channels, channels), :] = fim
        row = times(row, (fre, fim))


def power_tables(h, base_ref, fre_ref, fim_ref, channels):
    base = base_ref[pl.ds(h, 8, stride=channels), :]
    fre = fre_ref[pl.ds(h, 16, stride=channels), :]
    fim = fim_ref[pl.ds(h, 16, stride=channels), :]
    turned = swap(base)
    power = jnp.concatenate(
        [base * fre[i : i + 1] + turned * fim[i : i + 1] for i in range(16)], axis=0
    )
    return power


def reversed_tables(h, base_ref, fre_ref, fim_ref, channels):
    base = jnp.concatenate(
        [base_ref[pl.ds(h + k * channels, 1), :] for k in range(7, -1, -1)], axis=0
    )
    fre = fre_ref[pl.ds(h, 16, stride=channels), :]
    fim = fim_ref[pl.ds(h, 16, stride=channels), :]
    turned = swap(base)
    return jnp.concatenate(
        [base * fre[i : i + 1] + turned * fim[i : i + 1] for i in range(15, -1, -1)], axis=0
    )


def doc_masks(seg_ref, mask_ref, row, pitch, chunks, docs):
    even = seg_ref[pl.ds(row, chunks, stride=2 * pitch), :]
    odd = seg_ref[pl.ds(row + pitch, chunks, stride=2 * pitch), :]
    pair = join(even, odd)
    for d in range(docs):
        for c in range(2):
            mask_ref[d * 2 + c] = jnp.where(pair[c] == float(d), 1.0, 0.0)


def join(even, odd):
    low = low_lanes(even.shape)
    return jnp.where(low, even, swap(odd)), jnp.where(low, swap(even), odd)


def spread(pair, mask_ref, docs):
    return jnp.concatenate(
        [pair[c] * mask_ref[d * 2 + c] for d in range(docs) for c in range(2)], axis=0
    )


def gathered(rows, mask_ref, chunks, docs):
    out = []
    for c in range(2):
        total = None
        for d in range(docs):
            at = (d * 2 + c) * chunks
            term = rows[at : at + chunks] * mask_ref[d * 2 + c]
            total = term if total is None else total + term
        out.append(total)
    return out


def scan_factors(h, fre_ref, fim_ref, channels, chunks, steps, backward):
    at = lax.broadcasted_iota(jnp.int32, (chunks, LANES), 0)
    out = []
    for s in range(steps):
        keep = at < chunks - (1 << s) if backward else at >= (1 << s)
        fre = fre_ref[pl.ds(h + (16 + s) * channels, 1), :]
        fim = fim_ref[pl.ds(h + (16 + s) * channels, 1), :]
        out.append((jnp.where(keep, fre, 0.0), jnp.where(keep, fim, 0.0)))
    return out


def scan_chunks(rows, factors, chunks, backward):
    at = lax.broadcasted_iota(jnp.int32, (chunks, LANES), 0)
    keep = at < chunks - 1 if backward else at >= 1
    out = []
    for i in range(rows.shape[0] // chunks):
        part = rows[i * chunks : (i + 1) * chunks]
        for s, factor in enumerate(factors):
            moved = pltpu.roll(part, chunks - (1 << s) if backward else 1 << s, 0)
            part = part + times(moved, factor)
        moved = pltpu.roll(part, chunks - 1 if backward else 1, 0)
        out.append(jnp.where(keep, moved, 0.0))
    return jnp.concatenate(out, axis=0)


def toeplitz(row):
    wide = jnp.broadcast_to(row, (LANES, LANES))
    wide = pltpu.roll(wide, 0, 1, stride=1, stride_axis=0)
    j = lax.broadcasted_iota(jnp.int32, (LANES, LANES), 0)
    t = lax.broadcasted_iota(jnp.int32, (LANES, LANES), 1)
    return jnp.where(t >= j, wide, 0.0)


def lag_sums(table):
    out = None
    j = lax.broadcasted_iota(jnp.int32, (8, LANES), 0)
    t = lax.broadcasted_iota(jnp.int32, (8, LANES), 1)
    for i in range(16):
        part = jnp.where(t >= j + 8 * i, table[8 * i : 8 * i + 8], 0.0)
        if i:
            part = pltpu.roll(part, LANES - 8 * i, 1)
        out = part if out is None else out + part
    for bit in (1, 2, 4):
        out = jnp.where((j & bit) != 0, pltpu.roll(out, LANES - bit, 1), out)
    return jnp.sum(out, axis=0, keepdims=True)


def wide_rows(row):
    return jnp.broadcast_to(row, (8, LANES))


def forward_kernel(
    sizes, recv_ref, lam_ref, weight_ref, skip_ref, out_ref, enter_ref, lag_ref,
    base_ref, fre_ref, fim_ref, mask_ref,
):
    channels, chunks, docs, steps, pitch, unroll = sizes
    power_setup(lam_ref[...], base_ref, fre_ref, fim_ref, steps, channels)
    doc_masks(recv_ref, mask_ref, channels, pitch, chunks, docs)

    def one(h):
        pair = join(
            recv_ref[pl.ds(h, chunks, stride=2 * pitch), :],
            recv_ref[pl.ds(h + pitch, chunks, stride=2 * pitch), :],
        )
        rows = halves(spread(pair, mask_ref, docs))
        power = halves(power_tables(h, base_ref, fre_ref, fim_ref, channels))
        back = halves(reversed_tables(h, base_ref, fre_ref, fim_ref, channels))
        weight = weight_ref[pl.ds(h, 1), :]
        low = low_lanes((1, LANES))
        lags = mm(halves(wide_rows(jnp.where(low, weight, -weight))), power, NT)[0:1]
        lag_ref[pl.ds(h, 1), :] = lags
        table = halves(toeplitz(lags))
        local = mm(rows, back, NN)
        enter = scan_chunks(
            local, scan_factors(h, fre_ref, fim_ref, channels, chunks, steps, False), chunks, False
        )
        enter_ref[h] = enter
        lam = as_factor(lam_ref[pl.ds(h, 1), :])
        coef = as_factor(times(weight, lam))
        ready = times(enter, coef)
        ready = jnp.where(low_lanes(ready.shape), ready, -ready)
        mixed = mm(rows, table, NN) + mm(halves(ready), power, NT)
        first, second = gathered(mixed, mask_ref, chunks, docs)
        skip = skip_ref[pl.ds(h, 1), :]
        first = first + skip * pair[0]
        second = second + skip * pair[1]
        even, odd = join(first, second)
        out_ref[pl.ds(h, chunks, stride=2 * channels), :] = even
        out_ref[pl.ds(h + channels, chunks, stride=2 * channels), :] = odd

    def several(i, carry):
        for k in range(unroll):
            one(i * unroll + k)
        return carry

    lax.fori_loop(0, channels // unroll, several, 0)


def backward_kernel(
    sizes, recv_ref, grad_ref, enter_ref, lag_ref, lam_ref, weight_ref, skip_ref, gain_ref, bias_ref,
    out_ref, sum_ref, first_ref, skipg_ref, gaing_ref, biasg_ref,
    base_ref, fre_ref, fim_ref, mask_ref,
):
    channels, chunks, docs, steps, pitch, unroll = sizes
    power_setup(lam_ref[...], base_ref, fre_ref, fim_ref, steps, channels)
    doc_masks(recv_ref, mask_ref, channels, pitch, chunks, docs)
    lag = lax.broadcasted_iota(jnp.int32, (LANES, LANES), 0).astype(F32)

    def one(h):
        pair = join(
            recv_ref[pl.ds(h, chunks, stride=2 * pitch), :],
            recv_ref[pl.ds(h + pitch, chunks, stride=2 * pitch), :],
        )
        gpair = join(
            grad_ref[pl.ds(h, chunks, stride=2 * channels), :],
            grad_ref[pl.ds(h + channels, chunks, stride=2 * channels), :],
        )
        rows = halves(spread(pair, mask_ref, docs))
        grows = halves(spread(gpair, mask_ref, docs))
        power32 = power_tables(h, base_ref, fre_ref, fim_ref, channels)
        back32 = reversed_tables(h, base_ref, fre_ref, fim_ref, channels)
        power, power1 = halves(power32), halves(power32 * lag)
        back, back1 = halves(back32), halves(back32 * (LANES - 1.0 - lag))
        weight = weight_ref[pl.ds(h, 1), :]
        lam = as_factor(lam_ref[pl.ds(h, 1), :])
        table = halves(toeplitz(lag_ref[pl.ds(h, 1), :]))
        enter = enter_ref[h]
        ahead = scan_factors(h, fre_ref, fim_ref, channels, chunks, steps, False)
        astern = scan_factors(h, fre_ref, fim_ref, channels, chunks, steps, True)
        hop = (
            fre_ref[pl.ds(h + 16 * channels, 1), :] * float(LANES),
            fim_ref[pl.ds(h + 16 * channels, 1), :] * float(LANES),
        )
        enter1 = scan_chunks(mm(rows, back1, NN) + times(enter, hop), ahead, chunks, False)
        seen = mm(grows, power, NN)
        seen1 = times(seen + mm(grows, power1, NN), lam)
        seen = times(seen, lam)
        seen_f = as_factor(seen)
        total = times(enter, seen_f)
        total1 = times(enter1, seen_f) + times(enter, as_factor(seen1))
        lags = halves(wide_rows(lag_sums(mm(rows, grows, TN))))
        sums = jnp.sum(total, axis=0, keepdims=True) + mm(lags, power, NN)[0:1]
        sums1 = jnp.sum(total1, axis=0, keepdims=True) + mm(lags, power1, NN)[0:1]
        sum_ref[pl.ds(h, 1), :] = sums
        first_ref[pl.ds(h, 1), :] = sums1
        leave = scan_chunks(times(seen, as_factor(weight)), astern, chunks, True)
        leave = jnp.where(low_lanes(leave.shape), leave, -leave)
        inner = mm(grows, table, NT) + mm(halves(leave), back, NT)
        gfirst, gsecond = gathered(inner, mask_ref, chunks, docs)
        skip = skip_ref[pl.ds(h, 1), :]
        gfirst = gfirst + skip * gpair[0]
        gsecond = gsecond + skip * gpair[1]
        even, odd = join(gfirst, gsecond)
        out_ref[pl.ds(h, chunks, stride=2 * channels), :] = even
        out_ref[pl.ds(h + channels, chunks, stride=2 * channels), :] = odd
        gain = gain_ref[pl.ds(h, 1), :]
        bias = bias_ref[pl.ds(h, 1), :]
        skipg_ref[pl.ds(h, 1), :] = jnp.sum(gpair[0] * pair[0] + gpair[1] * pair[1], axis=0, keepdims=True)
        biasg_ref[pl.ds(h, 1), :] = jnp.sum(gfirst + gsecond, axis=0, keepdims=True)
        gaing_ref[pl.ds(h, 1), :] = jnp.sum(
            gfirst * ((pair[0] - bias) / gain) + gsecond * ((pair[1] - bias) / gain), axis=0, keepdims=True
        )

    def several(i, carry):
        for k in range(unroll):
            one(i * unroll + k)
        return carry

    lax.fori_loop(0, channels // unroll, several, 0)


def kernel_sizes(recv_rows, channels, pieces, docs, unroll):
    chunks = pieces // 2
    steps = max(1, (chunks - 1).bit_length())
    return (channels, chunks, docs, steps, channels + 8, unroll)


def scratch(channels, chunks, docs, steps):
    return [
        pltpu.VMEM((8 * channels, LANES), F32),
        pltpu.VMEM(((16 + steps) * channels, LANES), F32),
        pltpu.VMEM(((16 + steps) * channels, LANES), F32),
        pltpu.VMEM((docs * 2, chunks, LANES), F32),
    ]


def recurrence(recv, lam, weight, skip, pieces, docs, unroll=2):
    channels = lam.shape[0]
    sizes = kernel_sizes(recv.shape[0], channels, pieces, docs, unroll)
    chunks, steps = sizes[1], sizes[3]
    rows = docs * 2 * chunks
    return pl.pallas_call(
        lambda *refs: forward_kernel(sizes, *refs),
        out_shape=(
            jax.ShapeDtypeStruct((pieces * channels, LANES), F32),
            jax.ShapeDtypeStruct((channels, rows, LANES), F32),
            jax.ShapeDtypeStruct((channels, LANES), F32),
        ),
        scratch_shapes=scratch(channels, chunks, docs, steps),
        compiler_params=pltpu.CompilerParams(vmem_limit_bytes=48 << 20),
        name="recurrence",
    )(recv, lam, weight, skip)


def recurrence_back(recv, grad, enter, lags, lam, weight, skip, gain, bias, pieces, docs, unroll=2):
    channels = lam.shape[0]
    sizes = kernel_sizes(recv.shape[0], channels, pieces, docs, unroll)
    chunks, steps = sizes[1], sizes[3]
    row = jax.ShapeDtypeStruct((channels, LANES), F32)
    return pl.pallas_call(
        lambda *refs: backward_kernel(sizes, *refs),
        out_shape=(jax.ShapeDtypeStruct((pieces * channels, LANES), F32), row, row, row, row, row),
        scratch_shapes=scratch(channels, chunks, docs, steps),
        compiler_params=pltpu.CompilerParams(vmem_limit_bytes=48 << 20),
        name="recurrence_back",
    )(recv, grad, enter, lags, lam, weight, skip, gain, bias)


EPSILON = 1e-05


def layer_norm(values, norm_gain, norm_shift):
    centre = values - jnp.mean(values, axis=-1, keepdims=True)
    spread_of = jnp.mean(centre * centre, axis=-1, keepdims=True)
    return centre * lax.rsqrt(spread_of + EPSILON) * norm_gain + norm_shift


def gelu_exact(values):
    return jax.nn.gelu(values, approximate=False)


def gated_unit(values):
    middle = values.shape[-1] // 2
    return values[..., :middle] * jax.nn.sigmoid(values[..., middle:])


def inner_rows(left, right):
    return lax.dot_general(left, right, TN, preferred_element_type=F32)


def outer_cols(left, right):
    return lax.dot_general(left, right, NT, preferred_element_type=F32)


def flipped(value, axis, bit):
    count = lax.axis_size(axis)
    return lax.ppermute(value, axis, [(i, i ^ bit) for i in range(count)])


def summed(value, axes):
    for axis in axes:
        bit = 1
        while bit < lax.axis_size(axis):
            value = value + flipped(value, axis, bit)
            bit *= 2
    return value


def mode_parts(params):
    decay_log, decay_freq, input_re, input_im, output_re, output_im, step_log = params
    step_size = jnp.exp(step_log)[:, None]
    real_part = -jnp.exp(decay_log)
    delta_re = step_size * real_part
    delta_im = step_size * decay_freq
    magnitude = jnp.exp(delta_re)
    lam_re, lam_im = (magnitude * jnp.cos(delta_im), magnitude * jnp.sin(delta_im))
    denominator = real_part * real_part + decay_freq * decay_freq
    num_re = lam_re - 1.0
    rat_re = (num_re * real_part + lam_im * decay_freq) / denominator
    rat_im = (lam_im * real_part - num_re * decay_freq) / denominator
    bbar_re = rat_re * input_re - rat_im * input_im
    bbar_im = rat_re * input_im + rat_im * input_re
    prod_re = 2.0 * (output_re * bbar_re - output_im * bbar_im)
    prod_im = 2.0 * (output_re * bbar_im + output_im * bbar_re)
    return (delta_re, delta_im, prod_re, prod_im), (lam_re, lam_im)


def packed(real, imag):
    return jnp.concatenate([real, imag], axis=1)


def on_device(
    tokens, segments, norm1_gain, norm1_bias, decay_log, decay_freq, input_re, input_im,
    output_re, output_im, step_log, skip_gain, glu_weight, glu_bias, norm2_gain, norm2_bias,
    ffn_in, ffn_in_bias, ffn_out, ffn_out_bias, cotangent,
):
    contexts, piece_len, features = tokens.shape
    rows = contexts * piece_len
    pieces, mine = lax.axis_size("seq"), lax.axis_index("seq")
    channels = features // pieces
    docs = max(1, pieces * piece_len // 256)
    params = (decay_log, decay_freq, input_re, input_im, output_re, output_im, step_log)

    def own(value):
        return lax.dynamic_slice_in_dim(value, mine * channels, channels, 0)

    def row_of(value):
        return jnp.broadcast_to(own(value)[:, None], (channels, LANES))

    parts, lam_pair = mode_parts(tuple(own(p) for p in params))
    lam, weight = packed(*lam_pair), packed(parts[2], parts[3])
    skip = row_of(skip_gain)

    floats = tokens.astype(F32).reshape(rows, features)
    centre = floats - jnp.mean(floats, axis=-1, keepdims=True)
    recip1 = lax.rsqrt(jnp.mean(centre * centre, axis=-1, keepdims=True) + EPSILON)
    unit1 = centre * recip1
    normed = unit1 * norm1_gain + norm1_bias
    turned = normed.T.reshape(pieces, channels, rows)
    seg_rows = jnp.broadcast_to(segments.astype(F32).reshape(1, 1, rows), (pieces, 8, rows))
    recv = lax.all_to_all(jnp.concatenate([turned, seg_rows], axis=1), "seq", 0, 0)
    recv = recv.reshape(pieces * (channels + 8), rows)
    mixed_rows, enter, lags = recurrence(recv, lam, weight, skip, pieces, docs, FORWARD_UNROLL)
    mixed = lax.all_to_all(mixed_rows.reshape(pieces, channels, rows), "seq", 0, 0)
    mixed = mixed.reshape(features, rows).T

    activation, gelu1_pull = jax.vjp(gelu_exact, mixed)
    flat_act = activation.astype(BF16)
    glu_pre = jnp.dot(flat_act, glu_weight, preferred_element_type=F32) + glu_bias
    glu_out, glu_pull = jax.vjp(gated_unit, glu_pre)
    hidden = floats + glu_out
    normed_two, norm2_pull = jax.vjp(layer_norm, hidden, norm2_gain, norm2_bias)
    norm2_low = normed_two.astype(BF16)
    ffn_pre = jnp.dot(norm2_low, ffn_in, preferred_element_type=F32) + ffn_in_bias
    ffn_act, gelu2_pull = jax.vjp(gelu_exact, ffn_pre)
    ffn_low = ffn_act.astype(BF16)
    ffn_res = jnp.dot(ffn_low, ffn_out, preferred_element_type=F32) + ffn_out_bias
    result = (hidden + ffn_res).astype(BF16).reshape(tokens.shape)
    up_low = cotangent.reshape(rows, features)
    upstream = up_low.astype(F32)
    grad_ffn_low = outer_cols(up_low, ffn_out)
    term_out = inner_rows(ffn_low, up_low)
    bias_out = jnp.sum(upstream, axis=0)
    pre_low = gelu2_pull(grad_ffn_low)[0].astype(BF16)
    grad_normed_two = outer_cols(pre_low, ffn_in)
    term_in = inner_rows(norm2_low, pre_low)
    bias_in = jnp.sum(pre_low.astype(F32), axis=0)
    hidden_part, grad_g2, grad_b2 = norm2_pull(grad_normed_two)
    grad_hidden = upstream + hidden_part
    glu_low = glu_pull(grad_hidden)[0].astype(BF16)
    grad_act = outer_cols(glu_low, glu_weight)
    term_glu = inner_rows(flat_act, glu_low)
    bias_glu = jnp.sum(glu_low.astype(F32), axis=0)
    grad_mixed = gelu1_pull(grad_act)[0]

    back = lax.all_to_all(grad_mixed.T.reshape(pieces, channels, rows), "seq", 0, 0)
    grad_rows, sums, firsts, part_skip, part_gain, part_bias = recurrence_back(
        recv, back.reshape(pieces * channels, rows), enter, lags, lam, weight, skip,
        row_of(norm1_gain), row_of(norm1_bias), pieces, docs, BACKWARD_UNROLL,
    )
    grad_normed = lax.all_to_all(grad_rows.reshape(pieces, channels, rows), "seq", 0, 0)
    grad_normed = grad_normed.reshape(features, rows).T
    scaled = grad_normed * norm1_gain
    token_part = recip1 * (
        scaled
        - jnp.mean(scaled, axis=-1, keepdims=True)
        - unit1 * jnp.mean(scaled * unit1, axis=-1, keepdims=True)
    )
    grad_tokens = (grad_hidden + token_part).astype(BF16).reshape(tokens.shape)

    vectors = jnp.stack([jnp.sum(v, axis=1) for v in (part_skip, part_gain, part_bias)], axis=1)
    vectors = jnp.pad(vectors, ((0, 0), (0, LANES - vectors.shape[1])))
    state = summed(jnp.concatenate([sums, firsts, vectors], axis=1), ("batch",))
    state = lax.all_to_all(jnp.broadcast_to(state[None], (pieces,) + state.shape), "seq", 0, 0)
    state = state.reshape(features, state.shape[2])
    half = LANES // 2
    m_re, m_im = state[:, :half], state[:, half:LANES]
    f_re, f_im = state[:, LANES : LANES + half], state[:, LANES + half : 2 * LANES]
    whole_parts, mode_pull = jax.vjp(lambda p: mode_parts(p)[0], params)
    w_re, w_im = whole_parts[2], whole_parts[3]
    grad_params = mode_pull(
        (w_re * f_re - w_im * f_im, -(w_re * f_im + w_im * f_re), m_re, -m_im)
    )[0]
    vectors = state[:, 2 * LANES : 2 * LANES + 3]
    small = summed(
        jnp.concatenate([bias_glu, grad_g2, grad_b2, bias_in, bias_out]).reshape(-1, LANES),
        ("seq", "batch"),
    ).reshape(-1)
    bias_glu, grad_g2, grad_b2, bias_in, bias_out = jnp.split(
        small, [2 * features, 3 * features, 4 * features, small.shape[0] - features]
    )
    row_sums = tuple(
        summed(lax.psum_scatter(term, "seq", scatter_dimension=0, tiled=True), ("batch",))
        for term in (term_out, term_in, term_glu)
    )
    return (
        result, grad_tokens, vectors[:, 1], vectors[:, 2], *grad_params, vectors[:, 0],
        row_sums[2], bias_glu, grad_g2, grad_b2, row_sums[1], bias_in, row_sums[0], bias_out,
    )


def solution(mesh):
    spread_over = P("batch", "seq", None)
    in_specs = (spread_over, P("batch", "seq")) + (P(),) * 18 + (spread_over,)
    rows = P("seq", None)
    out_specs = (spread_over,) * 2 + (P(),) * 10 + (rows,) + (P(),) * 3 + (rows, P(), rows, P())
    return jax.shard_map(
        on_device, mesh=mesh, in_specs=in_specs, out_specs=out_specs, check_vma=False
    )
```

time: 3840 us -> 664 us (0.17)
  matrix products: 2990 us -> 62.7 us
  other arithmetic: 384 us -> 31.1 us
  waiting for transfers between devices: 168 us -> 378 us
  local copies, waits for them, and re-layouts: 198 us -> 26.4 us
  Pallas kernels: 0 us -> 90.7 us
  blocking collectives: 72.6 us -> 18.7 us
    dot_general x31 -> x9, matrix products: 2990 us -> 62.7 us  [the longest x3 25 us: inner_rows(): return lax.dot_general(left, right, TN, preferred_element_type=F32)]
    reduce_scatter x3, waiting for transfers between devices: 0.06 us -> 264 us  [on_device(): lax.psum_scatter(term, 'seq', scatter_dimension=0, tiled=True)]
    psum x2 -> x0, waiting for transfers between devices: 166 us -> none  [the longest x1 89.8 us: on_device(): lax.psum((grad_g1, grad_b1, grad_params[0], grad_params[1], grad_params[2...]
    reduce_sum x14 -> x11, other arithmetic: 162 us -> 9.29 us  [the longest x1 3.91 us: mode_parts(): delta_re = step_size * real_part]
    pallas_call x0 -> x2, Pallas kernels: none -> 90.7 us  [the longest x1 57.9 us: recurrence_back(): pl.pallas_call(lambda *refs: backward_kernel(sizes, *refs), out_shape=(ja...]
    select_n x30 -> x0, other arithmetic: 87.7 us -> none  [turn(): jnp.where(position < mine, new, old)]
    mul x34 -> x4, other arithmetic: 88.1 us -> 1.77 us  [the longest x1 0.93 us: gelu_exact(): return jax.nn.gelu(values, approximate=False)]
    ppermute x1 -> x9, waiting for transfers between devices: 0.01 us -> 75 us  [flipped(): return lax.ppermute(value, axis, [(i, i ^ bit) for i in range(count)])]
  transfers between devices with their start and end apart: 10 -> 16, of which waited for: 2 -> 11; matrix products, arithmetic and copies ran while one was open for 62% -> 11% of each run, Pallas kernels for 0% -> 9%
where the time goes in v1:
time: 664 us; the launch traced here: 663 us
  waiting for transfers between devices  378 us (57%)
  Pallas kernels  90.7 us (14%)
  matrix products  62.7 us (9%)
  starting transfers between devices  40.4 us (6%)
  other arithmetic  31.1 us (5%)
  local copies, waits for them, and re-layouts  26.4 us (4%)
  blocking collectives  18.7 us (3%)
  between operations  14.3 us (2%)
    reduce_scatter x3, waiting for transfers between devices, on_device(): lax.psum_scatter(term, 'seq', scatter_dimension=0, tiled=True)  264 us
    ppermute x9, waiting for transfers between devices, flipped(): return lax.ppermute(value, axis, [(i, i ^ bit) for i in range(count)])  75 us
    pallas_call x1, Pallas kernels, recurrence_back(): pl.pallas_call(lambda *refs: backward_kernel(sizes, *refs), out_shape=(ja...  57.9 us
    pallas_call x1, Pallas kernels, recurrence(): pl.pallas_call(lambda *refs: forward_kernel(sizes, *refs), out_shape=(jax...  32.8 us
    dot_general x3, matrix products, inner_rows(): return lax.dot_general(left, right, TN, preferred_element_type=F32)  25 us
    dot_general x3, matrix products, outer_cols(): return lax.dot_general(left, right, NT, preferred_element_type=F32)  22.7 us
    all_to_all x1, waiting for transfers between devices, on_device(): lax.all_to_all(grad_mixed.T.reshape(pieces, channels, rows), 'seq', 0, 0)  22.2 us
    all_to_all x1, blocking collectives, on_device(): lax.all_to_all(mixed_rows.reshape(pieces, channels, rows), 'seq', 0, 0)  18.7 us
  transfers between devices with their start and end apart: 16, of which 11 were waited for; matrix products, arithmetic and copies ran while one was open for 11% of the time, Pallas kernels for 9%

profile of v1, /device:TPU:0, one launch (start us, length us, event | category | flops | bytes accessed | tf_op | source)
XLA Modules:
  0.0 662.8 jit_solution(4941218513440393756)
XLA Ops:
  12.7 7.4 %all-to-all-start = ((f32[16,72,128]{2,1,0:T(8,128)}), f32[16,72,128]{2,1,0:T(8,128)S(1)}, u32[]{:S(2)}, u32[]{:S(2)}) async-start(f32[16,72,128]{2,1,0:T(8,128)} %pad_maximum_fusion), calls=%async_computation | async-start | bytes 1179648 | tf_op jit(solution)/shard_map/all_to_all | solution.py:431
  24.5 11.1 %all-to-all-done = f32[16,72,128]{2,1,0:T(8,128)S(1)} async-done(((f32[16,72,128]{2,1,0:T(8,128)}), f32[16,72,128]{2,1,0:T(8,128)S(1)}, u32[]{:S(2)}, u32[]{:S(2)}) %all-to-all-start) | async-done | bytes 589856 | tf_op jit(solution)/shard_map/all_to_all | solution.py:431
  35.7 32.8 %recurrence.1 = (f32[1024,128]{1,0:T(8,128)S(1)}, f32[64,64,128]{2,1,0:T(8,128)S(1)}, f32[64,128]{1,0:T(8,128)S(1)}) custom-call(f32[1152,128]{1,0:T(8,128)S(1)} %bitcast.146, f32[64,128]{1,0:T(8,128)S(1)} %pad_maximum_fusion.1.refs_1_.refs_4_, f32[64,128]{1,0:T(8,128)S(1)} %pad_maximum_fusion.2.refs_2_.refs_5_, f32[64,128]{1,0:T(8,128)S(1)} %broadcast_in_dim.18.refs_3_.refs_6_), custom_call_target="tpu_custom_call" | custom-call | tf_op jit(solution)/shard_map/recurrence/pallas_call | solution.py:312
  68.5 18.7 %all_to_all.25 = f32[16,64,128]{2,1,0:T(8,128)S(1)} all-to-all(f32[16,64,128]{2,1,0:T(8,128)S(1)} %bitcast.150), channel_id=1, replica_groups=mesh['batch'=2,'seq'=16] {'seq'}, dimensions={0} | all-to-all | bytes 1048576 | tf_op jit(solution)/shard_map/all_to_all | solution.py:434
  96.5 5.4 convolution_add_fusion
  102.0 8.3 %convert_reduce_fusion = (f32[4096]{0:T(1024)S(1)}, bf16[128,4096]{1,0:T(8,128)(2,1)S(1)}, f32[128,4096]{1,0:T(8,128)}) fusion(f32[128,4096]{1,0:T(8,128)S(1)} %convolution_add_fusion, bf16[128,1024]{1,0:T(8,128)(2,1)S(1)} %bitcast.155, bf16[4096,1024]{1,0:T(8,128)(2,1)S(1)} %bitcast.152), kind=kOutput, calls=%fused_computation.4 | convolution fusion | flops 1112535040 | bytes 13910016 | tf_op jit(solution)/shard_map/dot_general | solution.py:362
  111.3 8.2 %fusion.59 = f32[1024,4096]{1,0:T(8,128)} fusion(bf16[128,4096]{1,0:T(8,128)(2,1)S(1)} %get-tuple-element.107, f32[128,1024]{1,0:T(8,128)S(1)} %get-tuple-element.122, f32[1024]{0:T(1024)S(1)} %copy-done.30, f32[1024]{0:T(1024)S(1)} %copy-done.29, f32[128]{0:T(128)S(1)} %fusion.56, f32[128]{0:T(128)S(1)} %broadcast_multiply_fusion.4), kind=kOutput, calls=%fused_computation.187 | convolution fusion | flops 1074397184 | bytes 18359296 | tf_op jit(solution)/shard_map/dot_general | solution.py:358
  123.3 11.4 %fusion.69 = f32[4096,1024]{1,0:T(8,128)} fusion(bf16[128,4096]{1,0:T(8,128)(2,1)S(1)} %multiply_convert_fusion, bf16[128,1024]{1,0:T(8,128)(2,1)S(1)} %bitcast.156), kind=kOutput, calls=%fused_computation.192 | convolution fusion | flops 1073741824 | bytes 18087936 | tf_op jit(solution)/shard_map/dot_general | solution.py:358
  134.7 8.5 %multiply_reduce_fusion = (f32[1024]{0:T(1024)S(1)}, f32[128]{0:T(128)S(1)}, f32[1024]{0:T(1024)S(1)}, f32[128,1024]{1,0:T(8,128)S(1)}) fusion(f32[128,1024]{1,0:T(8,128)S(1)} %get-tuple-element.122, f32[128]{0:T(128)S(1)} %fusion.56, f32[128]{0:T(128)S(1)} %broadcast_multiply_fusion.4, f32[1024]{0:T(1024)S(1)} %copy-done.29, ...), kind=kOutput, calls=%fused_computation.69 | convolution fusion | flops 1074788224 | bytes 10499584 | tf_op jit(solution)/shard_map/dot_general | solution.py:362
  145.9 5.4 fusion.60
  151.4 5.9 fusion.15
  164.2 22.2 %all-to-all-done.2 = f32[16,64,128]{2,1,0:T(8,128)S(1)} async-done(((f32[16,64,128]{2,1,0:T(8,128)}), f32[16,64,128]{2,1,0:T(8,128)S(1)}, u32[]{:S(2)}, u32[]{:S(2)}) %all-to-all-start.2) | async-done | bytes 524320 | tf_op jit(solution)/shard_map/all_to_all | solution.py:466
  186.5 57.9 %recurrence_back.1 = (f32[1024,128]{1,0:T(8,128)S(1)}, f32[64,128]{1,0:T(8,128)S(1)}, f32[64,128]{1,0:T(8,128)S(1)}, f32[64,128]{1,0:T(8,128)S(1)}, f32[64,128]{1,0:T(8,128)S(1)}, /*index=5*/f32[64,128]{1,0:T(8,128)S(1)}) custom-call(f32[1152,128]{1,0:T(8,128)S(1)} %bitcast.147, f32[1024,128]{1,0:T(8,128)S(1)} %bitcast.148, ...), custom_call_target="tpu_custom_call" | custom-call | tf_op jit(solution)/shard_map/recurrence_back/pallas_call | solution.py:330
  245.2 10.7 %all-to-all-start.3 = ((f32[16,64,128]{2,1,0:T(8,128)}), f32[16,64,128]{2,1,0:T(8,128)S(1)}, u32[]{:S(2)}, u32[]{:S(2)}) async-start(f32[16,64,128]{2,1,0:T(8,128)} %bitcast.149), calls=%async_computation.3 | async-start | bytes 1048576 | tf_op jit(solution)/shard_map/all_to_all | solution.py:471
  263.9 6.5 all-to-all-done.3
  271.7 4.2 all-to-all-start.4
  279.2 13.9 %collective-permute-done.3 = f32[72,128]{1,0:T(8,128)S(1)} collective-permute-done((f32[72,128]{1,0:T(8,128)S(1)}, f32[72,128]{1,0:T(8,128)S(1)}, u32[]{:S(2)}, u32[]{:S(2)}) %collective-permute-start.3) | collective-permute-done | bytes 36896 | tf_op jit(solution)/shard_map/ppermute | solution.py:367
  293.2 36.0 %collective-permute-done.4 = f32[72,128]{1,0:T(8,128)S(1)} collective-permute-done((f32[72,128]{1,0:T(8,128)S(1)}, f32[72,128]{1,0:T(8,128)S(1)}, u32[]{:S(2)}, u32[]{:S(2)}) %collective-permute-start.4) | collective-permute-done | bytes 36896 | tf_op jit(solution)/shard_map/ppermute | solution.py:367
  329.1 4.8 collective-permute-start.5
  333.9 13.5 %collective-permute-done.5 = f32[72,128]{1,0:T(8,128)S(1)} collective-permute-done((f32[72,128]{1,0:T(8,128)S(1)}, f32[72,128]{1,0:T(8,128)S(1)}, u32[]{:S(2)}, u32[]{:S(2)}) %collective-permute-start.5) | collective-permute-done | bytes 36896 | tf_op jit(solution)/shard_map/ppermute | solution.py:367
  348.9 5.3 fusion.7
  367.7 161.5 %reduce-scatter.8.cloned.1.call-done = f32[256,1024]{1,0:T(8,128)} async-done(((f32[4096,1024]{1,0:T(8,128)}), f32[256,1024]{1,0:T(8,128)}) %reduce-scatter.8.cloned.1.call-update) | async-done | bytes 1048592 | tf_op jit(solution)/shard_map/reduce_scatter | solution.py:503
  534.7 102.1 %reduce-scatter.4.cloned.1.call-done = f32[64,2048]{1,0:T(8,128)} async-done(((f32[1024,2048]{1,0:T(8,128)}), f32[64,2048]{1,0:T(8,128)}) %reduce-scatter.4.cloned.1.call-update) | async-done | bytes 524304 | tf_op jit(solution)/shard_map/reduce_scatter | solution.py:503
  643.6 7.2 %collective-permute-done.1 = f32[64,2048]{1,0:T(8,128)S(1)} collective-permute-done((f32[64,2048]{1,0:T(8,128)}, f32[64,2048]{1,0:T(8,128)S(1)}, u32[]{:S(2)}, u32[]{:S(2)}) %collective-permute-start.1) | collective-permute-done | bytes 524320 | tf_op jit(solution)/shard_map/ppermute | solution.py:367
  (189 shorter events, 79.6 us)
Async XLA Ops:
  11.6 12.4 %copy-start.33 = (f32[1024]{0:T(1024)S(1)}, f32[1024]{0:T(1024)}, u32[]{:S(2)}) copy-start(f32[1024]{0:T(1024)} %param.31) | copy-start | bytes 12292
  12.7 22.9 %all-to-all-start = ((f32[16,72,128]{2,1,0:T(8,128)}), f32[16,72,128]{2,1,0:T(8,128)S(1)}, u32[]{:S(2)}, u32[]{:S(2)}) async-start(f32[16,72,128]{2,1,0:T(8,128)} %pad_maximum_fusion), calls=%async_computation | async-start | bytes 1179648 | tf_op jit(solution)/shard_map/all_to_all | solution.py:431
  20.1 347.1 %reduce-scatter.6.cloned.1.call-start = ((), (), s32[]{:S(2)}) async-start(), calls=%async_computation.9 | async-start | bytes 17825792 | tf_op jit(solution)/shard_map/reduce_scatter | solution.py:503
  95.7 47.5 %copy-start.1 = (f32[128,1024]{1,0:T(8,128)}, f32[128,1024]{1,0:T(8,128)S(1)}, u32[]{:S(2)}) copy-start(f32[128,1024]{1,0:T(8,128)S(1)} %get-tuple-element.122) | copy-start | bytes 1572868
  119.6 409.6 %reduce-scatter.8.cloned.1.call-start = ((), (), s32[]{:S(2)}) async-start(), calls=%async_computation.10 | async-start | bytes 17825792 | tf_op jit(solution)/shard_map/reduce_scatter | solution.py:503
  134.7 502.2 %reduce-scatter.4.cloned.1.call-start = ((), (), s32[]{:S(2)}) async-start(), calls=%async_computation.8 | async-start | bytes 8912896 | tf_op jit(solution)/shard_map/reduce_scatter | solution.py:503
  159.4 27.0 %all-to-all-start.2 = ((f32[16,64,128]{2,1,0:T(8,128)}), f32[16,64,128]{2,1,0:T(8,128)S(1)}, u32[]{:S(2)}, u32[]{:S(2)}) async-start(f32[16,64,128]{2,1,0:T(8,128)} %bitcast.160), calls=%async_computation.2 | async-start | bytes 1048576 | tf_op jit(solution)/shard_map/all_to_all | solution.py:466
  245.2 25.2 %all-to-all-start.3 = ((f32[16,64,128]{2,1,0:T(8,128)}), f32[16,64,128]{2,1,0:T(8,128)S(1)}, u32[]{:S(2)}, u32[]{:S(2)}) async-start(f32[16,64,128]{2,1,0:T(8,128)} %bitcast.149), calls=%async_computation.3 | async-start | bytes 1048576 | tf_op jit(solution)/shard_map/all_to_all | solution.py:471
  258.7 5.2 collective-permute-start
  271.7 77.2 %copy-start.2 = (f32[128,1024]{1,0:T(8,128)S(1)}, f32[128,1024]{1,0:T(8,128)}, u32[]{:S(2)}) copy-start(f32[128,1024]{1,0:T(8,128)} %copy-done.1) | copy-start | bytes 1572868
  271.7 77.2 %copy-start.4 = (bf16[128,4096]{1,0:T(8,128)(2,1)S(1)}, bf16[128,4096]{1,0:T(8,128)(2,1)}, u32[]{:S(2)}) copy-start(bf16[128,4096]{1,0:T(8,128)(2,1)} %copy-done.3) | copy-start | bytes 3145732
  271.7 77.2 %copy-start.34 = (f32[1024]{0:T(1024)S(1)}, f32[1024]{0:T(1024)}, u32[]{:S(2)}) copy-start(f32[1024]{0:T(1024)} %param.40) | copy-start | bytes 12292
  271.7 87.0 %all-to-all-start.4 = ((f32[16,64,384]{2,1,0:T(8,128)}), f32[16,64,384]{2,1,0:T(8,128)S(1)}, u32[]{:S(2)}, u32[]{:S(2)}) async-start(f32[16,64,384]{2,1,0:T(8,128)} %broadcast_in_dim.23), calls=%async_computation.4 | async-start | bytes 3145728 | tf_op jit(solution)/shard_map/all_to_all | solution.py:484
  276.0 1.3 collective-permute-start.2
  277.3 15.7 %collective-permute-start.3 = (f32[72,128]{1,0:T(8,128)S(1)}, f32[72,128]{1,0:T(8,128)S(1)}, u32[]{:S(2)}, u32[]{:S(2)}) collective-permute-start(f32[72,128]{1,0:T(8,128)S(1)} %bitcast_add_fusion.1), channel_id=1, source_target_pairs={{0,2},{1,3},{2,0},{3,1},{4,6},{5,7},{6,4},{7,5},{8,10},{9,11},{10,... | collective-permute-start | bytes 110600 | tf_op jit(solution)/shard_map/ppermute | solution.py:367
  293.1 36.0 %collective-permute-start.4 = (f32[72,128]{1,0:T(8,128)S(1)}, f32[72,128]{1,0:T(8,128)S(1)}, u32[]{:S(2)}, u32[]{:S(2)}) collective-permute-start(f32[72,128]{1,0:T(8,128)S(1)} %fusion.82), channel_id=1, source_target_pairs={{0,4},{1,5},{2,6},{3,7},{4,0},{5,1},{6,2},{7,3},{8,12},{9,13},{10,... | collective-permute-start | bytes 110600 | tf_op jit(solution)/shard_map/ppermute | solution.py:367
  329.1 18.3 %collective-permute-start.5 = (f32[72,128]{1,0:T(8,128)S(1)}, f32[72,128]{1,0:T(8,128)S(1)}, u32[]{:S(2)}, u32[]{:S(2)}) collective-permute-start(f32[72,128]{1,0:T(8,128)S(1)} %add.185), channel_id=1, source_target_pairs={{0,8},{1,9},{2,10},{3,11},{4,12},{5,13},{6,14},{7,15},{8,0},{9,1},... | collective-permute-start | bytes 110600 | tf_op jit(solution)/shard_map/ppermute | solution.py:367
  347.4 6.9 %collective-permute-start.6 = (f32[72,128]{1,0:T(8,128)S(1)}, f32[72,128]{1,0:T(8,128)S(1)}, u32[]{:S(2)}, u32[]{:S(2)}) collective-permute-start(f32[72,128]{1,0:T(8,128)S(1)} %add.186), channel_id=1, source_target_pairs={{0,16},{16,0},{1,17},{17,1},{2,18},{18,2},{3,19},{19,3},{4,20},{20... | collective-permute-start | bytes 110600 | tf_op jit(solution)/shard_map/ppermute | solution.py:367
  367.2 284.5 %collective-permute-start.7 = (f32[64,4096]{1,0:T(8,128)}, f32[64,4096]{1,0:T(8,128)}, u32[]{:S(2)}, u32[]{:S(2)}) collective-permute-start(f32[64,4096]{1,0:T(8,128)} %reduce-scatter.6.cloned.1.call-done), channel_id=1, source_target_pairs={{0,16},{16,0},{1,17},{17,1},{2,18},{18,2},{3,19},{19,3},{4,20},{20... | collective-permute-start | bytes 3145736 | tf_op jit(solution)/shard_map/ppermute | solution.py:367
  529.2 124.8 %collective-permute-start.8 = (f32[256,1024]{1,0:T(8,128)}, f32[256,1024]{1,0:T(8,128)}, u32[]{:S(2)}, u32[]{:S(2)}) collective-permute-start(f32[256,1024]{1,0:T(8,128)} %reduce-scatter.8.cloned.1.call-done), channel_id=1, source_target_pairs={{0,16},{16,0},{1,17},{17,1},{2,18},{18,2},{3,19},{19,3},{4,20},{20... | collective-permute-start | bytes 3145736 | tf_op jit(solution)/shard_map/ppermute | solution.py:367
  530.6 109.7 %copy-start.21 = (f32[1024,64]{0,1:T(8,128)S(1)}, f32[1024,64]{0,1:T(8,128)}, u32[]{:S(2)}) copy-start(f32[1024,64]{0,1:T(8,128)} %param.25) | copy-start | bytes 786436
  532.6 107.7 %copy-start.24 = (f32[1024,64]{0,1:T(8,128)S(1)}, f32[1024,64]{0,1:T(8,128)}, u32[]{:S(2)}) copy-start(f32[1024,64]{0,1:T(8,128)} %get-tuple-element.110) | copy-start | bytes 786436
  532.6 107.7 %copy-start.25 = (f32[1024,64]{0,1:T(8,128)S(1)}, f32[1024,64]{0,1:T(8,128)}, u32[]{:S(2)}) copy-start(f32[1024,64]{0,1:T(8,128)} %get-tuple-element.115) | copy-start | bytes 786436
  636.9 13.9 %collective-permute-start.1 = (f32[64,2048]{1,0:T(8,128)}, f32[64,2048]{1,0:T(8,128)S(1)}, u32[]{:S(2)}, u32[]{:S(2)}) collective-permute-start(f32[64,2048]{1,0:T(8,128)} %reduce-scatter.4.cloned.1.call-done), channel_id=1, source_target_pairs={{0,16},{16,0},{1,17},{17,1},{2,18},{18,2},{3,19},{19,3},{4,20},{20... | collective-permute-start | bytes 1572872 | tf_op jit(solution)/shard_map/ppermute | solution.py:367
  (30 other events, 130.4 us)
Sparse Core Ops, SparseCore 0:
  119.7 227.5 reduce-scatter.5
  351.3 177.7 reduce-scatter.7
  533.3 103.5 reduce-scatter.3

commit v2 on v1

v2 whole, which is shorter than its diff:
```python
import jax, jax.numpy as jnp
from jax import lax
from jax.sharding import PartitionSpec as P
from jax.experimental import pallas as pl
from jax.experimental.pallas import tpu as pltpu
F32, BF16 = jnp.float32, jnp.bfloat16
LANES = 128
HALF = 64
FORWARD_UNROLL = 16
BACKWARD_UNROLL = 8
NN = (((1,), (0,)), ((), ()))
NT = (((1,), (1,)), ((), ()))
TN = (((0,), (0,)), ((), ()))


def halves(value):
    high = value.astype(BF16)
    return high, (value - high.astype(F32)).astype(BF16)


def dot(left, right, dims):
    return lax.dot_general(left, right, dims, preferred_element_type=F32)


def beside(parts):
    return jnp.concatenate(parts, axis=1)


def below(parts):
    return jnp.concatenate(parts, axis=0)


def mm(left, right):
    table = beside(right)
    out = dot(beside(left), below([table, table]), NN)
    return out[:, :LANES] + out[:, LANES:]


def mm_turned(left, right):
    out = dot(beside(left), below([beside([right[0]] * 2), beside([right[1]] * 2)]), NT)
    return out[:, :LANES] + out[:, LANES:]


def swap(value):
    return pltpu.roll(value, HALF, value.ndim - 1)


def low_lanes(shape):
    return lax.broadcasted_iota(jnp.int32, shape, len(shape) - 1) < HALF


def as_factor(value):
    turned = swap(value)
    low = low_lanes(value.shape)
    return jnp.where(low, value, turned), jnp.where(low, -turned, value)


def times(value, factor):
    return value * factor[0] + swap(value) * factor[1]


def power_setup(lam, base_ref, fre_ref, fim_ref, steps, channels):
    one = jnp.where(low_lanes(lam.shape), 1.0, 0.0)
    factor = as_factor(lam)
    row = one
    for k in range(8):
        base_ref[pl.ds(k * channels, channels), :] = row
        row = times(row, factor)
    eight = as_factor(row)
    row = one
    for i in range(16):
        fre, fim = as_factor(row)
        fre_ref[pl.ds(i * channels, channels), :] = fre
        fim_ref[pl.ds(i * channels, channels), :] = fim
        row = times(row, eight)
    for s in range(steps):
        fre, fim = as_factor(row)
        fre_ref[pl.ds((16 + s) * channels, channels), :] = fre
        fim_ref[pl.ds((16 + s) * channels, channels), :] = fim
        row = times(row, (fre, fim))


def power_tables(h, base_ref, fre_ref, fim_ref, channels):
    base = base_ref[pl.ds(h, 8, stride=channels), :]
    turned = swap(base)
    return below([
        base * fre_ref[pl.ds(h + i * channels, 1), :] + turned * fim_ref[pl.ds(h + i * channels, 1), :]
        for i in range(16)
    ])


def reversed_tables(h, base_ref, fre_ref, fim_ref, channels):
    base = below([base_ref[pl.ds(h + k * channels, 1), :] for k in range(7, -1, -1)])
    turned = swap(base)
    return below([
        base * fre_ref[pl.ds(h + i * channels, 1), :] + turned * fim_ref[pl.ds(h + i * channels, 1), :]
        for i in range(15, -1, -1)
    ])


def doc_masks(seg_ref, mask_ref, row, pitch, chunks, docs, turn):
    even = seg_ref[pl.ds(row, chunks, stride=2 * pitch), :]
    odd = seg_ref[pl.ds(row + pitch, chunks, stride=2 * pitch), :]
    pair = join(even, odd)
    at = lax.broadcasted_iota(jnp.int32, (LANES, LANES), 0)
    to = lax.broadcasted_iota(jnp.int32, (LANES, LANES), 1)
    turning = jnp.where(at + to == LANES - 1, 1.0, 0.0).astype(BF16)
    for d in range(docs):
        for c in range(2):
            mask = jnp.where(pair[c] == float(d), 1.0, 0.0)
            mask_ref[d * 2 + c] = mask
            if turn:
                mask_ref[(docs + d) * 2 + c] = dot(mask.astype(BF16), turning, NN)


def join(even, odd):
    low = low_lanes(even.shape)
    return jnp.where(low, even, swap(odd)), jnp.where(low, swap(even), odd)


def join_turned(even, odd):
    low = low_lanes(even.shape)
    return jnp.where(low, swap(odd), even), jnp.where(low, odd, swap(even))


def apart_turned(first, second):
    low = low_lanes(first.shape)
    return jnp.where(low, swap(second), first), jnp.where(low, second, swap(first))


def spread(pair, mask_ref, docs, base=0):
    return below([pair[c] * mask_ref[base + d * 2 + c] for d in range(docs) for c in range(2)])


def gathered(rows, mask_ref, chunks, docs, base=0):
    out = []
    for c in range(2):
        total = None
        for d in range(docs):
            at = (d * 2 + c) * chunks
            term = rows[at : at + chunks] * mask_ref[base + d * 2 + c]
            total = term if total is None else total + term
        out.append(total)
    return out


def scan_factors(h, fre_ref, fim_ref, channels, chunks, steps, backward):
    at = lax.broadcasted_iota(jnp.int32, (chunks, LANES), 0)
    out = []
    for s in range(steps):
        keep = at < chunks - (1 << s) if backward else at >= (1 << s)
        fre = fre_ref[pl.ds(h + (16 + s) * channels, 1), :]
        fim = fim_ref[pl.ds(h + (16 + s) * channels, 1), :]
        out.append((jnp.where(keep, fre, 0.0), jnp.where(keep, fim, 0.0)))
    return out


def scan_chunks(rows, factors, chunks, backward):
    at = lax.broadcasted_iota(jnp.int32, (chunks, LANES), 0)
    keep = at < chunks - 1 if backward else at >= 1
    out = []
    for i in range(rows.shape[0] // chunks):
        part = rows[i * chunks : (i + 1) * chunks]
        for s, factor in enumerate(factors):
            moved = pltpu.roll(part, chunks - (1 << s) if backward else 1 << s, 0)
            part = part + times(moved, factor)
        moved = pltpu.roll(part, chunks - 1 if backward else 1, 0)
        out.append(jnp.where(keep, moved, 0.0))
    return jnp.concatenate(out, axis=0)


def toeplitz(row):
    wide = jnp.broadcast_to(row, (LANES, LANES))
    wide = pltpu.roll(wide, 0, 1, stride=1, stride_axis=0)
    j = lax.broadcasted_iota(jnp.int32, (LANES, LANES), 0)
    t = lax.broadcasted_iota(jnp.int32, (LANES, LANES), 1)
    return jnp.where(t >= j, wide, 0.0)


def turned_lag_sums(table):
    moved = pltpu.roll(table, 0, 1, stride=1, stride_axis=0)
    at = lax.broadcasted_iota(jnp.int32, (LANES, LANES), 0)
    lane = lax.broadcasted_iota(jnp.int32, (LANES, LANES), 1)
    return jnp.sum(jnp.where(lane >= at, moved, 0.0), axis=0, keepdims=True)


def together(works):
    while works:
        works = [work for work in works if next(work, None)]


def first_rows(first, second):
    at = lax.broadcasted_iota(jnp.int32, (8, LANES), 0)
    return jnp.where(at == 0, first, jnp.where(at == 1, second, 0.0))


def forward_kernel(
    sizes, recv_ref, lam_ref, weight_ref, skip_ref, out_ref, enter_ref, lag_ref,
    base_ref, fre_ref, fim_ref, mask_ref,
):
    channels, chunks, docs, steps, pitch, unroll = sizes
    rows = docs * 2 * chunks
    power_setup(lam_ref[...], base_ref, fre_ref, fim_ref, steps, channels)
    doc_masks(recv_ref, mask_ref, channels, pitch, chunks, docs, False)

    def one(h):
        pair = join(
            recv_ref[pl.ds(h, chunks, stride=2 * pitch), :],
            recv_ref[pl.ds(h + pitch, chunks, stride=2 * pitch), :],
        )
        inputs = halves(spread(pair, mask_ref, docs))
        power = halves(power_tables(h, base_ref, fre_ref, fim_ref, channels))
        yield True
        back = halves(reversed_tables(h, base_ref, fre_ref, fim_ref, channels))
        weight = weight_ref[pl.ds(h, 1), :]
        low = low_lanes((1, LANES))
        signed = halves(jnp.where(low, weight, -weight))
        both = first_rows(signed[0].astype(F32), signed[1].astype(F32)).astype(BF16)
        yield True
        lags = dot(both, below(power), NT)
        lags = lags[0:1] + lags[1:2]
        lags = lags[:, :LANES] + lags[:, LANES:]
        lag_ref[pl.ds(h, 1), :] = lags
        yield True
        table = halves(toeplitz(lags))
        yield True
        out = dot(below(inputs), beside([back[0], table[0]]), NN)
        out = out[:rows] + out[rows:] + dot(inputs[0], beside([back[1], table[1]]), NN)
        yield True
        enter = scan_chunks(
            out[:, :LANES], scan_factors(h, fre_ref, fim_ref, channels, chunks, steps, False), chunks, False
        )
        enter_ref[h] = enter
        yield True
        lam = as_factor(lam_ref[pl.ds(h, 1), :])
        coef = as_factor(times(weight, lam))
        coef = (jnp.where(low, coef[0], -coef[0]), jnp.where(low, coef[1], -coef[1]))
        yield True
        mixed = out[:, LANES:] + mm_turned(halves(times(enter, coef)), power)
        yield True
        first, second = gathered(mixed, mask_ref, chunks, docs)
        skip = skip_ref[pl.ds(h, 1), :]
        even, odd = join(first + skip * pair[0], second + skip * pair[1])
        out_ref[pl.ds(h, chunks, stride=2 * channels), :] = even
        out_ref[pl.ds(h + channels, chunks, stride=2 * channels), :] = odd

    def several(i, carry):
        together([one(i * unroll + k) for k in range(unroll)])
        return carry

    lax.fori_loop(0, channels // unroll, several, 0)


def backward_kernel(
    sizes, recv_ref, grad_ref, enter_ref, lag_ref, lam_ref, weight_ref, skip_ref,
    out_ref, sum_ref, first_ref, lagsum_ref, bias_ref,
    base_ref, fre_ref, fim_ref, mask_ref,
):
    channels, chunks, docs, steps, pitch, unroll = sizes
    rows = docs * 2 * chunks
    power_setup(lam_ref[...], base_ref, fre_ref, fim_ref, steps, channels)
    doc_masks(recv_ref, mask_ref, channels, pitch, chunks, docs, True)
    reach = (LANES - 1 - lax.broadcasted_iota(jnp.int32, (1, LANES), 1)).astype(F32)

    def one(h):
        pair = join(
            recv_ref[pl.ds(h, chunks, stride=2 * pitch), :],
            recv_ref[pl.ds(h + pitch, chunks, stride=2 * pitch), :],
        )
        gpair = join_turned(
            grad_ref[pl.ds(h, chunks, stride=2 * channels), :],
            grad_ref[pl.ds(h + channels, chunks, stride=2 * channels), :],
        )
        inputs = spread(pair, mask_ref, docs)
        grads = spread(gpair, mask_ref, docs, docs * 2)
        ih, il = halves(inputs)
        gh, gl = halves(grads)
        yield True
        lagsum = turned_lag_sums(dot(below([gh, gl, gh]), below([ih, ih, il]), TN))
        lagsum_ref[pl.ds(h, 1), :] = lagsum
        yield True
        power = halves(power_tables(h, base_ref, fre_ref, fim_ref, channels))
        yield True
        back = halves(reversed_tables(h, base_ref, fre_ref, fim_ref, channels))
        weight = weight_ref[pl.ds(h, 1), :]
        lam = as_factor(lam_ref[pl.ds(h, 1), :])
        yield True
        table = halves(toeplitz(lag_ref[pl.ds(h, 1), :]))
        yield True
        enter = enter_ref[h]
        ahead = scan_factors(h, fre_ref, fim_ref, channels, chunks, steps, False)
        astern = scan_factors(h, fre_ref, fim_ref, channels, chunks, steps, True)
        i1h, i1l = halves(inputs * reach)
        g1h, g1l = halves(grads * reach)
        lh, ll = halves(first_rows(lagsum, lagsum * reach))
        yield True
        out = mm((below([i1h, gh, g1h, lh]), below([i1l, gl, g1l, ll])), back)
        yield True
        hop = (
            fre_ref[pl.ds(h + 16 * channels, 1), :] * float(LANES),
            fim_ref[pl.ds(h + 16 * channels, 1), :] * float(LANES),
        )
        turned = swap(enter)
        enter1 = scan_chunks(
            out[:rows] + enter * hop[0] + turned * hop[1], ahead, chunks, False
        )
        yield True
        seen = out[rows : 2 * rows]
        seen1 = seen + out[2 * rows : 3 * rows]
        seen_t = swap(seen)

        def summed_product(plain, crossed):
            plain = jnp.sum(plain, axis=0, keepdims=True)
            crossed = jnp.sum(crossed, axis=0, keepdims=True)
            low = low_lanes((1, LANES))
            plain, crossed = plain - swap(plain), crossed + swap(crossed)
            return times(jnp.where(low, plain, crossed), lam)

        sum_ref[pl.ds(h, 1), :] = (
            summed_product(enter * seen, turned * seen) + out[3 * rows : 3 * rows + 1]
        )
        first_ref[pl.ds(h, 1), :] = summed_product(
            enter1 * seen + enter * seen1, enter1 * seen_t + turned * seen1
        ) + out[3 * rows + 1 : 3 * rows + 2]
        yield True
        coef = as_factor(times(weight, lam))
        leave = scan_chunks(seen * coef[0] + seen_t * coef[1], astern, chunks, True)
        leave = jnp.where(low_lanes(leave.shape), leave, -leave)
        yield True
        inner = mm((gh, gl), table) + mm_turned(halves(leave), power)
        yield True
        gfirst, gsecond = gathered(inner, mask_ref, chunks, docs, docs * 2)
        skip = skip_ref[pl.ds(h, 1), :]
        gfirst = gfirst + skip * gpair[0]
        gsecond = gsecond + skip * gpair[1]
        bias_ref[pl.ds(h, 1), :] = jnp.sum(gfirst + gsecond, axis=0, keepdims=True)
        even, odd = apart_turned(gfirst, gsecond)
        out_ref[pl.ds(h, chunks, stride=2 * channels), :] = even
        out_ref[pl.ds(h + channels, chunks, stride=2 * channels), :] = odd

    def several(i, carry):
        together([one(i * unroll + k) for k in range(unroll)])
        return carry

    lax.fori_loop(0, channels // unroll, several, 0)


REACH = 512


def kernel_sizes(recv_rows, channels, pieces, docs, unroll):
    chunks = pieces // 2
    unroll = min(channels, max(1, unroll * 64 // (docs * 2 * chunks)))
    steps = min((chunks - 1).bit_length(), (REACH // LANES - 1).bit_length())
    return (channels, chunks, docs, steps, channels + 8, unroll)


def scratch(channels, chunks, docs, steps):
    return [
        pltpu.VMEM((8 * channels, LANES), F32),
        pltpu.VMEM(((16 + steps) * channels, LANES), F32),
        pltpu.VMEM(((16 + steps) * channels, LANES), F32),
        pltpu.VMEM((docs * 4, chunks, LANES), F32),
    ]


def recurrence(recv, lam, weight, skip, pieces, docs, unroll=2):
    channels = lam.shape[0]
    sizes = kernel_sizes(recv.shape[0], channels, pieces, docs, unroll)
    chunks, steps = sizes[1], sizes[3]
    rows = docs * 2 * chunks
    return pl.pallas_call(
        lambda *refs: forward_kernel(sizes, *refs),
        out_shape=(
            jax.ShapeDtypeStruct((pieces * channels, LANES), F32),
            jax.ShapeDtypeStruct((channels, rows, LANES), F32),
            jax.ShapeDtypeStruct((channels, LANES), F32),
        ),
        scratch_shapes=scratch(channels, chunks, docs, steps),
        compiler_params=pltpu.CompilerParams(vmem_limit_bytes=48 << 20),
        cost_estimate=estimate(16),
        name="recurrence",
    )(recv, lam, weight, skip)


def recurrence_back(recv, grad, enter, lags, lam, weight, skip, pieces, docs, unroll=2):
    channels = lam.shape[0]
    sizes = kernel_sizes(recv.shape[0], channels, pieces, docs, unroll)
    chunks, steps = sizes[1], sizes[3]
    row = jax.ShapeDtypeStruct((channels, LANES), F32)
    return pl.pallas_call(
        lambda *refs: backward_kernel(sizes, *refs),
        out_shape=(jax.ShapeDtypeStruct((pieces * channels, LANES), F32), row, row, row, row),
        scratch_shapes=scratch(channels, chunks, docs, steps),
        compiler_params=pltpu.CompilerParams(vmem_limit_bytes=48 << 20),
        cost_estimate=estimate(30),
        name="recurrence_back",
    )(recv, grad, enter, lags, lam, weight, skip)


EPSILON = 1e-05
MIB = 1 << 20


def estimate(micros, moved=0):
    return pl.CostEstimate(flops=int(micros * 1e9), transcendentals=0, bytes_accessed=int(moved))


def bell(values):
    share = 0.5 + 0.5 * lax.erf(values * 0.7071067811865476)
    return share, values * jnp.exp(-0.5 * values * values) * 0.3989422804014327


def sent_rows(values, out_ref, channels):
    turned = values.T
    for s in range(out_ref.shape[0]):
        out_ref[s, 0:channels, :] = turned[s * channels : (s + 1) * channels]


def normalize(values):
    centre = values - jnp.mean(values, axis=1, keepdims=True)
    recip = lax.rsqrt(jnp.mean(centre * centre, axis=1, keepdims=True) + EPSILON)
    return centre * recip, recip


def norm_back(grad, unit, recip):
    return recip * (
        grad
        - jnp.mean(grad, axis=1, keepdims=True)
        - unit * jnp.mean(grad * unit, axis=1, keepdims=True)
    )


def turning(size):
    at = lax.broadcasted_iota(jnp.int32, (size, size), 0)
    to = lax.broadcasted_iota(jnp.int32, (size, size), 1)
    return jnp.where(at + to == size - 1, 1.0, 0.0).astype(BF16)


def first_kernel(tokens_ref, cot_ref, seg_ref, gain_ref, bias_ref, send_ref, up_ref):
    pieces, pitch, rows = send_ref.shape
    channels = pitch - 8
    unit, _ = normalize(tokens_ref[...].astype(F32))
    sent_rows(unit * gain_ref[...] + bias_ref[...], send_ref, channels)
    seg = jnp.broadcast_to(seg_ref[...].astype(F32), (8, rows))
    for s in range(pieces):
        send_ref[s, channels:pitch, :] = seg
    up_ref[...] = cot_ref[...].astype(F32)


def last_kernel(back_ref, tokens_ref, gain_ref, hidden_ref, out_ref):
    unit, recip = normalize(tokens_ref[...].astype(F32))
    turn = turning(tokens_ref.shape[0])
    high, low = halves(back_ref[...])
    grad = (dot(turn, high, NT) + dot(turn, low, NT)) * gain_ref[...]
    out_ref[...] = (hidden_ref[...] + norm_back(grad, unit, recip)).astype(BF16)


def fetch(source, target, sems, chunks, rows):
    out = []
    wide = source.shape[0 if rows else 1] // chunks
    for i in range(chunks):
        part = (pl.ds(i * wide, wide), slice(None)) if rows else (slice(None), pl.ds(i * wide, wide))
        copy = pltpu.make_async_copy(source.at[part], target.at[part], sems.at[i])
        copy.start()
        out.append(copy)
    return out


def by_core(values, place_ref, out_ref, at, pieces):
    wide = values.shape[1] // pieces
    for s in range(pieces):
        slot = (s % 2) ^ place_ref[0]
        out_ref[slot, at, :, (s // 2) * wide : (s // 2 + 1) * wide] = values[:, s * wide : (s + 1) * wide]


def upward_kernel(
    pieces, place_ref, mixed_ref, tokens_ref, glu_bias_ref, gain_ref, bias_ref, ffn_bias_ref, glu_ref, ffn_ref,
    acts_ref, keep_ref, pre_ref, hidden_ref, slope1_ref, slope2_ref, low_ref,
    glu_v, ffn_v, glu_sem, ffn_sem,
):
    rows, features = tokens_ref.shape
    glu_copies = fetch(glu_ref, glu_v, glu_sem, 4, False)
    ffn_copies = fetch(ffn_ref, ffn_v, ffn_sem, 8, False)
    mixed = mixed_ref[...].T
    share, steep = bell(mixed)
    slope1_ref[...] = share + steep
    act = (mixed * share).astype(BF16)
    by_core(act.astype(F32), place_ref, acts_ref, 0, pieces)
    wide = glu_ref.shape[1] // 4
    for i in range(4):
        glu_copies[i].wait()
        at = slice(i * wide, (i + 1) * wide)
        pre_ref[:, at] = (
            jnp.dot(act, glu_v[:, at], preferred_element_type=F32) + glu_bias_ref[:, at]
        )
    hidden = tokens_ref[...].astype(F32) + pre_ref[:, :features] * jax.nn.sigmoid(pre_ref[:, features:])
    hidden_ref[...] = hidden
    unit, _ = normalize(hidden)
    normed = (unit * gain_ref[...] + bias_ref[...]).astype(BF16)
    by_core(normed.astype(F32), place_ref, acts_ref, 1, pieces)
    wide = ffn_ref.shape[1] // 8
    block = ffn_ref.shape[1] // pieces // 2
    for i in range(8):
        ffn_copies[i].wait()
        at = slice(i * wide, (i + 1) * wide)
        ffn_pre = jnp.dot(normed, ffn_v[:, at], preferred_element_type=F32) + ffn_bias_ref[:, at]
        share, steep = bell(ffn_pre)
        slope2_ref[:, at] = share + steep
        low = (ffn_pre * share).astype(BF16)
        low_ref[:, at] = low
        wider = low.astype(F32)
        for k in range(wide // block):
            index = (i * wide) // block + k
            piece, half = index // 2, index % 2
            keep_ref[
                half ^ place_ref[1], (piece % 2) ^ place_ref[0], :,
                (piece // 2) * block : (piece // 2 + 1) * block,
            ] = wider[:, k * block : (k + 1) * block]


def downward_kernel(
    place_ref, cot_ref, slope2_ref, hidden_ref, pre_ref, slope1_ref, gain_ref, out_w_ref, in_w_ref, glu_w_ref,
    sent_pre_ref, sent_glu_ref, grad_hidden_ref, turned_ref, in_sum_ref, glu_sum_ref, gain_sum_ref,
    bias_sum_ref, out_sum_ref,
    out_v, in_v, glu_v, out_sem, in_sem, glu_sem,
):
    rows, features = cot_ref.shape
    inner = out_w_ref.shape[0]
    wide = inner // 8
    out_copies = fetch(out_w_ref, out_v, out_sem, 8, True)
    in_copies = fetch(in_w_ref, in_v, in_sem, 8, False)
    glu_copies = fetch(glu_w_ref, glu_v, glu_sem, 1, False)
    cot = cot_ref[...]
    up = cot.astype(F32)
    out_sum_ref[...] = jnp.sum(up, axis=0, keepdims=True)
    total = jnp.zeros((rows, features), F32)
    for i in range(8):
        at = slice(i * wide, (i + 1) * wide)
        out_copies[i].wait()
        grad = lax.dot_general(cot, out_v[at, :], NT, preferred_element_type=F32)
        low = (grad * slope2_ref[:, at]).astype(BF16)
        wider = low.astype(F32)
        in_sum_ref[:, at] = jnp.sum(wider, axis=0, keepdims=True)
        sent_pre_ref[(i // 4) ^ place_ref[1], :, (i % 4) * wide : (i % 4 + 1) * wide] = wider
        in_copies[i].wait()
        total = total + lax.dot_general(low, in_v[:, at], NT, preferred_element_type=F32)
    unit, recip = normalize(hidden_ref[...])
    gain_sum_ref[...] = jnp.sum(total * unit, axis=0, keepdims=True)
    bias_sum_ref[...] = jnp.sum(total, axis=0, keepdims=True)
    grad_hidden = up + norm_back(total * gain_ref[...], unit, recip)
    grad_hidden_ref[...] = grad_hidden
    gate = jax.nn.sigmoid(pre_ref[:, features:])
    first = (grad_hidden * gate).astype(BF16)
    second = (grad_hidden * pre_ref[:, :features] * (gate * (1.0 - gate))).astype(BF16)
    glu_copies[0].wait()
    grad_act = None
    for k, part in enumerate((first, second)):
        wider = part.astype(F32)
        at = slice(k * features, (k + 1) * features)
        glu_sum_ref[:, at] = jnp.sum(wider, axis=0, keepdims=True)
        sent_glu_ref[k ^ place_ref[1]] = wider
        term = lax.dot_general(part, glu_v[:, at], NT, preferred_element_type=F32)
        grad_act = term if grad_act is None else grad_act + term
    turn = turning(rows)
    high, low = halves(grad_act * slope1_ref[...])
    turned_ref[...] = (dot(turn, high, NN) + dot(turn, low, NN)).T


def product_kernel(count, place_ref, *refs):
    lefts, rights = refs[:count], refs[count : 2 * count]
    keep_ref, send_ref, scratch_ref = refs[2 * count :]
    total = None
    for left, right in zip(lefts, rights):
        term = lax.dot_general(
            left[...].astype(BF16), right[...].astype(BF16), TN, preferred_element_type=F32
        )
        total = term if total is None else total + term
    scratch_ref[...] = total
    height = keep_ref.shape[1]
    for i in range(keep_ref.shape[0]):
        for ref, other in ((keep_ref, 0), (send_ref, 1)):
            block = 2 * i + (place_ref[2] ^ other)
            ref[i] = scratch_ref[pl.ds(pl.multiple_of(block * height, 8), height), :]


SMEM = pl.BlockSpec(memory_space=pltpu.SMEM)
VMEM = pl.BlockSpec(memory_space=pltpu.VMEM)
ANY = pl.BlockSpec(memory_space=pl.ANY)


def shaped(*shape, dtype=F32):
    return jax.ShapeDtypeStruct(shape, dtype)


def params_of(mib):
    return pltpu.CompilerParams(vmem_limit_bytes=mib * MIB)


def first_norm(tokens, cot, seg, gain, bias, pieces):
    rows, features = tokens.shape
    return pl.pallas_call(
        first_kernel,
        out_shape=(shaped(pieces, features // pieces + 8, rows), shaped(rows, features)),
        compiler_params=params_of(16), cost_estimate=estimate(4), name="first_norm",
    )(tokens, cot, seg, gain, bias)


def last_norm(back, tokens, gain, grad_hidden):
    return pl.pallas_call(
        last_kernel, out_shape=shaped(*tokens.shape, dtype=BF16),
        compiler_params=params_of(16), cost_estimate=estimate(4), name="last_norm",
    )(back, tokens, gain, grad_hidden)


def upward(place, mixed, tokens, glu_bias, gain, bias, ffn_bias, glu_weight, ffn_in, pieces):
    rows, features = tokens.shape
    inner = ffn_in.shape[1]
    return pl.pallas_call(
        lambda *refs: upward_kernel(pieces, *refs),
        in_specs=[SMEM] + [VMEM] * 6 + [ANY] * 2,
        out_shape=(
            shaped(2, 2, rows, features // 2), shaped(2, 2, rows, inner // 4), shaped(rows, 2 * features),
            shaped(rows, features), shaped(rows, features), shaped(rows, inner), shaped(rows, inner, dtype=BF16),
        ),
        scratch_shapes=[
            pltpu.VMEM(glu_weight.shape, BF16), pltpu.VMEM(ffn_in.shape, BF16),
            pltpu.SemaphoreType.DMA((4,)), pltpu.SemaphoreType.DMA((8,)),
        ],
        compiler_params=params_of(40), cost_estimate=estimate(14), name="upward",
    )(place, mixed, tokens, glu_bias, gain, bias, ffn_bias, glu_weight, ffn_in)


def downward(place, cot, slope2, hidden, pre, slope1, gain, ffn_out, ffn_in, glu_weight):
    rows, features = cot.shape
    inner = ffn_in.shape[1]
    return pl.pallas_call(
        downward_kernel,
        in_specs=[SMEM] + [VMEM] * 6 + [ANY] * 3,
        out_shape=(
            shaped(2, rows, inner // 2), shaped(2, rows, features), shaped(rows, features),
            shaped(features, rows), shaped(1, inner), shaped(1, 2 * features), shaped(1, features),
            shaped(1, features), shaped(1, features),
        ),
        scratch_shapes=[
            pltpu.VMEM(ffn_out.shape, BF16), pltpu.VMEM(ffn_in.shape, BF16), pltpu.VMEM(glu_weight.shape, BF16),
            pltpu.SemaphoreType.DMA((8,)), pltpu.SemaphoreType.DMA((8,)), pltpu.SemaphoreType.DMA((1,)),
        ],
        compiler_params=params_of(48), cost_estimate=estimate(18), name="downward",
    )(place, cot, slope2, hidden, pre, slope1, gain, ffn_out, ffn_in, glu_weight)


def products(place, lefts, rights, blocks):
    count = len(lefts)
    tall, wide = lefts[0].shape[-1], rights[0].shape[-1]
    out = shaped(blocks // 2, tall // blocks, wide)
    return pl.pallas_call(
        lambda *refs: product_kernel(count, *refs),
        in_specs=[SMEM] + [VMEM] * (2 * count),
        out_shape=(out, out),
        scratch_shapes=[pltpu.VMEM((tall, wide), F32)],
        compiler_params=params_of(40), cost_estimate=estimate(4), name="products",
    )(place, *lefts, *rights)


def flipped(value, axis, bit):
    count = lax.axis_size(axis)
    return lax.ppermute(value, axis, [(i, i ^ bit) for i in range(count)])


def summed(value, axes):
    for axis in axes:
        bit = 1
        while bit < lax.axis_size(axis):
            value = value + flipped(value, axis, bit)
            bit *= 2
    return value


def halved(value, dim, which):
    first = lax.index_in_dim(value, 0, dim, keepdims=False)
    second = lax.index_in_dim(value, 1, dim, keepdims=False)
    pick = which == 0
    return jnp.where(pick, first, second), jnp.where(pick, second, first)


def across(value, bit=1):
    return flipped(value, "seq", bit)


def over_batch(value):
    return flipped(value, "batch", 1)


def over_line(blocks, mine):
    bit = 4
    while blocks.shape[0] > 1:
        pairs = blocks.reshape((blocks.shape[0] // 2, 2) + blocks.shape[1:])
        keep, send = halved(pairs, 1, (mine // bit) % 2)
        blocks = keep + across(send, bit)
        bit *= 2
    return blocks[0]


def mode_parts(params):
    decay_log, decay_freq, input_re, input_im, output_re, output_im, step_log = params
    step_size = jnp.exp(step_log)[:, None]
    real_part = -jnp.exp(decay_log)
    delta_re = step_size * real_part
    delta_im = step_size * decay_freq
    magnitude = jnp.exp(delta_re)
    lam_re, lam_im = (magnitude * jnp.cos(delta_im), magnitude * jnp.sin(delta_im))
    denominator = real_part * real_part + decay_freq * decay_freq
    num_re = lam_re - 1.0
    rat_re = (num_re * real_part + lam_im * decay_freq) / denominator
    rat_im = (lam_im * real_part - num_re * decay_freq) / denominator
    bbar_re = rat_re * input_re - rat_im * input_im
    bbar_im = rat_re * input_im + rat_im * input_re
    prod_re = 2.0 * (output_re * bbar_re - output_im * bbar_im)
    prod_im = 2.0 * (output_re * bbar_im + output_im * bbar_re)
    return (delta_re, delta_im, prod_re, prod_im), (lam_re, lam_im)


def packed(real, imag):
    return jnp.concatenate([real, imag], axis=1)


def on_device(
    tokens, segments, norm1_gain, norm1_bias, decay_log, decay_freq, input_re, input_im,
    output_re, output_im, step_log, skip_gain, glu_weight, glu_bias, norm2_gain, norm2_bias,
    ffn_in, ffn_in_bias, ffn_out, ffn_out_bias, cotangent,
):
    contexts, piece_len, features = tokens.shape
    rows = contexts * piece_len
    pieces, mine = lax.axis_size("seq"), lax.axis_index("seq")
    channels = features // pieces
    docs = max(1, pieces * piece_len // 256)
    params = (decay_log, decay_freq, input_re, input_im, output_re, output_im, step_log)
    batch_bit = lax.axis_index("batch") % 2
    place = jnp.stack([mine % 2, batch_bit, (mine // 2) % 2]).astype(jnp.int32)

    def own(value):
        return lax.dynamic_slice_in_dim(value, mine * channels, channels, 0)

    def row_of(value):
        return jnp.broadcast_to(own(value)[:, None], (channels, LANES))

    def line(value):
        return value.reshape(1, -1)

    def by_channel(value):
        return lax.all_to_all(value, "seq", 0, 0)

    parts, lam_pair = mode_parts(tuple(own(p) for p in params))
    lam, weight = packed(*lam_pair), packed(parts[2], parts[3])
    skip = row_of(skip_gain)
    flat = tokens.reshape(rows, features)
    cot = cotangent.reshape(rows, features)

    send, up = first_norm(
        flat, cot, segments.reshape(1, rows), line(norm1_gain), line(norm1_bias), pieces
    )
    recv = by_channel(send).reshape(pieces * (channels + 8), rows)
    up_x = over_batch(up)
    ups = [up, up_x, across(up), across(up_x)]
    mixed_rows, enter, lags = recurrence(recv, lam, weight, skip, pieces, docs, FORWARD_UNROLL)
    mixed = by_channel(mixed_rows.reshape(pieces, channels, rows)).reshape(features, rows)
    acts, ffn_parts, glu_pre, hidden, slope1, slope2, ffn_low = upward(
        place, mixed, flat, line(glu_bias), line(norm2_gain), line(norm2_bias), line(ffn_in_bias),
        glu_weight, ffn_in, pieces,
    )
    pre_parts, glu_parts, grad_hidden, turned, bias_in, bias_glu, grad_g2, grad_b2, bias_out = downward(
        place, cot, slope2, hidden, glu_pre, slope1, line(norm2_gain), ffn_out, ffn_in, glu_weight
    )

    ffn_x = over_batch(ffn_parts[1])
    acts, pre_parts, glu_parts, ffn_x = lax.optimization_barrier((acts, pre_parts, glu_parts, ffn_x))
    lefts = [ffn_parts[0, 0], ffn_x[0], across(ffn_parts[0, 1]), across(ffn_x[1])]
    keep_out, send_out = products(place, lefts, ups, pieces // 2)
    acts_x = over_batch(acts)
    acts_c, acts_cx = across(acts[1]), across(acts_x[1])
    pre_x = over_batch(pre_parts[1])
    rights = [pre_parts[0], pre_x, across(pre_parts[0]), across(pre_x)]
    lefts = [acts[0, 1], acts_x[0, 1], acts_c[1], acts_cx[1]]
    keep_in, send_in = products(place, lefts, rights, pieces // 2)
    glu_x = over_batch(glu_parts[1])
    rights = [glu_parts[0], glu_x, across(glu_parts[0]), across(glu_x)]
    lefts = [acts[0, 0], acts_x[0, 0], acts_c[0], acts_cx[0]]
    keep_glu, send_glu = products(place, lefts, rights, pieces // 2)

    def joined(keep, sent, axis):
        value = over_line(keep + across(sent, 2), mine)
        bit = 2
        while bit < lax.axis_size("batch"):
            value = value + flipped(value, "batch", bit)
            bit *= 2
        other = over_batch(value)
        pick = batch_bit == 0
        return jnp.concatenate(
            [jnp.where(pick, value, other), jnp.where(pick, other, value)], axis=axis
        )

    back = by_channel(turned.reshape(pieces, channels, rows)).reshape(pieces * channels, rows)
    back, send_out = lax.optimization_barrier((back, send_out))
    sum_out = joined(keep_out, send_out, 0)
    grad_rows, sums, firsts, lagsum, bias_part = recurrence_back(
        recv, back, enter, lags, lam, weight, skip, pieces, docs, BACKWARD_UNROLL
    )
    small = jnp.concatenate([bias_glu, grad_g2, grad_b2, bias_in, bias_out], axis=1)
    grad_rows, small, ffn_low = lax.optimization_barrier((grad_rows, small, ffn_low))
    ffn_res = jnp.dot(ffn_low, ffn_out, preferred_element_type=F32) + ffn_out_bias
    result = (hidden + ffn_res).astype(BF16).reshape(tokens.shape)
    grad_normed = by_channel(grad_rows.reshape(pieces, channels, rows)).reshape(features, rows)
    grad_tokens = last_norm(grad_normed, flat, line(norm1_gain), grad_hidden).reshape(tokens.shape)

    sum_in = joined(keep_in, send_in, 1)
    sum_glu = joined(keep_glu, send_glu, 1)

    vectors = jnp.concatenate([lagsum[:, LANES - 1], jnp.sum(bias_part, axis=1)]).reshape(1, -1)
    vectors = jnp.pad(vectors, ((0, 7), (0, 2 * LANES - vectors.shape[1])))
    state = jnp.concatenate([jnp.concatenate([sums, firsts], axis=1), vectors], axis=0)
    state = summed(state, ("batch",))
    state = by_channel(jnp.broadcast_to(state[None], (pieces,) + state.shape))
    vectors = state[:, channels]
    grad_skip = vectors[:, :channels].reshape(features)
    grad_bias1 = vectors[:, channels : 2 * channels].reshape(features)
    state = state[:, :channels].reshape(features, 2 * LANES)
    half = LANES // 2
    m_re, m_im = state[:, :half], state[:, half:LANES]
    f_re, f_im = state[:, LANES : LANES + half], state[:, LANES + half : 2 * LANES]
    whole_parts, mode_pull = jax.vjp(lambda p: mode_parts(p)[0], params)
    w_re, w_im = whole_parts[2], whole_parts[3]
    grad_params = mode_pull(
        (w_re * f_re - w_im * f_im, -(w_re * f_im + w_im * f_re), m_re, -m_im)
    )[0]
    grad_gain1 = (
        jnp.sum(w_re * m_re - w_im * m_im, axis=1) + skip_gain * grad_skip - norm1_bias * grad_bias1
    ) / norm1_gain
    small = summed(small.reshape(-1, LANES), ("seq", "batch")).reshape(-1)
    bias_glu, grad_g2, grad_b2, bias_in, bias_out = jnp.split(
        small, [2 * features, 3 * features, 4 * features, small.shape[0] - features]
    )
    return (
        result, grad_tokens, grad_gain1, grad_bias1, *grad_params, grad_skip,
        sum_glu, bias_glu, grad_g2, grad_b2, sum_in, bias_in, sum_out, bias_out,
    )


def solution(mesh):
    spread_over = P("batch", "seq", None)
    in_specs = (spread_over, P("batch", "seq")) + (P(),) * 18 + (spread_over,)
    rows = P("seq", None)
    out_specs = (spread_over,) * 2 + (P(),) * 10 + (rows,) + (P(),) * 3 + (rows, P(), rows, P())
    return jax.shard_map(
        on_device, mesh=mesh, in_specs=in_specs, out_specs=out_specs, check_vma=False
    )
```

time: 664 us -> 387 us (0.58)
  waiting for transfers between devices: 378 us -> 165 us
  matrix products: 62.7 us -> 5.4 us
  local copies, waits for them, and re-layouts: 26.4 us -> 50.6 us
  starting transfers between devices: 40.4 us -> 62.3 us
  blocking collectives: 18.7 us -> 0 us
  Pallas kernels: 90.7 us -> 72.1 us
  between operations: 14.3 us -> 1.44 us
    reduce_scatter x3 -> x0, waiting for transfers between devices: 264 us -> none  [on_device(): lax.psum_scatter(term, 'seq', scatter_dimension=0, tiled=True)]
    ppermute x9 -> x33, waiting for transfers between devices: 75 us -> 154 us  [flipped(): return lax.ppermute(value, axis, [(i, i ^ bit) for i in range(count)])]
    dot_general x8 -> x0, matrix products: 57.3 us -> none  [the longest x3 25 us: inner_rows(): return lax.dot_general(left, right, TN, preferred_element_type=F32)]
    pallas_call x0 -> x7, Pallas kernels: none -> 36.7 us  [the longest x1 12.9 us: downward(): pl.pallas_call(downward_kernel, in_specs=[SMEM] + [VMEM] * 6 + [ANY] * 3,...]
    pallas_call x1, Pallas kernels: 57.9 us -> 24.4 us  [recurrence_back(): pl.pallas_call(lambda *refs: backward_kernel(sizes, *refs), out_shape=(ja...]
    all_to_all x4 -> x5, waiting for transfers between devices: 39.8 us -> 11.2 us  [by_channel(): return lax.all_to_all(value, 'seq', 0, 0)]
    pallas_call x1, Pallas kernels: 32.8 us -> 11 us  [recurrence(): pl.pallas_call(lambda *refs: forward_kernel(sizes, *refs), out_shape=(jax...]
    ppermute x9 -> x33, starting transfers between devices: 13.8 us -> 33.2 us  [flipped(): return lax.ppermute(value, axis, [(i, i ^ bit) for i in range(count)])]
  transfers between devices with their start and end apart: 16 -> 38, of which waited for: 11 -> 13; matrix products, arithmetic and copies ran while one was open for 11% -> 17% of each run, Pallas kernels for 9% -> 16%
where the time goes in v2:
time: 387 us; the launch traced here: 385 us
  waiting for transfers between devices  165 us (43%)
  Pallas kernels  72.1 us (19%)
  starting transfers between devices  62.3 us (16%)
  local copies, waits for them, and re-layouts  50.6 us (13%)
  other arithmetic  27.9 us (7%)
  matrix products  5.4 us (1%)
    ppermute x33, waiting for transfers between devices, flipped(): return lax.ppermute(value, axis, [(i, i ^ bit) for i in range(count)])  154 us
    ppermute x33, starting transfers between devices, flipped(): return lax.ppermute(value, axis, [(i, i ^ bit) for i in range(count)])  33.2 us
    all_to_all x5, starting transfers between devices, by_channel(): return lax.all_to_all(value, 'seq', 0, 0)  29.1 us
    pallas_call x1, Pallas kernels, recurrence_back(): pl.pallas_call(lambda *refs: backward_kernel(sizes, *refs), out_shape=(ja...  24.4 us
    unnamed x125, local copies, waits for them, and re-layouts  22.5 us
    pallas_call x1, Pallas kernels, downward(): pl.pallas_call(downward_kernel, in_specs=[SMEM] + [VMEM] * 6 + [ANY] * 3,...  12.9 us
    pallas_call x3, Pallas kernels, products(): pl.pallas_call(lambda *refs: product_kernel(count, *refs), in_specs=[SMEM...  12.3 us
    all_to_all x5, waiting for transfers between devices, by_channel(): return lax.all_to_all(value, 'seq', 0, 0)  11.2 us
  transfers between devices with their start and end apart: 38, of which 13 were waited for; matrix products, arithmetic and copies ran while one was open for 17% of the time, Pallas kernels for 16%

profile of v2, /device:TPU:0, one launch (start us, length us, event | category | flops | bytes accessed | tf_op | source)
XLA Modules:
  0.0 384.8 jit_solution(4124081045735436733)
XLA Ops:
  6.1 7.4 %all-to-all-start = ((f32[16,72,128]{2,1,0:T(8,128)}), f32[16,72,128]{2,1,0:T(8,128)S(1)}, u32[]{:S(2)}, u32[]{:S(2)}) async-start(f32[16,72,128]{2,1,0:T(8,128)} %get-tuple-element.61), calls=%async_computation | async-start | bytes 1179648 | tf_op jit(solution)/shard_map/all_to_all | solution.py:752
  17.8 11.2 %all-to-all-done = f32[16,72,128]{2,1,0:T(8,128)S(1)} async-done(((f32[16,72,128]{2,1,0:T(8,128)}), f32[16,72,128]{2,1,0:T(8,128)S(1)}, u32[]{:S(2)}, u32[]{:S(2)}) %all-to-all-start) | async-done | bytes 589856 | tf_op jit(solution)/shard_map/all_to_all | solution.py:752
  29.1 11.0 %recurrence.1 = (f32[1024,128]{1,0:T(8,128)}, f32[64,64,128]{2,1,0:T(8,128)S(1)}, f32[64,128]{1,0:T(8,128)S(1)}) custom-call(f32[1152,128]{1,0:T(8,128)S(1)} %bitcast.164, f32[64,128]{1,0:T(8,128)S(1)} %pad_maximum_fusion.3.refs_1_.refs_4_, f32[64,128]{1,0:T(8,128)S(1)} %pad_maximum_fusion.4.refs_2_.refs_5_, f32[64,128]{1,0:T(8,128)S(1)} %broadcast_in_dim.4.refs_3_.refs_6_), custom_call_target="tpu_custom_call" | custom-call | flops 16000000000 | tf_op jit(solution)/shard_map/recurrence/pallas_call | solution.py:372
  41.5 4.4 %all-to-all-start.1 = ((f32[16,64,128]{2,1,0:T(8,128)}), f32[16,64,128]{2,1,0:T(8,128)S(1)}, u32[]{:S(2)}, u32[]{:S(2)}) async-start(f32[16,64,128]{2,1,0:T(8,128)} %bitcast.8), calls=%async_computation.1 | async-start | bytes 1048576 | tf_op jit(solution)/shard_map/all_to_all | solution.py:752
  47.7 12.9 %collective-permute-done.3.refs_6_ = f32[128,1024]{1,0:T(8,128)} collective-permute-done((f32[128,1024]{1,0:T(8,128)}, f32[128,1024]{1,0:T(8,128)}, u32[]{:S(2)}, u32[]{:S(2)}) %collective-permute-start.3) | collective-permute-done | bytes 524320 | tf_op jit(solution)/shard_map/ppermute | solution.py:668
  62.8 7.8 %upward.1 = (f32[2,2,128,512]{3,2,1,0:T(8,128)}, f32[2,2,128,1024]{3,2,1,0:T(8,128)S(1)}, f32[128,2048]{1,0:T(8,128)S(1)}, f32[128,1024]{1,0:T(8,128)S(1)}, f32[...) custom-call(s32[3]{0:T(128)S(1)} %pad_add_fusion.refs_0_.place_ref, ...), custom_call_target="tpu_custom_call" | custom-call | flops 14000000000 | tf_op jit(solution)/shard_map/upward/pallas_call | solution.py:619
  74.3 12.9 %downward.1 = (f32[2,128,2048]{2,1,0:T(8,128)}, f32[2,128,1024]{2,1,0:T(8,128)S(1)}, f32[128,1024]{1,0:T(8,128)S(1)}, f32[1024,128]{1,0:T(8,128)S(1)}, f32[1,409...) custom-call(s32[3]{0:T(128)S(1)} %pad_add_fusion.refs_0_.place_ref, ...), custom_call_target="tpu_custom_call" | custom-call | flops 17999998976 | tf_op jit(solution)/shard_map/downward/pallas_call | solution.py:637
  88.9 5.8 %all-to-all-start.2 = ((f32[16,64,128]{2,1,0:T(8,128)}), f32[16,64,128]{2,1,0:T(8,128)}, u32[]{:S(2)}, u32[]{:S(2)}) async-start(f32[16,64,128]{2,1,0:T(8,128)} %bitcast.168), calls=%async_computation.2 | async-start | bytes 1048576 | tf_op jit(solution)/shard_map/all_to_all | solution.py:752
  109.9 4.3 %products.3 = (f32[4,128,1024]{2,1,0:T(8,128)S(1)}, f32[4,128,1024]{2,1,0:T(8,128)S(1)}) custom-call(s32[3]{0:T(128)S(1)} %pad_add_fusion.refs_0_.place_ref, f32[128,1024]{1,0:T(8,128)S(1)} %copy-done.9, f32[128,1024]{1,0:T(8,128)S(1)} %get-tuple-element.161.refs_2_, f32[128,1024]{1,0:T(8,128)} %collective-permute-done.1.refs_3_, ...), custom_call_target="tpu_custom_call" | custom-call | flops 4000000000 | tf_op jit(solution)/shard_map/products/pallas_call | solution.py:657
  119.7 24.4 %recurrence_back.1 = (f32[1024,128]{1,0:T(8,128)S(1)}, f32[64,128]{1,0:T(8,128)S(1)}, f32[64,128]{1,0:T(8,128)S(1)}, f32[64,128]{1,0:T(8,128)S(1)}, f32[64,128]{1,0:T(8,128)S(1)}) custom-call(f32[1152,128]{1,0:T(8,128)S(1)} %bitcast.165, f32[1024,128]{1,0:T(8,128)} %bitcast.15.refs_1_, f32[64,64,128]{2,1,0:T(8,128)S(1)} %copy-done.36, ...), custom_call_target="tpu_custom_call" | custom-call | flops 30000001024 | tf_op jit(solution)/shard_map/recurrence_back/pallas_call | solution.py:391
  145.8 5.9 %all-to-all-start.3 = ((f32[16,64,128]{2,1,0:T(8,128)}), f32[16,64,128]{2,1,0:T(8,128)}, u32[]{:S(2)}, u32[]{:S(2)}) async-start(f32[16,64,128]{2,1,0:T(8,128)} %bitcast.167), calls=%async_computation.3 | async-start | bytes 1048576 | tf_op jit(solution)/shard_map/all_to_all | solution.py:752
  151.7 5.4 %fusion.1 = bf16[128,1024]{1,0:T(8,128)(2,1)} fusion(f32[128,1024]{1,0:T(8,128)} %copy-done.5, bf16[128,4096]{1,0:T(8,128)(2,1)S(1)} %get-tuple-element.85, bf16[4096,1024]{1,0:T(8,128)(2,1)} %out_w_ref.1, f32[1024]{0:T(1024)S(1)} %copy-done.53), kind=kOutput, calls=%fused_computation.2 | convolution fusion | flops 1074135040 | bytes 10227712 | tf_op jit(solution)/shard_map/dot_general | solution.py:811
  159.9 2.4 collective-permute-done.18
  162.3 2.6 collective-permute-start.19
  182.1 5.7 %all-to-all-start.4 = ((f32[16,72,256]{2,1,0:T(8,128)}), f32[16,72,256]{2,1,0:T(8,128)}, u32[]{:S(2)}, u32[]{:S(2)}) async-start(f32[16,72,256]{2,1,0:T(8,128)} %broadcast_in_dim.5), calls=%async_computation.4 | async-start | bytes 2359296 | tf_op jit(solution)/shard_map/all_to_all | solution.py:752
  190.7 2.8 products.4
  198.4 5.2 %products.5 = (f32[4,64,2048]{2,1,0:T(8,128)S(1)}, f32[4,64,2048]{2,1,0:T(8,128)}) custom-call(s32[3]{0:T(128)S(1)} %pad_add_fusion.refs_0_.place_ref, f32[128,512]{1,0:T(8,128)S(1)} %get-tuple-element.152.refs_1_, f32[128,512]{1,0:T(8,128)S(1)} %get-tuple-element.150.refs_2_, f32[128,512]{1,0:T(8,128)S(1)} %copy-done.11, ...), custom_call_target="tpu_custom_call" | custom-call | flops 4000000000 | tf_op jit(solution)/shard_map/products/pallas_call | solution.py:657
  203.7 29.1 %collective-permute-done.29 = f32[4,128,1024]{2,1,0:T(8,128)} collective-permute-done((f32[4,128,1024]{2,1,0:T(8,128)}, f32[4,128,1024]{2,1,0:T(8,128)}, u32[]{:S(2)}, u32[]{:S(2)}) %collective-permute-start.29) | collective-permute-done | bytes 2097184 | tf_op jit(solution)/shard_map/ppermute | solution.py:668
  238.2 20.2 %collective-permute-done.13 = f32[4,64,1024]{2,1,0:T(8,128)S(1)} collective-permute-done((f32[4,64,1024]{2,1,0:T(8,128)S(1)}, f32[4,64,1024]{2,1,0:T(8,128)S(1)}, u32[]{:S(2)}, u32[]{:S(2)}) %collective-permute-start.13) | collective-permute-done | bytes 1048608 | tf_op jit(solution)/shard_map/ppermute | solution.py:668
  267.0 2.9 multiply_add_fusion
  280.6 22.1 %collective-permute-done.25 = f32[4,64,2048]{2,1,0:T(8,128)} collective-permute-done((f32[4,64,2048]{2,1,0:T(8,128)}, f32[4,64,2048]{2,1,0:T(8,128)}, u32[]{:S(2)}, u32[]{:S(2)}) %collective-permute-start.25) | collective-permute-done | bytes 2097184 | tf_op jit(solution)/shard_map/ppermute | solution.py:668
  314.1 29.2 %collective-permute-done.26 = f32[2,64,2048]{2,1,0:T(8,128)} collective-permute-done((f32[2,64,2048]{2,1,0:T(8,128)}, f32[2,64,2048]{2,1,0:T(8,128)}, u32[]{:S(2)}, u32[]{:S(2)}) %collective-permute-start.26) | collective-permute-done | bytes 1048608 | tf_op jit(solution)/shard_map/ppermute | solution.py:668
  347.4 22.3 %collective-permute-done.27 = f32[1,64,2048]{2,1,0:T(8,128)S(1)} collective-permute-done((f32[1,64,2048]{2,1,0:T(8,128)S(1)}, f32[1,64,2048]{2,1,0:T(8,128)S(1)}, u32[]{:S(2)}, u32[]{:S(2)}) %collective-permute-start.27) | collective-permute-done | bytes 524320 | tf_op jit(solution)/shard_map/ppermute | solution.py:668
  372.3 11.3 %collective-permute-done.28 = f32[64,2048]{1,0:T(8,128)S(1)} collective-permute-done((f32[64,2048]{1,0:T(8,128)S(1)}, f32[64,2048]{1,0:T(8,128)S(1)}, u32[]{:S(2)}, u32[]{:S(2)}) %collective-permute-start.28) | collective-permute-done | bytes 524320 | tf_op jit(solution)/shard_map/ppermute | solution.py:668
  (259 shorter events, 114.1 us)
Async XLA Ops:
  6.1 22.9 %all-to-all-start = ((f32[16,72,128]{2,1,0:T(8,128)}), f32[16,72,128]{2,1,0:T(8,128)S(1)}, u32[]{:S(2)}, u32[]{:S(2)}) async-start(f32[16,72,128]{2,1,0:T(8,128)} %get-tuple-element.61), calls=%async_computation | async-start | bytes 1179648 | tf_op jit(solution)/shard_map/all_to_all | solution.py:752
  41.5 19.1 %all-to-all-start.1 = ((f32[16,64,128]{2,1,0:T(8,128)}), f32[16,64,128]{2,1,0:T(8,128)S(1)}, u32[]{:S(2)}, u32[]{:S(2)}) async-start(f32[16,64,128]{2,1,0:T(8,128)} %bitcast.8), calls=%async_computation.1 | async-start | bytes 1048576 | tf_op jit(solution)/shard_map/all_to_all | solution.py:752
  47.5 60.2 %collective-permute-start.4 = (f32[128,1024]{1,0:T(8,128)}, f32[128,1024]{1,0:T(8,128)}, u32[]{:S(2)}, u32[]{:S(2)}) collective-permute-start(f32[128,1024]{1,0:T(8,128)} %get-tuple-element.73.refs_5_), channel_id=1, source_target_pairs={{0,1},{1,0},{2,3},{3,2},{4,5},{5,4},{6,7},{7,6},{8,9},{9,8},{10,11... | collective-permute-start | bytes 1572872 | tf_op jit(solution)/shard_map/ppermute | solution.py:668
  60.5 47.6 %collective-permute-start.5 = (f32[128,1024]{1,0:T(8,128)}, f32[128,1024]{1,0:T(8,128)}, u32[]{:S(2)}, u32[]{:S(2)}) collective-permute-start(f32[128,1024]{1,0:T(8,128)} %collective-permute-done.3.refs_6_), channel_id=1, source_target_pairs={{0,1},{1,0},{2,3},{3,2},{4,5},{5,4},{6,7},{7,6},{8,9},{9,8},{10,11... | collective-permute-start | bytes 1572872 | tf_op jit(solution)/shard_map/ppermute | solution.py:668
  72.6 25.9 %collective-permute-start = (f32[2,128,1024]{2,1,0:T(8,128)}, f32[2,128,1024]{2,1,0:T(8,128)}, u32[]{:S(2)}, u32[]{:S(2)}) collective-permute-start(f32[2,128,1024]{2,1,0:T(8,128)} %slice_bitcast_fusion.6), channel_id=1, source_target_pairs={{0,16},{16,0},{1,17},{17,1},{2,18},{18,2},{3,19},{19,3},{4,20},{20... | collective-permute-start | bytes 3145736 | tf_op jit(solution)/shard_map/ppermute | solution.py:668
  74.1 34.3 %collective-permute-start.1 = (f32[128,1024]{1,0:T(8,128)S(1)}, f32[128,1024]{1,0:T(8,128)}, u32[]{:S(2)}, u32[]{:S(2)}) collective-permute-start(f32[128,1024]{1,0:T(8,128)S(1)} %get-tuple-element.144), channel_id=1, source_target_pairs={{0,1},{1,0},{2,3},{3,2},{4,5},{5,4},{6,7},{7,6},{8,9},{9,8},{10,11... | collective-permute-start | bytes 1572872 | tf_op jit(solution)/shard_map/ppermute | solution.py:668
  88.9 26.7 %all-to-all-start.2 = ((f32[16,64,128]{2,1,0:T(8,128)}), f32[16,64,128]{2,1,0:T(8,128)}, u32[]{:S(2)}, u32[]{:S(2)}) async-start(f32[16,64,128]{2,1,0:T(8,128)} %bitcast.168), calls=%async_computation.2 | async-start | bytes 1048576 | tf_op jit(solution)/shard_map/all_to_all | solution.py:752
  98.5 77.9 %collective-permute-start.7 = (f32[2,2,128,512]{3,2,1,0:T(8,128)}, f32[2,2,128,512]{3,2,1,0:T(8,128)}, u32[]{:S(2)}, u32[]{:S(2)}) collective-permute-start(f32[2,2,128,512]{3,2,1,0:T(8,128)} %get-tuple-element.92), channel_id=1, source_target_pairs={{0,16},{16,0},{1,17},{17,1},{2,18},{18,2},{3,19},{19,3},{4,20},{20... | collective-permute-start | bytes 3145736 | tf_op jit(solution)/shard_map/ppermute | solution.py:668
  107.6 81.3 %collective-permute-start.22 = (f32[128,2048]{1,0:T(8,128)}, f32[128,2048]{1,0:T(8,128)}, u32[]{:S(2)}, u32[]{:S(2)}) collective-permute-start(f32[128,2048]{1,0:T(8,128)} %get-tuple-element.142), channel_id=1, source_target_pairs={{0,16},{16,0},{1,17},{17,1},{2,18},{18,2},{3,19},{19,3},{4,20},{20... | collective-permute-start | bytes 3145736 | tf_op jit(solution)/shard_map/ppermute | solution.py:668
  108.2 59.2 %collective-permute-start.8 = (f32[2,128,512]{2,1,0:T(8,128)}, f32[2,128,512]{2,1,0:T(8,128)}, u32[]{:S(2)}, u32[]{:S(2)}) collective-permute-start(f32[2,128,512]{2,1,0:T(8,128)} %slice_bitcast_fusion.12), channel_id=1, source_target_pairs={{0,1},{1,0},{2,3},{3,2},{4,5},{5,4},{6,7},{7,6},{8,9},{9,8},{10,11... | collective-permute-start | bytes 1572872 | tf_op jit(solution)/shard_map/ppermute | solution.py:668
  108.4 66.2 %collective-permute-start.10 = (f32[128,1024]{1,0:T(8,128)}, f32[128,1024]{1,0:T(8,128)}, u32[]{:S(2)}, u32[]{:S(2)}) collective-permute-start(f32[128,1024]{1,0:T(8,128)} %get-tuple-element.154), channel_id=1, source_target_pairs={{0,16},{16,0},{1,17},{17,1},{2,18},{18,2},{3,19},{19,3},{4,20},{20... | collective-permute-start | bytes 1572872 | tf_op jit(solution)/shard_map/ppermute | solution.py:668
  145.8 34.2 %all-to-all-start.3 = ((f32[16,64,128]{2,1,0:T(8,128)}), f32[16,64,128]{2,1,0:T(8,128)}, u32[]{:S(2)}, u32[]{:S(2)}) async-start(f32[16,64,128]{2,1,0:T(8,128)} %bitcast.167), calls=%async_computation.3 | async-start | bytes 1048576 | tf_op jit(solution)/shard_map/all_to_all | solution.py:752
  172.3 18.2 %collective-permute-start.11 = (f32[128,1024]{1,0:T(8,128)}, f32[128,1024]{1,0:T(8,128)}, u32[]{:S(2)}, u32[]{:S(2)}) collective-permute-start(f32[128,1024]{1,0:T(8,128)} %get-tuple-element.155.refs_5_), channel_id=1, source_target_pairs={{0,1},{1,0},{2,3},{3,2},{4,5},{5,4},{6,7},{7,6},{8,9},{9,8},{10,11... | collective-permute-start | bytes 1572872 | tf_op jit(solution)/shard_map/ppermute | solution.py:668
  174.6 58.3 %collective-permute-start.29 = (f32[4,128,1024]{2,1,0:T(8,128)}, f32[4,128,1024]{2,1,0:T(8,128)}, u32[]{:S(2)}, u32[]{:S(2)}) collective-permute-start(f32[4,128,1024]{2,1,0:T(8,128)} %copy-done.22), channel_id=1, source_target_pairs={{0,2},{1,3},{2,0},{3,1},{4,6},{5,7},{6,4},{7,5},{8,10},{9,11},{10,... | collective-permute-start | bytes 6291464 | tf_op jit(solution)/shard_map/ppermute | solution.py:668
  182.1 79.3 %all-to-all-start.4 = ((f32[16,72,256]{2,1,0:T(8,128)}), f32[16,72,256]{2,1,0:T(8,128)}, u32[]{:S(2)}, u32[]{:S(2)}) async-start(f32[16,72,256]{2,1,0:T(8,128)} %broadcast_in_dim.5), calls=%async_computation.4 | async-start | bytes 2359296 | tf_op jit(solution)/shard_map/all_to_all | solution.py:752
  193.5 64.8 %collective-permute-start.13 = (f32[4,64,1024]{2,1,0:T(8,128)S(1)}, f32[4,64,1024]{2,1,0:T(8,128)S(1)}, u32[]{:S(2)}, u32[]{:S(2)}) collective-permute-start(f32[4,64,1024]{2,1,0:T(8,128)S(1)} %get-tuple-element.95), channel_id=1, source_target_pairs={{0,2},{1,3},{2,0},{3,1},{4,6},{5,7},{6,4},{7,5},{8,10},{9,11},{10,... | collective-permute-start | bytes 3145736 | tf_op jit(solution)/shard_map/ppermute | solution.py:668
  203.5 99.1 %collective-permute-start.25 = (f32[4,64,2048]{2,1,0:T(8,128)}, f32[4,64,2048]{2,1,0:T(8,128)}, u32[]{:S(2)}, u32[]{:S(2)}) collective-permute-start(f32[4,64,2048]{2,1,0:T(8,128)} %get-tuple-element.99), channel_id=1, source_target_pairs={{0,2},{1,3},{2,0},{3,1},{4,6},{5,7},{6,4},{7,5},{8,10},{9,11},{10,... | collective-permute-start | bytes 6291464 | tf_op jit(solution)/shard_map/ppermute | solution.py:668
  236.1 74.4 %collective-permute-start.30 = (f32[2,128,1024]{2,1,0:T(8,128)}, f32[2,128,1024]{2,1,0:T(8,128)}, u32[]{:S(2)}, u32[]{:S(2)}) collective-permute-start(f32[2,128,1024]{2,1,0:T(8,128)} %select_bitcast_fusion), channel_id=1, source_target_pairs={{0,4},{1,5},{2,6},{3,7},{4,0},{5,1},{6,2},{7,3},{8,12},{9,13},{10,... | collective-permute-start | bytes 3145736 | tf_op jit(solution)/shard_map/ppermute | solution.py:668
  278.7 31.2 %collective-permute-start.15 = (f32[1,64,1024]{2,1,0:T(8,128)S(1)}, f32[1,64,1024]{2,1,0:T(8,128)S(1)}, u32[]{:S(2)}, u32[]{:S(2)}) collective-permute-start(f32[1,64,1024]{2,1,0:T(8,128)S(1)} %select_bitcast_fusion.5), channel_id=1, source_target_pairs={{0,8},{1,9},{2,10},{3,11},{4,12},{5,13},{6,14},{7,15},{8,0},{9,1},... | collective-permute-start | bytes 786440 | tf_op jit(solution)/shard_map/ppermute | solution.py:668
  307.0 36.3 %collective-permute-start.26 = (f32[2,64,2048]{2,1,0:T(8,128)}, f32[2,64,2048]{2,1,0:T(8,128)}, u32[]{:S(2)}, u32[]{:S(2)}) collective-permute-start(f32[2,64,2048]{2,1,0:T(8,128)} %select_bitcast_fusion.1), channel_id=1, source_target_pairs={{0,4},{1,5},{2,6},{3,7},{4,0},{5,1},{6,2},{7,3},{8,12},{9,13},{10,... | collective-permute-start | bytes 3145736 | tf_op jit(solution)/shard_map/ppermute | solution.py:668
  309.9 36.7 %collective-permute-start.16 = (f32[64,1024]{1,0:T(8,128)S(1)}, f32[64,1024]{1,0:T(8,128)S(1)}, u32[]{:S(2)}, u32[]{:S(2)}) collective-permute-start(f32[64,1024]{1,0:T(8,128)S(1)} %fusion.11), channel_id=1, source_target_pairs={{0,16},{16,0},{1,17},{17,1},{2,18},{18,2},{3,19},{19,3},{4,20},{20... | collective-permute-start | bytes 786440 | tf_op jit(solution)/shard_map/ppermute | solution.py:668
  312.2 34.4 %collective-permute-start.31 = (f32[1,128,1024]{2,1,0:T(8,128)S(1)}, f32[1,128,1024]{2,1,0:T(8,128)S(1)}, u32[]{:S(2)}, u32[]{:S(2)}) collective-permute-start(f32[1,128,1024]{2,1,0:T(8,128)S(1)} %select_bitcast_fusion.2), channel_id=1, source_target_pairs={{0,8},{1,9},{2,10},{3,11},{4,12},{5,13},{6,14},{7,15},{8,0},{9,1},... | collective-permute-start | bytes 1572872 | tf_op jit(solution)/shard_map/ppermute | solution.py:668
  344.8 24.8 %collective-permute-start.27 = (f32[1,64,2048]{2,1,0:T(8,128)S(1)}, f32[1,64,2048]{2,1,0:T(8,128)S(1)}, u32[]{:S(2)}, u32[]{:S(2)}) collective-permute-start(f32[1,64,2048]{2,1,0:T(8,128)S(1)} %select_bitcast_fusion.3), channel_id=1, source_target_pairs={{0,8},{1,9},{2,10},{3,11},{4,12},{5,13},{6,14},{7,15},{8,0},{9,1},... | collective-permute-start | bytes 1572872 | tf_op jit(solution)/shard_map/ppermute | solution.py:668
  346.8 24.5 %collective-permute-start.32 = (f32[128,1024]{1,0:T(8,128)S(1)}, f32[128,1024]{1,0:T(8,128)S(1)}, u32[]{:S(2)}, u32[]{:S(2)}) collective-permute-start(f32[128,1024]{1,0:T(8,128)S(1)} %fusion.4), channel_id=1, source_target_pairs={{0,16},{16,0},{1,17},{17,1},{2,18},{18,2},{3,19},{19,3},{4,20},{20... | collective-permute-start | bytes 1572872 | tf_op jit(solution)/shard_map/ppermute | solution.py:668
  (69 other events, 618.2 us)

commit v3 on v2

--- a/solution.py
+++ b/solution.py
@@ -1,3 +1,5 @@
+import functools
+
 import jax, jax.numpy as jnp
 from jax import lax
 from jax.sharding import PartitionSpec as P
@@ -268,8 +270,8 @@
             recv_ref[pl.ds(h + pitch, chunks, stride=2 * pitch), :],
         )
         gpair = join_turned(
-            grad_ref[pl.ds(h, chunks, stride=2 * channels), :],
-            grad_ref[pl.ds(h + channels, chunks, stride=2 * channels), :],
+            grad_ref[pl.ds(h, chunks, stride=2 * pitch), :],
+            grad_ref[pl.ds(h + pitch, chunks, stride=2 * pitch), :],
         )
         inputs = spread(pair, mask_ref, docs)
         grads = spread(gpair, mask_ref, docs, docs * 2)
@@ -415,6 +417,25 @@
     turned = values.T
     for s in range(out_ref.shape[0]):
         out_ref[s, 0:channels, :] = turned[s * channels : (s + 1) * channels]
+
+
+def share_rows(length, pieces):
+    share = length // pieces
+    return max(1, share // LANES), min(share, LANES)
+
+
+def share_vectors(refs, out_ref, first):
+    pieces = out_ref.shape[0]
+    at = first
+    for s in range(pieces):
+        out_ref[s, first : first + 8, :] = jnp.zeros((8, LANES), F32)
+    for ref in refs:
+        count, wide = share_rows(ref.shape[1], pieces)
+        for s in range(pieces):
+            for r in range(count):
+                start = (s * count + r) * wide
+                out_ref[s, at + r : at + r + 1, :wide] = ref[:, start : start + wide]
+        at += count
 
 
 def normalize(values):
@@ -521,8 +542,8 @@
 
 def downward_kernel(
     place_ref, cot_ref, slope2_ref, hidden_ref, pre_ref, slope1_ref, gain_ref, out_w_ref, in_w_ref, glu_w_ref,
-    sent_pre_ref, sent_glu_ref, grad_hidden_ref, turned_ref, in_sum_ref, glu_sum_ref, gain_sum_ref,
-    bias_sum_ref, out_sum_ref,
+    sent_pre_ref, sent_glu_ref, grad_hidden_ref, turned_ref,
+    in_sum_ref, glu_sum_ref, gain_sum_ref, bias_sum_ref, out_sum_ref,
     out_v, in_v, glu_v, out_sem, in_sem, glu_sem,
 ):
     rows, features = cot_ref.shape
@@ -564,12 +585,15 @@
         grad_act = term if grad_act is None else grad_act + term
     turn = turning(rows)
     high, low = halves(grad_act * slope1_ref[...])
-    turned_ref[...] = (dot(turn, high, NN) + dot(turn, low, NN)).T
+    sent_rows(dot(turn, high, NN) + dot(turn, low, NN), turned_ref, turned_ref.shape[1] - 8)
+    share_vectors(
+        (in_sum_ref, glu_sum_ref, gain_sum_ref, bias_sum_ref, out_sum_ref), turned_ref, turned_ref.shape[1] - 8
+    )
 
 
 def product_kernel(count, place_ref, *refs):
     lefts, rights = refs[:count], refs[count : 2 * count]
-    keep_ref, send_ref, scratch_ref = refs[2 * count :]
+    outs, scratch_ref = refs[2 * count : -1], refs[-1]
     total = None
     for left, right in zip(lefts, rights):
         term = lax.dot_general(
@@ -577,11 +601,12 @@
         )
         total = term if total is None else total + term
     scratch_ref[...] = total
-    height = keep_ref.shape[1]
-    for i in range(keep_ref.shape[0]):
-        for ref, other in ((keep_ref, 0), (send_ref, 1)):
-            block = 2 * i + (place_ref[2] ^ other)
-            ref[i] = scratch_ref[pl.ds(pl.multiple_of(block * height, 8), height), :]
+    blocks, height, wide = outs[0].shape
+    for i in range(blocks):
+        for k, ref in enumerate(outs):
+            block = 2 * i + (place_ref[2] ^ (k % 2))
+            columns = slice(k // 2 * wide, (k // 2 + 1) * wide)
+            ref[i] = scratch_ref[pl.ds(pl.multiple_of(block * height, 8), height), columns]
 
 
 SMEM = pl.BlockSpec(memory_space=pltpu.SMEM)
@@ -631,7 +656,7 @@
     )(place, mixed, tokens, glu_bias, gain, bias, ffn_bias, glu_weight, ffn_in)
 
 
-def downward(place, cot, slope2, hidden, pre, slope1, gain, ffn_out, ffn_in, glu_weight):
+def downward(place, cot, slope2, hidden, pre, slope1, gain, ffn_out, ffn_in, glu_weight, pieces):
     rows, features = cot.shape
     inner = ffn_in.shape[1]
     return pl.pallas_call(
@@ -639,10 +664,11 @@
         in_specs=[SMEM] + [VMEM] * 6 + [ANY] * 3,
         out_shape=(
             shaped(2, rows, inner // 2), shaped(2, rows, features), shaped(rows, features),
-            shaped(features, rows), shaped(1, inner), shaped(1, 2 * features), shaped(1, features),
-            shaped(1, features), shaped(1, features),
+            shaped(pieces, features // pieces + 8, rows),
         ),
         scratch_shapes=[
+            pltpu.VMEM((1, inner), F32), pltpu.VMEM((1, 2 * features), F32), pltpu.VMEM((1, features), F32),
+            pltpu.VMEM((1, features), F32), pltpu.VMEM((1, features), F32),
             pltpu.VMEM(ffn_out.shape, BF16), pltpu.VMEM(ffn_in.shape, BF16), pltpu.VMEM(glu_weight.shape, BF16),
             pltpu.SemaphoreType.DMA((8,)), pltpu.SemaphoreType.DMA((8,)), pltpu.SemaphoreType.DMA((1,)),
         ],
@@ -650,14 +676,14 @@
     )(place, cot, slope2, hidden, pre, slope1, gain, ffn_out, ffn_in, glu_weight)
 
 
-def products(place, lefts, rights, blocks):
+def products(place, lefts, rights, blocks, chunks=1):
     count = len(lefts)
     tall, wide = lefts[0].shape[-1], rights[0].shape[-1]
-    out = shaped(blocks // 2, tall // blocks, wide)
+    out = shaped(blocks // 2, tall // blocks, wide // chunks)
     return pl.pallas_call(
         lambda *refs: product_kernel(count, *refs),
         in_specs=[SMEM] + [VMEM] * (2 * count),
-        out_shape=(out, out),
+        out_shape=(out,) * (2 * chunks),
         scratch_shapes=[pltpu.VMEM((tall, wide), F32)],
         compiler_params=params_of(40), cost_estimate=estimate(4), name="products",
     )(place, *lefts, *rights)
@@ -692,14 +718,28 @@
     return flipped(value, "batch", 1)
 
 
-def over_line(blocks, mine):
-    bit = 4
-    while blocks.shape[0] > 1:
+class Halving:
+    def __init__(self, keep, got, mine):
+        self.keep, self.got, self.mine, self.bit = keep, got, mine, 4
+
+    def step(self):
+        blocks = self.keep + self.got
         pairs = blocks.reshape((blocks.shape[0] // 2, 2) + blocks.shape[1:])
-        keep, send = halved(pairs, 1, (mine // bit) % 2)
-        blocks = keep + across(send, bit)
-        bit *= 2
-    return blocks[0]
+        self.keep, send = halved(pairs, 1, (self.mine // self.bit) % 2)
+        self.got = across(send, self.bit)
+        self.bit *= 2
+
+    def finish(self):
+        while self.keep.shape[0] > 1:
+            self.step()
+        return (self.keep + self.got)[0]
+
+
+def tied(works, *others):
+    out = lax.optimization_barrier(tuple(work.got for work in works) + others)
+    for work, got in zip(works, out):
+        work.got = got
+    return out[len(works) :]
 
 
 def mode_parts(params):
@@ -769,59 +809,83 @@
         place, mixed, flat, line(glu_bias), line(norm2_gain), line(norm2_bias), line(ffn_in_bias),
         glu_weight, ffn_in, pieces,
     )
-    pre_parts, glu_parts, grad_hidden, turned, bias_in, bias_glu, grad_g2, grad_b2, bias_out = downward(
-        place, cot, slope2, hidden, glu_pre, slope1, line(norm2_gain), ffn_out, ffn_in, glu_weight
+    pre_parts, glu_parts, grad_hidden, turned = downward(
+        place, cot, slope2, hidden, glu_pre, slope1, line(norm2_gain), ffn_out, ffn_in, glu_weight, pieces
     )
 
     ffn_x = over_batch(ffn_parts[1])
     acts, pre_parts, glu_parts, ffn_x = lax.optimization_barrier((acts, pre_parts, glu_parts, ffn_x))
+    acts_x, pre_x, glu_x = over_batch(acts), over_batch(pre_parts[1]), over_batch(glu_parts[1])
     lefts = [ffn_parts[0, 0], ffn_x[0], across(ffn_parts[0, 1]), across(ffn_x[1])]
     keep_out, send_out = products(place, lefts, ups, pieces // 2)
-    acts_x = over_batch(acts)
+    back = by_channel(turned)
+    shares = jnp.sum(back[:, channels:], axis=0)
+    back, send_out = lax.optimization_barrier((back, send_out))
+    out = Halving(keep_out, across(send_out, 2), mine)
+    grad_rows, sums, firsts, lagsum, bias_part = recurrence_back(
+        recv, back.reshape(pieces * (channels + 8), rows), enter, lags, lam, weight, skip,
+        pieces, docs, BACKWARD_UNROLL,
+    )
+    (grad_rows,) = tied([out], grad_rows)
+    out.step()
+    grad_normed = by_channel(grad_rows.reshape(pieces, channels, rows)).reshape(features, rows)
     acts_c, acts_cx = across(acts[1]), across(acts_x[1])
-    pre_x = over_batch(pre_parts[1])
+    glu_own, out.keep = lax.optimization_barrier((glu_parts[0], out.keep))
+    rights = [glu_own, glu_x, across(glu_parts[0]), across(glu_x)]
+    lefts = [acts[0, 0], acts_x[0, 0], acts_c[0], acts_cx[0]]
+    keep_glu, send_glu = products(place, lefts, rights, pieces // 2)
     rights = [pre_parts[0], pre_x, across(pre_parts[0]), across(pre_x)]
     lefts = [acts[0, 1], acts_x[0, 1], acts_c[1], acts_cx[1]]
-    keep_in, send_in = products(place, lefts, rights, pieces // 2)
-    glu_x = over_batch(glu_parts[1])
-    rights = [glu_parts[0], glu_x, across(glu_parts[0]), across(glu_x)]
-    lefts = [acts[0, 0], acts_x[0, 0], acts_c[0], acts_cx[0]]
-    keep_glu, send_glu = products(place, lefts, rights, pieces // 2)
-
-    def joined(keep, sent, axis):
-        value = over_line(keep + across(sent, 2), mine)
+    chunk_in = products(place, lefts, rights, pieces // 2, 2)
+    glu = Halving(keep_glu, across(send_glu, 2), mine)
+    chunk_in = tied([out], *chunk_in)
+    out.step()
+    first, second = (
+        Halving(keep, across(sent, 2), mine) for keep, sent in (chunk_in[:2], chunk_in[2:])
+    )
+
+    vectors = jnp.concatenate([lagsum[:, LANES - 1], jnp.sum(bias_part, axis=1)]).reshape(1, -1)
+    vectors = jnp.pad(vectors, ((0, 7), (0, LANES - vectors.shape[1])))
+    vectors = jnp.concatenate([vectors, shares], axis=1)
+    state = jnp.concatenate([jnp.concatenate([sums, firsts], axis=1), vectors], axis=0)
+    state = summed(state, ("batch",))
+    state = by_channel(jnp.broadcast_to(state[None], (pieces,) + state.shape))
+    glu.step()
+    (grad_normed, ffn_low) = tied([first], grad_normed, ffn_low)
+    first.step()
+    ffn_res = jnp.dot(ffn_low, ffn_out, preferred_element_type=F32) + ffn_out_bias
+    result = (hidden + ffn_res).astype(BF16).reshape(tokens.shape)
+    grad_tokens = last_norm(grad_normed, flat, line(norm1_gain), grad_hidden).reshape(tokens.shape)
+
+    def all_batches(value):
         bit = 2
         while bit < lax.axis_size("batch"):
             value = value + flipped(value, "batch", bit)
             bit *= 2
-        other = over_batch(value)
+        return value, over_batch(value)
+
+    def joined(value, other, axis):
         pick = batch_bit == 0
         return jnp.concatenate(
             [jnp.where(pick, value, other), jnp.where(pick, other, value)], axis=axis
         )
 
-    back = by_channel(turned.reshape(pieces, channels, rows)).reshape(pieces * channels, rows)
-    back, send_out = lax.optimization_barrier((back, send_out))
-    sum_out = joined(keep_out, send_out, 0)
-    grad_rows, sums, firsts, lagsum, bias_part = recurrence_back(
-        recv, back, enter, lags, lam, weight, skip, pieces, docs, BACKWARD_UNROLL
+    tied([second, glu])
+    second.step()
+    glu.step()
+    tied([first, out])
+    first.step()
+    half_out, other_out = all_batches(out.finish())
+    (state, other_out) = tied([second, glu], state, other_out)
+    second.step()
+    half_glu, other_glu = all_batches(glu.finish())
+    (other_glu,) = tied([second, first], other_glu)
+    half_in, other_in = all_batches(
+        jnp.concatenate([first.finish(), second.finish()], axis=1)
     )
-    small = jnp.concatenate([bias_glu, grad_g2, grad_b2, bias_in, bias_out], axis=1)
-    grad_rows, small, ffn_low = lax.optimization_barrier((grad_rows, small, ffn_low))
-    ffn_res = jnp.dot(ffn_low, ffn_out, preferred_element_type=F32) + ffn_out_bias
-    result = (hidden + ffn_res).astype(BF16).reshape(tokens.shape)
-    grad_normed = by_channel(grad_rows.reshape(pieces, channels, rows)).reshape(features, rows)
-    grad_tokens = last_norm(grad_normed, flat, line(norm1_gain), grad_hidden).reshape(tokens.shape)
-
-    sum_in = joined(keep_in, send_in, 1)
-    sum_glu = joined(keep_glu, send_glu, 1)
-
-    vectors = jnp.concatenate([lagsum[:, LANES - 1], jnp.sum(bias_part, axis=1)]).reshape(1, -1)
-    vectors = jnp.pad(vectors, ((0, 7), (0, 2 * LANES - vectors.shape[1])))
-    state = jnp.concatenate([jnp.concatenate([sums, firsts], axis=1), vectors], axis=0)
-    state = summed(state, ("batch",))
-    state = by_channel(jnp.broadcast_to(state[None], (pieces,) + state.shape))
-    vectors = state[:, channels]
+    sum_out, sum_glu = joined(half_out, other_out, 0), joined(half_glu, other_glu, 1)
+    sum_in = joined(half_in, other_in, 1)
+    vectors, shares = state[:, channels, :LANES], state[:, channels:, LANES:]
     grad_skip = vectors[:, :channels].reshape(features)
     grad_bias1 = vectors[:, channels : 2 * channels].reshape(features)
     state = state[:, :channels].reshape(features, 2 * LANES)
@@ -836,10 +900,12 @@
     grad_gain1 = (
         jnp.sum(w_re * m_re - w_im * m_im, axis=1) + skip_gain * grad_skip - norm1_bias * grad_bias1
     ) / norm1_gain
-    small = summed(small.reshape(-1, LANES), ("seq", "batch")).reshape(-1)
-    bias_glu, grad_g2, grad_b2, bias_in, bias_out = jnp.split(
-        small, [2 * features, 3 * features, 4 * features, small.shape[0] - features]
-    )
+    small, at = [], 0
+    for length in (ffn_in.shape[1], 2 * features, features, features, features):
+        count, wide = share_rows(length, pieces)
+        small.append(shares[:, at : at + count, :wide].reshape(length))
+        at += count
+    bias_in, bias_glu, grad_g2, grad_b2, bias_out = small
     return (
         result, grad_tokens, grad_gain1, grad_bias1, *grad_params, grad_skip,
         sum_glu, bias_glu, grad_g2, grad_b2, sum_in, bias_in, sum_out, bias_out,

time: 387 us -> 329 us (0.85)
  waiting for transfers between devices: 165 us -> 98.2 us
  other arithmetic: 27.9 us -> 37.9 us
  starting transfers between devices: 62.3 us -> 57.5 us
    ppermute x33 -> x31, waiting for transfers between devices: 154 us -> 70.7 us  [flipped(): return lax.ppermute(value, axis, [(i, i ^ bit) for i in range(count)])]
    all_to_all x5, waiting for transfers between devices: 11.2 us -> 27.5 us  [by_channel(): return lax.all_to_all(value, 'seq', 0, 0)]
    squeeze x3 -> x4, other arithmetic: 0.24 us -> 4.94 us  [finish(): return (self.keep + self.got)[0]]
    ppermute x33 -> x31, starting transfers between devices: 33.2 us -> 29.8 us  [flipped(): return lax.ppermute(value, axis, [(i, i ^ bit) for i in range(count)])]
    unnamed x125 -> x146, local copies, waits for them, and re-layouts: 22.5 us -> 23.6 us
  transfers between devices with their start and end apart: 38 -> 36, of which waited for: 13 -> 12; matrix products, arithmetic and copies ran while one was open for 17% -> 22% of each run, Pallas kernels for 16% -> 19%
where the time goes in v3:
time: 329 us; the launch traced here: 326 us
  waiting for transfers between devices  98.2 us (30%)
  Pallas kernels  73.4 us (22%)
  starting transfers between devices  57.5 us (17%)
  local copies, waits for them, and re-layouts  52.3 us (16%)
  other arithmetic  37.9 us (12%)
  matrix products  5.44 us (2%)
    ppermute x31, waiting for transfers between devices, flipped(): return lax.ppermute(value, axis, [(i, i ^ bit) for i in range(count)])  70.7 us
    ppermute x31, starting transfers between devices, flipped(): return lax.ppermute(value, axis, [(i, i ^ bit) for i in range(count)])  29.8 us
    all_to_all x5, starting transfers between devices, by_channel(): return lax.all_to_all(value, 'seq', 0, 0)  27.8 us
    all_to_all x5, waiting for transfers between devices, by_channel(): return lax.all_to_all(value, 'seq', 0, 0)  27.5 us
    pallas_call x1, Pallas kernels, recurrence_back(): pl.pallas_call(lambda *refs: backward_kernel(sizes, *refs), out_shape=(ja...  24.4 us
    unnamed x146, local copies, waits for them, and re-layouts  23.6 us
    pallas_call x1, Pallas kernels, downward(): pl.pallas_call(downward_kernel, in_specs=[SMEM] + [VMEM] * 6 + [ANY] * 3,...  13.4 us
    pallas_call x3, Pallas kernels, products(): pl.pallas_call(lambda *refs: product_kernel(count, *refs), in_specs=[SMEM...  13.2 us
  transfers between devices with their start and end apart: 36, of which 12 were waited for; matrix products, arithmetic and copies ran while one was open for 22% of the time, Pallas kernels for 19%

profile of v3, /device:TPU:0, one launch (start us, length us, event | category | flops | bytes accessed | tf_op | source)
XLA Modules:
  0.0 326.1 jit_solution(16364035446019976743)
XLA Ops:
  5.9 7.4 %all-to-all-start = ((f32[16,72,128]{2,1,0:T(8,128)}), f32[16,72,128]{2,1,0:T(8,128)S(1)}, u32[]{:S(2)}, u32[]{:S(2)}) async-start(f32[16,72,128]{2,1,0:T(8,128)} %get-tuple-element.78), calls=%async_computation | async-start | bytes 1179648 | tf_op jit(solution)/shard_map/all_to_all | solution.py:792
  17.0 11.9 %all-to-all-done = f32[16,72,128]{2,1,0:T(8,128)S(1)} async-done(((f32[16,72,128]{2,1,0:T(8,128)}), f32[16,72,128]{2,1,0:T(8,128)S(1)}, u32[]{:S(2)}, u32[]{:S(2)}) %all-to-all-start) | async-done | bytes 589856 | tf_op jit(solution)/shard_map/all_to_all | solution.py:792
  29.0 11.0 %recurrence.1 = (f32[1024,128]{1,0:T(8,128)}, f32[64,64,128]{2,1,0:T(8,128)S(1)}, f32[64,128]{1,0:T(8,128)S(1)}) custom-call(f32[1152,128]{1,0:T(8,128)S(1)} %bitcast.179, f32[64,128]{1,0:T(8,128)S(1)} %pad_maximum_fusion.4.refs_1_.refs_4_, f32[64,128]{1,0:T(8,128)S(1)} %pad_maximum_fusion.5.refs_2_.refs_5_, f32[64,128]{1,0:T(8,128)S(1)} %broadcast_in_dim.4.refs_3_.refs_6_), custom_call_target="tpu_custom_call" | custom-call | flops 16000000000 | tf_op jit(solution)/shard_map/recurrence/pallas_call | solution.py:374
  41.4 4.4 %all-to-all-start.1 = ((f32[16,64,128]{2,1,0:T(8,128)}), f32[16,64,128]{2,1,0:T(8,128)S(1)}, u32[]{:S(2)}, u32[]{:S(2)}) async-start(f32[16,64,128]{2,1,0:T(8,128)} %bitcast.8), calls=%async_computation.1 | async-start | bytes 1048576 | tf_op jit(solution)/shard_map/all_to_all | solution.py:792
  47.6 12.5 %collective-permute-done.3.refs_6_ = f32[128,1024]{1,0:T(8,128)S(1)} collective-permute-done((f32[128,1024]{1,0:T(8,128)S(1)}, f32[128,1024]{1,0:T(8,128)S(1)}, u32[]{:S(2)}, u32[]{:S(2)}) %collective-permute-start.3) | collective-permute-done | bytes 524320 | tf_op jit(solution)/shard_map/ppermute | solution.py:694
  62.5 7.8 %upward.1 = (f32[2,2,128,512]{3,2,1,0:T(8,128)}, f32[2,2,128,1024]{3,2,1,0:T(8,128)S(1)}, f32[128,2048]{1,0:T(8,128)S(1)}, f32[128,1024]{1,0:T(8,128)S(1)}, f32[...) custom-call(s32[3]{0:T(128)S(1)} %pad_add_fusion.refs_0_.place_ref, ...), custom_call_target="tpu_custom_call" | custom-call | flops 14000000000 | tf_op jit(solution)/shard_map/upward/pallas_call | solution.py:644
  74.1 13.4 %downward.1 = (f32[2,128,2048]{2,1,0:T(8,128)}, f32[2,128,1024]{2,1,0:T(8,128)S(1)}, f32[128,1024]{1,0:T(8,128)S(1)}, f32[16,72,128]{2,1,0:T(8,128)}) custom-call(s32[3]{0:T(128)S(1)} %pad_add_fusion.refs_0_.place_ref, bf16[128,1024]{1,0:T(8,128)(2,1)S(1)} %bitcast.187, f32[128,4096]{1,0:T(8,128)} %copy-done.41, ...), custom_call_target="tpu_custom_call" | custom-call | flops 17999998976 | tf_op jit(solution)/shard_map/downward/pallas_call | solution.py:662
  88.3 5.8 %all-to-all-start.2 = ((f32[16,72,128]{2,1,0:T(8,128)}), f32[16,72,128]{2,1,0:T(8,128)}, u32[]{:S(2)}, u32[]{:S(2)}) async-start(f32[16,72,128]{2,1,0:T(8,128)} %get-tuple-element.91), calls=%async_computation.2 | async-start | bytes 1179648 | tf_op jit(solution)/shard_map/all_to_all | solution.py:792
  94.2 4.1 %collective-permute-done = f32[2,128,1024]{2,1,0:T(8,128)} collective-permute-done((f32[2,128,1024]{2,1,0:T(8,128)}, f32[2,128,1024]{2,1,0:T(8,128)}, u32[]{:S(2)}, u32[]{:S(2)}) %collective-permute-start) | collective-permute-done | bytes 1048608 | tf_op jit(solution)/shard_map/ppermute | solution.py:694
  109.7 4.0 %products.3 = (f32[4,128,1024]{2,1,0:T(8,128)S(1)}, f32[4,128,1024]{2,1,0:T(8,128)S(1)}) custom-call(s32[3]{0:T(128)S(1)} %pad_add_fusion.refs_0_.place_ref, f32[128,1024]{1,0:T(8,128)S(1)} %copy-done.8, f32[128,1024]{1,0:T(8,128)S(1)} %get-tuple-element.202.refs_2_, f32[128,1024]{1,0:T(8,128)} %collective-permute-done.1.refs_3_, ...), custom_call_target="tpu_custom_call" | custom-call | flops 4000000000 | tf_op jit(solution)/shard_map/products/pallas_call | solution.py:683
  116.7 8.0 %collective-permute-done.8 = f32[2,2,128,512]{3,2,1,0:T(8,128)} collective-permute-done((f32[2,2,128,512]{3,2,1,0:T(8,128)}, f32[2,2,128,512]{3,2,1,0:T(8,128)}, u32[]{:S(2)}, u32[]{:S(2)}) %collective-permute-start.8) | collective-permute-done | bytes 1048608 | tf_op jit(solution)/shard_map/ppermute | solution.py:694
  130.0 24.4 %recurrence_back.1 = (f32[1024,128]{1,0:T(8,128)S(1)}, f32[64,128]{1,0:T(8,128)S(1)}, f32[64,128]{1,0:T(8,128)S(1)}, f32[64,128]{1,0:T(8,128)S(1)}, f32[64,128]{1,0:T(8,128)S(1)}) custom-call(f32[1152,128]{1,0:T(8,128)S(1)} %bitcast.180, f32[1152,128]{1,0:T(8,128)} %bitcast.19.refs_1_, f32[64,64,128]{2,1,0:T(8,128)S(1)} %copy-done.43, ...), custom_call_target="tpu_custom_call" | custom-call | flops 30000001024 | tf_op jit(solution)/shard_map/recurrence_back/pallas_call | solution.py:393
  166.6 3.4 %products.5 = (f32[4,64,1024]{2,1,0:T(8,128)S(1)}, f32[4,64,1024]{2,1,0:T(8,128)}) custom-call(s32[3]{0:T(128)S(1)} %pad_add_fusion.refs_0_.place_ref, f32[128,512]{1,0:T(8,128)S(1)} %copy-done.9, f32[128,512]{1,0:T(8,128)S(1)} %get-tuple-element.197.refs_2_, f32[128,512]{1,0:T(8,128)S(1)} %get-tuple-element.209.refs_3_, ...), custom_call_target="tpu_custom_call" | custom-call | flops 4000000000 | tf_op jit(solution)/shard_map/products/pallas_call | solution.py:683
  176.8 5.8 %products.4 = (f32[4,64,1024]{2,1,0:T(8,128)S(1)}, f32[4,64,1024]{2,1,0:T(8,128)}, f32[4,64,1024]{2,1,0:T(8,128)S(1)}, f32[4,64,1024]{2,1,0:T(8,128)S(1)}) custom-call(s32[3]{0:T(128)S(1)} %pad_add_fusion.refs_0_.place_ref, f32[128,512]{1,0:T(8,128)S(1)} %get-tuple-element.200.refs_1_, f32[128,512]{1,0:T(8,128)S(1)} %copy-done.11, ...), custom_call_target="tpu_custom_call" | custom-call | flops 4000000000 | tf_op jit(solution)/shard_map/products/pallas_call | solution.py:683
  184.5 4.9 %collective-permute-done.7 = f32[2,128,1024]{2,1,0:T(8,128)} collective-permute-done((f32[2,128,1024]{2,1,0:T(8,128)}, f32[2,128,1024]{2,1,0:T(8,128)}, u32[]{:S(2)}, u32[]{:S(2)}) %collective-permute-start.7) | collective-permute-done | bytes 1048608 | tf_op jit(solution)/shard_map/ppermute | solution.py:694
  191.1 4.7 %all-to-all-start.3 = ((f32[16,64,128]{2,1,0:T(8,128)}), f32[16,64,128]{2,1,0:T(8,128)}, u32[]{:S(2)}, u32[]{:S(2)}) async-start(f32[16,64,128]{2,1,0:T(8,128)} %bitcast.181), calls=%async_computation.3 | async-start | bytes 1048576 | tf_op jit(solution)/shard_map/all_to_all | solution.py:792
  208.4 15.5 %all-to-all-done.3 = f32[16,64,128]{2,1,0:T(8,128)} async-done(((f32[16,64,128]{2,1,0:T(8,128)}), f32[16,64,128]{2,1,0:T(8,128)}, u32[]{:S(2)}, u32[]{:S(2)}) %all-to-all-start.3) | async-done | bytes 524320 | tf_op jit(solution)/shard_map/all_to_all | solution.py:792
  225.0 5.4 %all-to-all-start.4 = ((f32[16,72,256]{2,1,0:T(8,128)}), f32[16,72,256]{2,1,0:T(8,128)}, u32[]{:S(2)}, u32[]{:S(2)}) async-start(f32[16,72,256]{2,1,0:T(8,128)} %broadcast_in_dim.5), calls=%async_computation.4 | async-start | bytes 2359296 | tf_op jit(solution)/shard_map/all_to_all | solution.py:792
  233.9 19.4 %collective-permute-done.15 = f32[4,64,1024]{2,1,0:T(8,128)} collective-permute-done((f32[4,64,1024]{2,1,0:T(8,128)}, f32[4,64,1024]{2,1,0:T(8,128)}, u32[]{:S(2)}, u32[]{:S(2)}) %collective-permute-start.15) | collective-permute-done | bytes 1048608 | tf_op jit(solution)/shard_map/ppermute | solution.py:694
  255.3 4.0 %collective-permute-start.22 = (f32[1,64,1024]{2,1,0:T(8,128)}, f32[1,64,1024]{2,1,0:T(8,128)S(1)}, u32[]{:S(2)}, u32[]{:S(2)}) collective-permute-start(f32[1,64,1024]{2,1,0:T(8,128)} %select_bitcast_fusion.8), channel_id=1, source_target_pairs={{0,8},{1,9},{2,10},{3,11},{4,12},{5,13},{6,14},{7,15},{8,0},{9,1},... | collective-permute-start | bytes 786440 | tf_op jit(solution)/shard_map/ppermute | solution.py:694
  261.6 5.4 %fusion.1 = bf16[128,1024]{1,0:T(8,128)(2,1)} fusion(f32[128,1024]{1,0:T(8,128)S(1)} %copy-done.5, bf16[128,4096]{1,0:T(8,128)(2,1)S(1)} %get-tuple-element.108, bf16[4096,1024]{1,0:T(8,128)(2,1)} %out_w_ref.1, f32[1024]{0:T(1024)S(1)} %copy-done.66), kind=kOutput, calls=%fused_computation.2 | convolution fusion | flops 1074135040 | bytes 10227712 | tf_op jit(solution)/shard_map/dot_general | solution.py:856
  274.6 11.1 %collective-permute-done.21 = f32[2,64,1024]{2,1,0:T(8,128)} collective-permute-done((f32[2,64,1024]{2,1,0:T(8,128)}, f32[2,64,1024]{2,1,0:T(8,128)}, u32[]{:S(2)}, u32[]{:S(2)}) %collective-permute-start.21) | collective-permute-done | bytes 524320 | tf_op jit(solution)/shard_map/ppermute | solution.py:694
  298.5 2.9 multiply_add_fusion
  319.8 5.2 %collective-permute-done.30 = f32[64,2048]{1,0:T(8,128)S(1)} collective-permute-done((f32[64,2048]{1,0:T(8,128)S(1)}, f32[64,2048]{1,0:T(8,128)S(1)}, u32[]{:S(2)}, u32[]{:S(2)}) %collective-permute-start.30) | collective-permute-done | bytes 524320 | tf_op jit(solution)/shard_map/ppermute | solution.py:694
  (279 shorter events, 122.2 us)
Async XLA Ops:
  5.9 22.9 %all-to-all-start = ((f32[16,72,128]{2,1,0:T(8,128)}), f32[16,72,128]{2,1,0:T(8,128)S(1)}, u32[]{:S(2)}, u32[]{:S(2)}) async-start(f32[16,72,128]{2,1,0:T(8,128)} %get-tuple-element.78), calls=%async_computation | async-start | bytes 1179648 | tf_op jit(solution)/shard_map/all_to_all | solution.py:792
  47.4 60.1 %collective-permute-start.4 = (f32[128,1024]{1,0:T(8,128)S(1)}, f32[128,1024]{1,0:T(8,128)}, u32[]{:S(2)}, u32[]{:S(2)}) collective-permute-start(f32[128,1024]{1,0:T(8,128)S(1)} %get-tuple-element.89.refs_5_), channel_id=1, source_target_pairs={{0,1},{1,0},{2,3},{3,2},{4,5},{5,4},{6,7},{7,6},{8,9},{9,8},{10,11... | collective-permute-start | bytes 1572872 | tf_op jit(solution)/shard_map/ppermute | solution.py:694
  60.2 47.9 %collective-permute-start.5 = (f32[128,1024]{1,0:T(8,128)S(1)}, f32[128,1024]{1,0:T(8,128)}, u32[]{:S(2)}, u32[]{:S(2)}) collective-permute-start(f32[128,1024]{1,0:T(8,128)S(1)} %collective-permute-done.3.refs_6_), channel_id=1, source_target_pairs={{0,1},{1,0},{2,3},{3,2},{4,5},{5,4},{6,7},{7,6},{8,9},{9,8},{10,11... | collective-permute-start | bytes 1572872 | tf_op jit(solution)/shard_map/ppermute | solution.py:694
  72.6 25.7 %collective-permute-start = (f32[2,128,1024]{2,1,0:T(8,128)}, f32[2,128,1024]{2,1,0:T(8,128)}, u32[]{:S(2)}, u32[]{:S(2)}) collective-permute-start(f32[2,128,1024]{2,1,0:T(8,128)} %slice_bitcast_fusion.4), channel_id=1, source_target_pairs={{0,16},{16,0},{1,17},{17,1},{2,18},{18,2},{3,19},{19,3},{4,20},{20... | collective-permute-start | bytes 3145736 | tf_op jit(solution)/shard_map/ppermute | solution.py:694
  74.1 34.2 %collective-permute-start.1 = (f32[128,1024]{1,0:T(8,128)}, f32[128,1024]{1,0:T(8,128)}, u32[]{:S(2)}, u32[]{:S(2)}) collective-permute-start(f32[128,1024]{1,0:T(8,128)} %get-tuple-element.183), channel_id=1, source_target_pairs={{0,1},{1,0},{2,3},{3,2},{4,5},{5,4},{6,7},{7,6},{8,9},{9,8},{10,11... | collective-permute-start | bytes 1572872 | tf_op jit(solution)/shard_map/ppermute | solution.py:694
  88.3 26.7 %all-to-all-start.2 = ((f32[16,72,128]{2,1,0:T(8,128)}), f32[16,72,128]{2,1,0:T(8,128)}, u32[]{:S(2)}, u32[]{:S(2)}) async-start(f32[16,72,128]{2,1,0:T(8,128)} %get-tuple-element.91), calls=%async_computation.2 | async-start | bytes 1179648 | tf_op jit(solution)/shard_map/all_to_all | solution.py:792
  98.3 26.4 %collective-permute-start.8 = (f32[2,2,128,512]{3,2,1,0:T(8,128)}, f32[2,2,128,512]{3,2,1,0:T(8,128)}, u32[]{:S(2)}, u32[]{:S(2)}) collective-permute-start(f32[2,2,128,512]{3,2,1,0:T(8,128)} %get-tuple-element.99), channel_id=1, source_target_pairs={{0,16},{16,0},{1,17},{17,1},{2,18},{18,2},{3,19},{19,3},{4,20},{20... | collective-permute-start | bytes 3145736 | tf_op jit(solution)/shard_map/ppermute | solution.py:694
  107.5 51.4 %collective-permute-start.11 = (f32[128,2048]{1,0:T(8,128)}, f32[128,2048]{1,0:T(8,128)}, u32[]{:S(2)}, u32[]{:S(2)}) collective-permute-start(f32[128,2048]{1,0:T(8,128)} %get-tuple-element.181), channel_id=1, source_target_pairs={{0,16},{16,0},{1,17},{17,1},{2,18},{18,2},{3,19},{19,3},{4,20},{20... | collective-permute-start | bytes 3145736 | tf_op jit(solution)/shard_map/ppermute | solution.py:694
  108.0 46.5 %collective-permute-start.9 = (f32[2,128,512]{2,1,0:T(8,128)}, f32[2,128,512]{2,1,0:T(8,128)}, u32[]{:S(2)}, u32[]{:S(2)}) collective-permute-start(f32[2,128,512]{2,1,0:T(8,128)} %slice_bitcast_fusion.14), channel_id=1, source_target_pairs={{0,1},{1,0},{2,3},{3,2},{4,5},{5,4},{6,7},{7,6},{8,9},{9,8},{10,11... | collective-permute-start | bytes 1572872 | tf_op jit(solution)/shard_map/ppermute | solution.py:694
  108.2 50.4 %collective-permute-start.16 = (f32[128,1024]{1,0:T(8,128)}, f32[128,1024]{1,0:T(8,128)}, u32[]{:S(2)}, u32[]{:S(2)}) collective-permute-start(f32[128,1024]{1,0:T(8,128)} %get-tuple-element.195), channel_id=1, source_target_pairs={{0,16},{16,0},{1,17},{17,1},{2,18},{18,2},{3,19},{19,3},{4,20},{20... | collective-permute-start | bytes 1572872 | tf_op jit(solution)/shard_map/ppermute | solution.py:694
  115.1 47.8 %collective-permute-start.6 = (f32[4,128,1024]{2,1,0:T(8,128)}, f32[4,128,1024]{2,1,0:T(8,128)S(1)}, u32[]{:S(2)}, u32[]{:S(2)}) collective-permute-start(f32[4,128,1024]{2,1,0:T(8,128)} %copy-done.24), channel_id=1, source_target_pairs={{0,2},{1,3},{2,0},{3,1},{4,6},{5,7},{6,4},{7,5},{8,10},{9,11},{10,... | collective-permute-start | bytes 6291464 | tf_op jit(solution)/shard_map/ppermute | solution.py:694
  125.8 33.4 %collective-permute-start.10 = (f32[2,128,512]{2,1,0:T(8,128)S(1)}, f32[2,128,512]{2,1,0:T(8,128)S(1)}, u32[]{:S(2)}, u32[]{:S(2)}) collective-permute-start(f32[2,128,512]{2,1,0:T(8,128)S(1)} %slice_bitcast_fusion.11), channel_id=1, source_target_pairs={{0,1},{1,0},{2,3},{3,2},{4,5},{5,4},{6,7},{7,6},{8,9},{9,8},{10,11... | collective-permute-start | bytes 1572872 | tf_op jit(solution)/shard_map/ppermute | solution.py:694
  164.9 24.5 %collective-permute-start.7 = (f32[2,128,1024]{2,1,0:T(8,128)}, f32[2,128,1024]{2,1,0:T(8,128)}, u32[]{:S(2)}, u32[]{:S(2)}) collective-permute-start(f32[2,128,1024]{2,1,0:T(8,128)} %get-tuple-element.180), channel_id=1, source_target_pairs={{0,4},{1,5},{2,6},{3,7},{4,0},{5,1},{6,2},{7,3},{8,12},{9,13},{10,... | collective-permute-start | bytes 3145736 | tf_op jit(solution)/shard_map/ppermute | solution.py:694
  170.0 28.6 %collective-permute-start.19 = (f32[4,64,1024]{2,1,0:T(8,128)}, f32[4,64,1024]{2,1,0:T(8,128)}, u32[]{:S(2)}, u32[]{:S(2)}) collective-permute-start(f32[4,64,1024]{2,1,0:T(8,128)} %get-tuple-element.116), channel_id=1, source_target_pairs={{0,2},{1,3},{2,0},{3,1},{4,6},{5,7},{6,4},{7,5},{8,10},{9,11},{10,... | collective-permute-start | bytes 3145736 | tf_op jit(solution)/shard_map/ppermute | solution.py:694
  173.4 22.5 %collective-permute-start.23 = (f32[72,256]{1,0:T(8,128)}, f32[72,256]{1,0:T(8,128)}, u32[]{:S(2)}, u32[]{:S(2)}) collective-permute-start(f32[72,256]{1,0:T(8,128)} %fusion.16), channel_id=1, source_target_pairs={{0,16},{16,0},{1,17},{17,1},{2,18},{18,2},{3,19},{19,3},{4,20},{20... | collective-permute-start | bytes 221192 | tf_op jit(solution)/shard_map/ppermute | solution.py:694
  189.5 40.9 %collective-permute-start.14 = (f32[4,64,1024]{2,1,0:T(8,128)}, f32[4,64,1024]{2,1,0:T(8,128)}, u32[]{:S(2)}, u32[]{:S(2)}) collective-permute-start(f32[4,64,1024]{2,1,0:T(8,128)} %get-tuple-element.105), channel_id=1, source_target_pairs={{0,2},{1,3},{2,0},{3,1},{4,6},{5,7},{6,4},{7,5},{8,10},{9,11},{10,... | collective-permute-start | bytes 3145736 | tf_op jit(solution)/shard_map/ppermute | solution.py:694
  191.1 32.7 %all-to-all-start.3 = ((f32[16,64,128]{2,1,0:T(8,128)}), f32[16,64,128]{2,1,0:T(8,128)}, u32[]{:S(2)}, u32[]{:S(2)}) async-start(f32[16,64,128]{2,1,0:T(8,128)} %bitcast.181), calls=%async_computation.3 | async-start | bytes 1048576 | tf_op jit(solution)/shard_map/all_to_all | solution.py:792
  196.7 56.6 %collective-permute-start.15 = (f32[4,64,1024]{2,1,0:T(8,128)}, f32[4,64,1024]{2,1,0:T(8,128)}, u32[]{:S(2)}, u32[]{:S(2)}) collective-permute-start(f32[4,64,1024]{2,1,0:T(8,128)} %copy-done.25), channel_id=1, source_target_pairs={{0,2},{1,3},{2,0},{3,1},{4,6},{5,7},{6,4},{7,5},{8,10},{9,11},{10,... | collective-permute-start | bytes 3145736 | tf_op jit(solution)/shard_map/ppermute | solution.py:694
  201.3 32.6 %collective-permute-start.20 = (f32[2,64,1024]{2,1,0:T(8,128)}, f32[2,64,1024]{2,1,0:T(8,128)}, u32[]{:S(2)}, u32[]{:S(2)}) collective-permute-start(f32[2,64,1024]{2,1,0:T(8,128)} %select_bitcast_fusion.5), channel_id=1, source_target_pairs={{0,4},{1,5},{2,6},{3,7},{4,0},{5,1},{6,2},{7,3},{8,12},{9,13},{10,... | collective-permute-start | bytes 1572872 | tf_op jit(solution)/shard_map/ppermute | solution.py:694
  206.0 61.0 %collective-permute-start.25 = (f32[1,128,1024]{2,1,0:T(8,128)}, f32[1,128,1024]{2,1,0:T(8,128)}, u32[]{:S(2)}, u32[]{:S(2)}) collective-permute-start(f32[1,128,1024]{2,1,0:T(8,128)} %select_bitcast_fusion.2), channel_id=1, source_target_pairs={{0,8},{1,9},{2,10},{3,11},{4,12},{5,13},{6,14},{7,15},{8,0},{9,1},... | collective-permute-start | bytes 1572872 | tf_op jit(solution)/shard_map/ppermute | solution.py:694
  225.0 49.7 %all-to-all-start.4 = ((f32[16,72,256]{2,1,0:T(8,128)}), f32[16,72,256]{2,1,0:T(8,128)}, u32[]{:S(2)}, u32[]{:S(2)}) async-start(f32[16,72,256]{2,1,0:T(8,128)} %broadcast_in_dim.5), calls=%async_computation.4 | async-start | bytes 2359296 | tf_op jit(solution)/shard_map/all_to_all | solution.py:792
  231.9 37.8 %collective-permute-start.24 = (f32[2,64,1024]{2,1,0:T(8,128)S(1)}, f32[2,64,1024]{2,1,0:T(8,128)S(1)}, u32[]{:S(2)}, u32[]{:S(2)}) collective-permute-start(f32[2,64,1024]{2,1,0:T(8,128)S(1)} %select_bitcast_fusion.3), channel_id=1, source_target_pairs={{0,4},{1,5},{2,6},{3,7},{4,0},{5,1},{6,2},{7,3},{8,12},{9,13},{10,... | collective-permute-start | bytes 1572872 | tf_op jit(solution)/shard_map/ppermute | solution.py:694
  261.5 24.2 %collective-permute-start.21 = (f32[2,64,1024]{2,1,0:T(8,128)}, f32[2,64,1024]{2,1,0:T(8,128)}, u32[]{:S(2)}, u32[]{:S(2)}) collective-permute-start(f32[2,64,1024]{2,1,0:T(8,128)} %select_bitcast_fusion.4), channel_id=1, source_target_pairs={{0,4},{1,5},{2,6},{3,7},{4,0},{5,1},{6,2},{7,3},{8,12},{9,13},{10,... | collective-permute-start | bytes 1572872 | tf_op jit(solution)/shard_map/ppermute | solution.py:694
  274.6 34.6 %collective-permute-start.28 = (f32[1,64,1024]{2,1,0:T(8,128)}, f32[1,64,1024]{2,1,0:T(8,128)}, u32[]{:S(2)}, u32[]{:S(2)}) collective-permute-start(f32[1,64,1024]{2,1,0:T(8,128)} %select_bitcast_fusion.6), channel_id=1, source_target_pairs={{0,8},{1,9},{2,10},{3,11},{4,12},{5,13},{6,14},{7,15},{8,0},{9,1},... | collective-permute-start | bytes 786440 | tf_op jit(solution)/shard_map/ppermute | solution.py:694
  (80 other events, 687.7 us)

commit v4 on v3

--- a/solution.py
+++ b/solution.py
@@ -488,17 +488,27 @@
     return out
 
 
-def by_core(values, place_ref, out_ref, at, pieces):
+def by_core(values, place_ref, out_ref, pieces):
     wide = values.shape[1] // pieces
     for s in range(pieces):
-        slot = (s % 2) ^ place_ref[0]
-        out_ref[slot, at, :, (s // 2) * wide : (s // 2 + 1) * wide] = values[:, s * wide : (s + 1) * wide]
+        out_ref[(s % 2) ^ place_ref[0], :, (s // 2) * wide : (s // 2 + 1) * wide] = (
+            values[:, s * wide : (s + 1) * wide]
+        )
+
+
+def by_pair(values, place_ref, out_ref, pieces):
+    wide = values.shape[1] // pieces
+    for s in range(pieces):
+        at = (s // 8 * 2 + s // 2 % 2) * wide
+        out_ref[(s // 4 % 2) ^ place_ref[3], (s % 2) ^ place_ref[0], :, at : at + wide] = (
+            values[:, s * wide : (s + 1) * wide]
+        )
 
 
 def upward_kernel(
     pieces, place_ref, mixed_ref, tokens_ref, glu_bias_ref, gain_ref, bias_ref, ffn_bias_ref, glu_ref, ffn_ref,
-    acts_ref, keep_ref, pre_ref, hidden_ref, slope1_ref, slope2_ref, low_ref,
-    glu_v, ffn_v, glu_sem, ffn_sem,
+    act_ref, z2_ref, keep_here_ref, keep_there_ref, send_here_ref, send_there_ref, pre_ref, hidden_ref, slope1_ref, slope2_ref, low_ref,
+    glu_v, ffn_v, parts_ref, glu_sem, ffn_sem, out_sem,
 ):
     rows, features = tokens_ref.shape
     glu_copies = fetch(glu_ref, glu_v, glu_sem, 4, False)
@@ -507,7 +517,7 @@
     share, steep = bell(mixed)
     slope1_ref[...] = share + steep
     act = (mixed * share).astype(BF16)
-    by_core(act.astype(F32), place_ref, acts_ref, 0, pieces)
+    by_core(act.astype(F32), place_ref, act_ref, pieces)
     wide = glu_ref.shape[1] // 4
     for i in range(4):
         glu_copies[i].wait()
@@ -519,7 +529,7 @@
     hidden_ref[...] = hidden
     unit, _ = normalize(hidden)
     normed = (unit * gain_ref[...] + bias_ref[...]).astype(BF16)
-    by_core(normed.astype(F32), place_ref, acts_ref, 1, pieces)
+    by_pair(normed.astype(F32), place_ref, z2_ref, pieces)
     wide = ffn_ref.shape[1] // 8
     block = ffn_ref.shape[1] // pieces // 2
     for i in range(8):
@@ -534,17 +544,28 @@
         for k in range(wide // block):
             index = (i * wide) // block + k
             piece, half = index // 2, index % 2
-            keep_ref[
+            parts_ref[
                 half ^ place_ref[1], (piece % 2) ^ place_ref[0], :,
                 (piece // 2) * block : (piece // 2 + 1) * block,
             ] = wider[:, k * block : (k + 1) * block]
+    copies = []
+    for k, ref in enumerate((keep_here_ref, keep_there_ref, send_here_ref, send_there_ref)):
+        copies.append(pltpu.make_async_copy(parts_ref.at[k // 2, k % 2], ref, out_sem.at[k]))
+        copies[-1].start()
+    for copy in copies:
+        copy.wait()
+
+
+def store(ref, columns, value):
+    ref[:, columns] = value
 
 
 def downward_kernel(
-    place_ref, cot_ref, slope2_ref, hidden_ref, pre_ref, slope1_ref, gain_ref, out_w_ref, in_w_ref, glu_w_ref,
-    sent_pre_ref, sent_glu_ref, grad_hidden_ref, turned_ref,
+    place_ref, cot_ref, slope2_ref, hidden_ref, pre_ref, slope1_ref, gain_ref, act_ref, z2_ref,
+    out_w_ref, in_w_ref, glu_w_ref,
+    in_keep_ref, in_send_ref, glu_keep_ref, glu_send_ref, grad_hidden_ref, turned_ref,
     in_sum_ref, glu_sum_ref, gain_sum_ref, bias_sum_ref, out_sum_ref,
-    out_v, in_v, glu_v, out_sem, in_sem, glu_sem,
+    out_v, in_v, glu_v, parts_ref, out_sem, in_sem, glu_sem, keep_sem, send_sem,
 ):
     rows, features = cot_ref.shape
     inner = out_w_ref.shape[0]
@@ -552,6 +573,20 @@
     out_copies = fetch(out_w_ref, out_v, out_sem, 8, True)
     in_copies = fetch(in_w_ref, in_v, in_sem, 8, False)
     glu_copies = fetch(glu_w_ref, glu_v, glu_sem, 1, False)
+    copies = []
+
+    def pass_on(source, target, sem):
+        copies.append(pltpu.make_async_copy(source, target, sem))
+        copies[-1].start()
+
+    quarter, half = features // 4, features // 2
+    for k in range(2):
+        columns = slice(features + k * half, features + (k + 1) * half)
+        glu_keep_ref[:, columns] = act_ref[k]
+        glu_send_ref[:, columns] = act_ref[k]
+        columns = pl.ds(inner + k * quarter, quarter)
+        pass_on(z2_ref.at[0, k], in_keep_ref.at[:, columns], keep_sem.at[8 + k])
+        pass_on(z2_ref.at[1, k], in_send_ref.at[:, columns], send_sem.at[8 + k])
     cot = cot_ref[...]
     up = cot.astype(F32)
     out_sum_ref[...] = jnp.sum(up, axis=0, keepdims=True)
@@ -563,7 +598,10 @@
         low = (grad * slope2_ref[:, at]).astype(BF16)
         wider = low.astype(F32)
         in_sum_ref[:, at] = jnp.sum(wider, axis=0, keepdims=True)
-        sent_pre_ref[(i // 4) ^ place_ref[1], :, (i % 4) * wide : (i % 4 + 1) * wide] = wider
+        parts_ref[:, at] = wider
+        columns = pl.ds(i * wide, wide)
+        pass_on(parts_ref.at[:, columns], in_keep_ref.at[:, columns], keep_sem.at[i])
+        pass_on(parts_ref.at[:, columns], in_send_ref.at[:, columns], send_sem.at[i])
         in_copies[i].wait()
         total = total + lax.dot_general(low, in_v[:, at], NT, preferred_element_type=F32)
     unit, recip = normalize(hidden_ref[...])
@@ -580,7 +618,10 @@
         wider = part.astype(F32)
         at = slice(k * features, (k + 1) * features)
         glu_sum_ref[:, at] = jnp.sum(wider, axis=0, keepdims=True)
-        sent_glu_ref[k ^ place_ref[1]] = wider
+        kept = k ^ place_ref[1] == 0
+        columns = slice(0, features)
+        pl.when(kept)(functools.partial(store, glu_keep_ref, columns, wider))
+        pl.when(jnp.logical_not(kept))(functools.partial(store, glu_send_ref, columns, wider))
         term = lax.dot_general(part, glu_v[:, at], NT, preferred_element_type=F32)
         grad_act = term if grad_act is None else grad_act + term
     turn = turning(rows)
@@ -589,29 +630,45 @@
     share_vectors(
         (in_sum_ref, glu_sum_ref, gain_sum_ref, bias_sum_ref, out_sum_ref), turned_ref, turned_ref.shape[1] - 8
     )
-
-
-def product_kernel(count, place_ref, *refs):
-    lefts, rights = refs[:count], refs[count : 2 * count]
-    outs, scratch_ref = refs[2 * count : -1], refs[-1]
-    total = None
-    for left, right in zip(lefts, rights):
-        term = lax.dot_general(
-            left[...].astype(BF16), right[...].astype(BF16), TN, preferred_element_type=F32
-        )
-        total = term if total is None else total + term
-    scratch_ref[...] = total
-    blocks, height, wide = outs[0].shape
-    for i in range(blocks):
-        for k, ref in enumerate(outs):
-            block = 2 * i + (place_ref[2] ^ (k % 2))
-            columns = slice(k // 2 * wide, (k // 2 + 1) * wide)
-            ref[i] = scratch_ref[pl.ds(pl.multiple_of(block * height, 8), height), columns]
+    for copy in copies:
+        copy.wait()
+
+
+def product_kernel(spans, by_batch, place_ref, *refs):
+    many = 1 + max(at for span in spans for at, _ in span)
+    values, outs, scratch_ref = refs[:many], refs[many:-1], refs[-1]
+    start = 0
+    for k in range(len(spans[0]) - 1):
+        total = None
+        for span in spans:
+            (left, rows), (right, columns) = span[0], span[k + 1]
+            term = dot(
+                values[left][:, rows].astype(BF16), values[right][:, columns].astype(BF16), TN
+            )
+            total = term if total is None else total + term
+        scratch_ref[:, start : start + total.shape[1]] = total
+        start += total.shape[1]
+    blocks, height, _ = outs[0].shape
+    start = 0
+    for k, ref in enumerate(outs):
+        wide = ref.shape[2]
+        for i in range(blocks):
+            if by_batch:
+                half = scratch_ref.shape[1] // 2
+                columns = pl.ds(pl.multiple_of((place_ref[1] ^ (k % 2)) * half + start, LANES), wide)
+                ref[i] = scratch_ref[i * height : (i + 1) * height, columns]
+            else:
+                block = 2 * i + (place_ref[2] ^ (k % 2))
+                ref[i] = scratch_ref[
+                    pl.ds(pl.multiple_of(block * height, 8), height), start : start + wide
+                ]
+        start += k % 2 * wide
 
 
 SMEM = pl.BlockSpec(memory_space=pltpu.SMEM)
 VMEM = pl.BlockSpec(memory_space=pltpu.VMEM)
-ANY = pl.BlockSpec(memory_space=pl.ANY)
+WHOLE = pl.BlockSpec()
+HBM = pl.BlockSpec(memory_space=pltpu.HBM)
 
 
 def shaped(*shape, dtype=F32):
@@ -643,50 +700,145 @@
     inner = ffn_in.shape[1]
     return pl.pallas_call(
         lambda *refs: upward_kernel(pieces, *refs),
-        in_specs=[SMEM] + [VMEM] * 6 + [ANY] * 2,
+        in_specs=[SMEM] + [VMEM] * 6 + [HBM] * 2,
+        out_specs=(WHOLE, WHOLE) + (HBM,) * 4 + (WHOLE,) * 5,
         out_shape=(
-            shaped(2, 2, rows, features // 2), shaped(2, 2, rows, inner // 4), shaped(rows, 2 * features),
+            shaped(2, rows, features // 2), shaped(2, 2, rows, features // 4),
+            *(shaped(rows, inner // 4),) * 4, shaped(rows, 2 * features),
             shaped(rows, features), shaped(rows, features), shaped(rows, inner), shaped(rows, inner, dtype=BF16),
         ),
         scratch_shapes=[
             pltpu.VMEM(glu_weight.shape, BF16), pltpu.VMEM(ffn_in.shape, BF16),
-            pltpu.SemaphoreType.DMA((4,)), pltpu.SemaphoreType.DMA((8,)),
+            pltpu.VMEM((2, 2, rows, inner // 4), F32),
+            pltpu.SemaphoreType.DMA((4,)), pltpu.SemaphoreType.DMA((8,)), pltpu.SemaphoreType.DMA((4,)),
         ],
-        compiler_params=params_of(40), cost_estimate=estimate(14), name="upward",
+        compiler_params=params_of(56), cost_estimate=estimate(14), name="upward",
     )(place, mixed, tokens, glu_bias, gain, bias, ffn_bias, glu_weight, ffn_in)
 
 
-def downward(place, cot, slope2, hidden, pre, slope1, gain, ffn_out, ffn_in, glu_weight, pieces):
+def downward(place, cot, slope2, hidden, pre, slope1, gain, act, z2, ffn_out, ffn_in, glu_weight, pieces):
     rows, features = cot.shape
     inner = ffn_in.shape[1]
     return pl.pallas_call(
         downward_kernel,
-        in_specs=[SMEM] + [VMEM] * 6 + [ANY] * 3,
+        in_specs=[SMEM] + [VMEM] * 8 + [HBM] * 3,
+        out_specs=(HBM, HBM) + (WHOLE,) * 4,
         out_shape=(
-            shaped(2, rows, inner // 2), shaped(2, rows, features), shaped(rows, features),
+            shaped(rows, inner + features // 2), shaped(rows, inner + features // 2),
+            shaped(rows, 2 * features), shaped(rows, 2 * features),
+            shaped(rows, features),
             shaped(pieces, features // pieces + 8, rows),
         ),
         scratch_shapes=[
             pltpu.VMEM((1, inner), F32), pltpu.VMEM((1, 2 * features), F32), pltpu.VMEM((1, features), F32),
             pltpu.VMEM((1, features), F32), pltpu.VMEM((1, features), F32),
             pltpu.VMEM(ffn_out.shape, BF16), pltpu.VMEM(ffn_in.shape, BF16), pltpu.VMEM(glu_weight.shape, BF16),
+            pltpu.VMEM((rows, inner), F32),
             pltpu.SemaphoreType.DMA((8,)), pltpu.SemaphoreType.DMA((8,)), pltpu.SemaphoreType.DMA((1,)),
+            pltpu.SemaphoreType.DMA((10,)), pltpu.SemaphoreType.DMA((10,)),
         ],
-        compiler_params=params_of(48), cost_estimate=estimate(18), name="downward",
-    )(place, cot, slope2, hidden, pre, slope1, gain, ffn_out, ffn_in, glu_weight)
-
-
-def products(place, lefts, rights, blocks, chunks=1):
-    count = len(lefts)
-    tall, wide = lefts[0].shape[-1], rights[0].shape[-1]
-    out = shaped(blocks // 2, tall // blocks, wide // chunks)
+        compiler_params=params_of(56), cost_estimate=estimate(18), name="downward",
+    )(place, cot, slope2, hidden, pre, slope1, gain, act, z2, ffn_out, ffn_in, glu_weight)
+
+
+def products(place, values, spans, tall, wide, blocks, chunks=1, by_batch=False):
+    if by_batch:
+        out = shaped(blocks, tall // blocks, wide // 2 // chunks)
+    else:
+        out = shaped(blocks // 2, tall // blocks, wide // chunks)
     return pl.pallas_call(
-        lambda *refs: product_kernel(count, *refs),
-        in_specs=[SMEM] + [VMEM] * (2 * count),
+        lambda *refs: product_kernel(spans, by_batch, *refs),
+        in_specs=[SMEM] + [VMEM] * len(values),
         out_shape=(out,) * (2 * chunks),
         scratch_shapes=[pltpu.VMEM((tall, wide), F32)],
-        compiler_params=params_of(40), cost_estimate=estimate(4), name="products",
-    )(place, *lefts, *rights)
+        compiler_params=params_of(28), cost_estimate=estimate(4), name="products",
+    )(place, *values)
+
+
+def assemble_kernel(axis, place_ref, *refs):
+    parts, out_ref = refs[:-1], refs[-1]
+    many = len(parts) // 2
+    half = out_ref.shape[axis] // 2
+    for k in range(2):
+        start = (place_ref[1] ^ k) * half
+        for part in parts[k * many : (k + 1) * many]:
+            size = part.shape[axis]
+            if axis:
+                out_ref[:, pl.ds(pl.multiple_of(start, LANES), size)] = part[...]
+            else:
+                out_ref[pl.ds(pl.multiple_of(start, 8), size), :] = part[...]
+            start = start + size
+
+
+def assembled(place, own, others, axis):
+    shape = list(own[0].shape)
+    shape[axis] = 2 * sum(part.shape[axis] for part in own)
+    return pl.pallas_call(
+        functools.partial(assemble_kernel, axis),
+        in_specs=[SMEM] + [VMEM] * (len(own) + len(others)),
+        out_shape=shaped(*shape), compiler_params=params_of(16), cost_estimate=estimate(1), name="assembled",
+    )(place, *own, *others)
+
+
+def pull_kernel(lengths, place_ref, own_ref, other_ref, *refs):
+    out_c, out_b, weight, out_d, out_a, gain_in, bias_in, skip_in, step_in, real_in, freq_in = refs[:11]
+    decay_ref, freq_ref, in_re_ref, in_im_ref, out_re_ref, out_im_ref = refs[11:17]
+    step_ref, skip_ref, gain_ref, bias_ref = refs[17:21]
+    vector_refs, products_ref, slopes_ref = refs[21:-2], refs[-2], refs[-1]
+    blocks, pitch, _ = own_ref.shape
+    channels = pitch - 8
+    first_core = place_ref[0] == 0
+    half = LANES // 2
+    for s in range(2 * blocks):
+        own, other = own_ref[s // 2], other_ref[s // 2]
+        here = first_core if s % 2 == 0 else jnp.logical_not(first_core)
+        state = jnp.where(here, own, other)
+        at = slice(s * channels, (s + 1) * channels)
+        total = as_factor(state[:channels, :LANES])
+        moment = as_factor(state[:channels, LANES:])
+        grad_c = times(out_c[at, :], total)
+        out_re_ref[at, :] = grad_c[:, :half]
+        out_im_ref[at, :] = -grad_c[:, half:]
+        grad_b = times(out_b[at, :], total)
+        in_re_ref[at, :] = grad_b[:, :half]
+        in_im_ref[at, :] = -grad_b[:, half:]
+        table = weight[at, :]
+        products_ref[at, :] = table * total[0] + swap(table) * total[1]
+        grad_d = times(table, moment) + times(out_d[at, :], total)
+        grad_a = times(out_a[at, :], total) + step_in[at, :] * grad_d
+        decay_ref[at, :] = real_in[at, :half] * grad_a[:, :half]
+        freq_ref[at, :] = -grad_a[:, half:]
+        slopes_ref[at, :] = step_in[at, :] * (real_in[at, :] * grad_d - freq_in[at, :] * swap(grad_d))
+        columns = slice(s * channels, (s + 1) * channels)
+        skip_ref[:, columns] = state[channels : channels + 1, :channels]
+        bias_ref[:, columns] = state[channels : channels + 1, channels : 2 * channels]
+        row = channels
+        for ref, length in zip(vector_refs, lengths):
+            count, wide = share_rows(length, 2 * blocks)
+            for r in range(count):
+                start = (s * count + r) * wide
+                ref[:, start : start + wide] = state[row + r : row + r + 1, LANES : LANES + wide]
+            row += count
+    ones = jnp.where(low_lanes((8, LANES)), 1.0, 0.0).astype(BF16)
+    sums = []
+    for ref in (slopes_ref, products_ref):
+        high, low = halves(ref[...])
+        sums.append((dot(ones, high, NT) + dot(ones, low, NT))[0:1])
+    step_ref[...] = sums[0]
+    gain_ref[...] = (sums[1] + skip_in[...] * skip_ref[...] - bias_in[...] * bias_ref[...]) / gain_in[...]
+
+
+def pulled(place, own, other, tables, gain, bias, skip, step, real, freq, lengths):
+    features = tables[0].shape[0]
+    row = shaped(1, features)
+    table = shaped(features, LANES // 2)
+    return pl.pallas_call(
+        functools.partial(pull_kernel, lengths),
+        in_specs=[SMEM] + [VMEM] * 13,
+        out_shape=(table,) * 6 + (row,) * 4 + tuple(shaped(1, length) for length in lengths),
+        scratch_shapes=[pltpu.VMEM((features, LANES), F32)] * 2,
+        compiler_params=params_of(32), cost_estimate=estimate(4), name="pulled",
+    )(place, own, other, *tables, gain, bias, skip, step, real, freq)
 
 
 def flipped(value, axis, bit):
@@ -719,18 +871,18 @@
 
 
 class Halving:
-    def __init__(self, keep, got, mine):
-        self.keep, self.got, self.mine, self.bit = keep, got, mine, 4
+    def __init__(self, keep, got, mine, bits):
+        self.keep, self.got, self.mine, self.bits = keep, got, mine, list(bits)
 
     def step(self):
+        bit = self.bits.pop(0)
         blocks = self.keep + self.got
         pairs = blocks.reshape((blocks.shape[0] // 2, 2) + blocks.shape[1:])
-        self.keep, send = halved(pairs, 1, (self.mine // self.bit) % 2)
-        self.got = across(send, self.bit)
-        self.bit *= 2
+        self.keep, send = halved(pairs, 1, (self.mine // bit) % 2)
+        self.got = across(send, bit)
 
     def finish(self):
-        while self.keep.shape[0] > 1:
+        while self.bits:
             self.step()
         return (self.keep + self.got)[0]
 
@@ -742,23 +894,37 @@
     return out[len(works) :]
 
 
-def mode_parts(params):
+def times_pair(left, right):
+    return left[0] * right[0] - left[1] * right[1], left[0] * right[1] + left[1] * right[0]
+
+
+def mode_tables(params):
     decay_log, decay_freq, input_re, input_im, output_re, output_im, step_log = params
     step_size = jnp.exp(step_log)[:, None]
     real_part = -jnp.exp(decay_log)
     delta_re = step_size * real_part
     delta_im = step_size * decay_freq
     magnitude = jnp.exp(delta_re)
-    lam_re, lam_im = (magnitude * jnp.cos(delta_im), magnitude * jnp.sin(delta_im))
+    lam = (magnitude * jnp.cos(delta_im), magnitude * jnp.sin(delta_im))
     denominator = real_part * real_part + decay_freq * decay_freq
-    num_re = lam_re - 1.0
-    rat_re = (num_re * real_part + lam_im * decay_freq) / denominator
-    rat_im = (lam_im * real_part - num_re * decay_freq) / denominator
-    bbar_re = rat_re * input_re - rat_im * input_im
-    bbar_im = rat_re * input_im + rat_im * input_re
-    prod_re = 2.0 * (output_re * bbar_re - output_im * bbar_im)
-    prod_im = 2.0 * (output_re * bbar_im + output_im * bbar_re)
-    return (delta_re, delta_im, prod_re, prod_im), (lam_re, lam_im)
+    inverse = (real_part / denominator, -decay_freq / denominator)
+    num_re = lam[0] - 1.0
+    ratio = (
+        (num_re * real_part + lam[1] * decay_freq) / denominator,
+        (lam[1] * real_part - num_re * decay_freq) / denominator,
+    )
+    doubled = (2.0 * output_re, 2.0 * output_im)
+    bbar = times_pair(ratio, (input_re, input_im))
+    weight = times_pair(doubled, bbar)
+    both = times_pair(times_pair(doubled, (input_re, input_im)), inverse)
+    tables = (
+        (2.0 * bbar[0], 2.0 * bbar[1]),
+        times_pair(doubled, ratio),
+        weight,
+        times_pair(both, lam),
+        tuple(-part for part in times_pair(both, ratio)),
+    )
+    return lam, weight, tables, step_size, real_part
 
 
 def packed(real, imag):
@@ -777,7 +943,8 @@
     docs = max(1, pieces * piece_len // 256)
     params = (decay_log, decay_freq, input_re, input_im, output_re, output_im, step_log)
     batch_bit = lax.axis_index("batch") % 2
-    place = jnp.stack([mine % 2, batch_bit, (mine // 2) % 2]).astype(jnp.int32)
+    place = jnp.stack([mine % 2, batch_bit, (mine // 2) % 2, (mine // 4) % 2]).astype(jnp.int32)
+    high_bits = [1 << k for k in range(3, pieces.bit_length() - 1)]
 
     def own(value):
         return lax.dynamic_slice_in_dim(value, mine * channels, channels, 0)
@@ -791,8 +958,8 @@
     def by_channel(value):
         return lax.all_to_all(value, "seq", 0, 0)
 
-    parts, lam_pair = mode_parts(tuple(own(p) for p in params))
-    lam, weight = packed(*lam_pair), packed(parts[2], parts[3])
+    lam_pair, weight_pair = mode_tables(tuple(own(p) for p in params))[:2]
+    lam, weight = packed(*lam_pair), packed(*weight_pair)
     skip = row_of(skip_gain)
     flat = tokens.reshape(rows, features)
     cot = cotangent.reshape(rows, features)
@@ -800,62 +967,76 @@
     send, up = first_norm(
         flat, cot, segments.reshape(1, rows), line(norm1_gain), line(norm1_bias), pieces
     )
-    recv = by_channel(send).reshape(pieces * (channels + 8), rows)
+    recv = by_channel(send)
+    _, _, tables, step_size, real_part = mode_tables(params)
+    tables = tuple(packed(*pair) for pair in tables)
+    around = (
+        jnp.broadcast_to(step_size, tables[0].shape),
+        packed(real_part, real_part),
+        packed(decay_freq, decay_freq),
+    )
+    recv = recv.reshape(pieces * (channels + 8), rows)
     up_x = over_batch(up)
     ups = [up, up_x, across(up), across(up_x)]
     mixed_rows, enter, lags = recurrence(recv, lam, weight, skip, pieces, docs, FORWARD_UNROLL)
-    mixed = by_channel(mixed_rows.reshape(pieces, channels, rows)).reshape(features, rows)
-    acts, ffn_parts, glu_pre, hidden, slope1, slope2, ffn_low = upward(
+    mixed = by_channel(mixed_rows.reshape(pieces, channels, rows))
+    mixed, *ups = lax.optimization_barrier((mixed, *ups))
+    mixed = mixed.reshape(features, rows)
+    act_parts, z2_parts, ffn_here, ffn_there, ffn_send_here, ffn_send_there, glu_pre, hidden, slope1, slope2, ffn_low = upward(
         place, mixed, flat, line(glu_bias), line(norm2_gain), line(norm2_bias), line(ffn_in_bias),
         glu_weight, ffn_in, pieces,
     )
-    pre_parts, glu_parts, grad_hidden, turned = downward(
-        place, cot, slope2, hidden, glu_pre, slope1, line(norm2_gain), ffn_out, ffn_in, glu_weight, pieces
-    )
-
-    ffn_x = over_batch(ffn_parts[1])
-    acts, pre_parts, glu_parts, ffn_x = lax.optimization_barrier((acts, pre_parts, glu_parts, ffn_x))
-    acts_x, pre_x, glu_x = over_batch(acts), over_batch(pre_parts[1]), over_batch(glu_parts[1])
-    lefts = [ffn_parts[0, 0], ffn_x[0], across(ffn_parts[0, 1]), across(ffn_x[1])]
-    keep_out, send_out = products(place, lefts, ups, pieces // 2)
+    in_keep, in_send, glu_keep, glu_send, grad_hidden, turned = downward(
+        place, cot, slope2, hidden, glu_pre, slope1, line(norm2_gain), act_parts, z2_parts, ffn_out, ffn_in, glu_weight, pieces
+    )
+
+    inner = ffn_in.shape[1]
+    ffn_x, ffn_xo = over_batch(ffn_send_here), over_batch(ffn_send_there)
+    in_z = across(in_send, 4)
+    glu_send, ffn_x, ffn_xo = lax.optimization_barrier((glu_send, ffn_x, ffn_xo))
+    glu_x = over_batch(glu_send)
+    every = slice(None)
+    values = [ffn_here, ffn_x, across(ffn_there), across(ffn_xo)] + ups
+    spans = [[(i, every), (i + 4, every)] for i in range(4)]
+    keep_out, send_out = products(place, values, spans, inner // 4, features, pieces // 2)
     back = by_channel(turned)
+    lags, send_out = lax.optimization_barrier((lags, send_out))
     shares = jnp.sum(back[:, channels:], axis=0)
-    back, send_out = lax.optimization_barrier((back, send_out))
-    out = Halving(keep_out, across(send_out, 2), mine)
+    out = Halving(keep_out, across(send_out, 2), mine, [4] + high_bits)
     grad_rows, sums, firsts, lagsum, bias_part = recurrence_back(
         recv, back.reshape(pieces * (channels + 8), rows), enter, lags, lam, weight, skip,
         pieces, docs, BACKWARD_UNROLL,
     )
-    (grad_rows,) = tied([out], grad_rows)
-    out.step()
-    grad_normed = by_channel(grad_rows.reshape(pieces, channels, rows)).reshape(features, rows)
-    acts_c, acts_cx = across(acts[1]), across(acts_x[1])
-    glu_own, out.keep = lax.optimization_barrier((glu_parts[0], out.keep))
-    rights = [glu_own, glu_x, across(glu_parts[0]), across(glu_x)]
-    lefts = [acts[0, 0], acts_x[0, 0], acts_c[0], acts_cx[0]]
-    keep_glu, send_glu = products(place, lefts, rights, pieces // 2)
-    rights = [pre_parts[0], pre_x, across(pre_parts[0]), across(pre_x)]
-    lefts = [acts[0, 1], acts_x[0, 1], acts_c[1], acts_cx[1]]
-    chunk_in = products(place, lefts, rights, pieces // 2, 2)
-    glu = Halving(keep_glu, across(send_glu, 2), mine)
-    chunk_in = tied([out], *chunk_in)
-    out.step()
-    first, second = (
-        Halving(keep, across(sent, 2), mine) for keep, sent in (chunk_in[:2], chunk_in[2:])
-    )
-
     vectors = jnp.concatenate([lagsum[:, LANES - 1], jnp.sum(bias_part, axis=1)]).reshape(1, -1)
     vectors = jnp.pad(vectors, ((0, 7), (0, LANES - vectors.shape[1])))
     vectors = jnp.concatenate([vectors, shares], axis=1)
     state = jnp.concatenate([jnp.concatenate([sums, firsts], axis=1), vectors], axis=0)
     state = summed(state, ("batch",))
-    state = by_channel(jnp.broadcast_to(state[None], (pieces,) + state.shape))
-    glu.step()
-    (grad_normed, ffn_low) = tied([first], grad_normed, ffn_low)
-    first.step()
-    ffn_res = jnp.dot(ffn_low, ffn_out, preferred_element_type=F32) + ffn_out_bias
-    result = (hidden + ffn_res).astype(BF16).reshape(tokens.shape)
-    grad_tokens = last_norm(grad_normed, flat, line(norm1_gain), grad_hidden).reshape(tokens.shape)
+    in_c = across(in_keep)
+    grad_rows, glu_x, in_z, in_c, state, tables, around = tied(
+        [out], grad_rows, glu_x, in_z, in_c, state, tables, around
+    )
+    out.step()
+    grad_normed = by_channel(grad_rows.reshape(pieces, channels, rows)).reshape(features, rows)
+    in_keep, out.keep = lax.optimization_barrier((in_keep, out.keep))
+    quarter, half = features // 4, features // 2
+    values = [in_keep, in_z, in_c, across(in_z)]
+    low_half, high_half = slice(0, inner // 2), slice(inner // 2, inner)
+    here, there = slice(inner, inner + quarter), slice(inner + quarter, inner + half)
+    spans = [[(i, here if i < 2 else there), (i, low_half), (i, high_half)] for i in range(4)]
+    keep_a, send_a, keep_b, send_b = products(
+        place, values, spans, quarter, inner, pieces // 4, 2, by_batch=True
+    )
+    first = Halving(keep_a, over_batch(send_a), mine, [2] + high_bits)
+    second = Halving(keep_b, over_batch(send_b), mine, [2] + high_bits)
+    glu_own = glu_keep
+    values = [glu_own, glu_x, across(glu_keep), across(glu_x)]
+    here, there = slice(features, features + half), slice(features + half, 2 * features)
+    spans = [[(i, here if i < 2 else there), (i, slice(0, features))] for i in range(4)]
+    keep_glu, send_glu = products(place, values, spans, half, features, pieces // 2)
+    (state,) = tied([out], state)
+    out.step()
+    glu = Halving(keep_glu, across(send_glu, 2), mine, [4] + high_bits)
 
     def all_batches(value):
         bit = 2
@@ -864,50 +1045,45 @@
             bit *= 2
         return value, over_batch(value)
 
-    def joined(value, other, axis):
-        pick = batch_bit == 0
-        return jnp.concatenate(
-            [jnp.where(pick, value, other), jnp.where(pick, other, value)], axis=axis
-        )
-
-    tied([second, glu])
+    groups = [[2 * i + c for i in range(pieces // 2)] for c in range(2)]
+    state = jnp.broadcast_to(state[None], (pieces // 2,) + state.shape)
+    state = lax.all_to_all(state, "seq", 0, 0, axis_index_groups=groups)
+
+    grad_normed, ffn_low = tied([first], grad_normed, ffn_low)
+    first.step()
+    ffn_res = jnp.dot(ffn_low, ffn_out, preferred_element_type=F32) + ffn_out_bias
+    result = (hidden + ffn_res).astype(BF16).reshape(tokens.shape)
+    grad_tokens = last_norm(grad_normed, flat, line(norm1_gain), grad_hidden).reshape(tokens.shape)
+    (first.keep,) = tied([glu], first.keep)
+    glu.step()
+
+    state, result, grad_tokens = tied([second, first, out, glu], state, result, grad_tokens)
+    state_c = across(state)
     second.step()
-    glu.step()
-    tied([first, out])
     first.step()
     half_out, other_out = all_batches(out.finish())
-    (state, other_out) = tied([second, glu], state, other_out)
+    glu.step()
+
+    lengths = (ffn_in.shape[1], 2 * features, features, features, features)
+    small = pulled(
+        place, state, state_c, tables, line(norm1_gain), line(norm1_bias), line(skip_gain), *around, lengths
+    )
+    other_out, *small = tied([second, glu, first], other_out, *small)
+    grad_params = small[:6]
+    vectors = [value.reshape(-1) for value in small[6:]]
+    grad_step, grad_skip, grad_gain1, grad_bias1 = vectors[:4]
+    bias_in, bias_glu, grad_g2, grad_b2, bias_out = vectors[4:]
     second.step()
+    half_a, other_a = all_batches(first.finish())
     half_glu, other_glu = all_batches(glu.finish())
-    (other_glu,) = tied([second, first], other_glu)
-    half_in, other_in = all_batches(
-        jnp.concatenate([first.finish(), second.finish()], axis=1)
-    )
-    sum_out, sum_glu = joined(half_out, other_out, 0), joined(half_glu, other_glu, 1)
-    sum_in = joined(half_in, other_in, 1)
-    vectors, shares = state[:, channels, :LANES], state[:, channels:, LANES:]
-    grad_skip = vectors[:, :channels].reshape(features)
-    grad_bias1 = vectors[:, channels : 2 * channels].reshape(features)
-    state = state[:, :channels].reshape(features, 2 * LANES)
-    half = LANES // 2
-    m_re, m_im = state[:, :half], state[:, half:LANES]
-    f_re, f_im = state[:, LANES : LANES + half], state[:, LANES + half : 2 * LANES]
-    whole_parts, mode_pull = jax.vjp(lambda p: mode_parts(p)[0], params)
-    w_re, w_im = whole_parts[2], whole_parts[3]
-    grad_params = mode_pull(
-        (w_re * f_re - w_im * f_im, -(w_re * f_im + w_im * f_re), m_re, -m_im)
-    )[0]
-    grad_gain1 = (
-        jnp.sum(w_re * m_re - w_im * m_im, axis=1) + skip_gain * grad_skip - norm1_bias * grad_bias1
-    ) / norm1_gain
-    small, at = [], 0
-    for length in (ffn_in.shape[1], 2 * features, features, features, features):
-        count, wide = share_rows(length, pieces)
-        small.append(shares[:, at : at + count, :wide].reshape(length))
-        at += count
-    bias_in, bias_glu, grad_g2, grad_b2, bias_out = small
+
+    other_a, other_glu = tied([second], other_a, other_glu)
+    half_b, other_b = all_batches(second.finish())
+    sum_out = assembled(place, [half_out], [other_out], 0)
+    sum_glu = assembled(place, [half_glu], [other_glu], 1)
+    sum_in = assembled(place, [half_a, half_b], [other_a, other_b], 1)
     return (
-        result, grad_tokens, grad_gain1, grad_bias1, *grad_params, grad_skip,
+        result, grad_tokens, grad_gain1, grad_bias1, *grad_params, grad_step, grad_skip,
         sum_glu, bias_glu, grad_g2, grad_b2, sum_in, bias_in, sum_out, bias_out,
     )
 

time: 329 us -> 307 us (0.933)
  local copies, waits for them, and re-layouts: 52.3 us -> 28.3 us
  Pallas kernels: 73.4 us -> 96.5 us
  waiting for transfers between devices: 98.2 us -> 75.8 us
  other arithmetic: 37.9 us -> 46 us
  matrix products: 5.44 us -> 2.02 us
    all_to_all x5 -> x4, waiting for transfers between devices: 27.5 us -> 3.14 us  [by_channel(): return lax.all_to_all(value, 'seq', 0, 0)]
    pallas_call x4 -> x8, Pallas kernels: 26.6 us -> 43.3 us  [the longest x3 16.4 us: products(): pl.pallas_call(lambda *refs: product_kernel(spans, by_batch, *refs), in_s...]
    squeeze x11 -> x0, local copies, waits for them, and re-layouts: 15.1 us -> none  [the longest x4 6.03 us: on_device(): lefts = [acts[0, 0], acts_x[0, 0], acts_c[0], acts_cx[0]]]
    sub x0 -> x4, other arithmetic: none -> 11.9 us  [times_pair(): left[0] * right[0] - left[1] * right[1]]
    concatenate x2 -> x5, other arithmetic: 0.15 us -> 7.87 us  [packed(): return jnp.concatenate([real, imag], axis=1)]
    slice x6 -> x0, local copies, waits for them, and re-layouts: 6.64 us -> none  [the longest x3 3.99 us: on_device(): small.append(shares[:, at:at + count, :wide].reshape(length))]
    pallas_call x1, Pallas kernels: 7.8 us -> 14.3 us  [upward(): pl.pallas_call(lambda *refs: upward_kernel(pieces, *refs), in_specs=[SMEM...]
    add_any x3 -> x0, other arithmetic: 6.02 us -> none  [the longest x1 2.92 us: mode_parts(): prod_re = 2.0 * (output_re * bbar_re - output_im * bbar_im)]
  transfers between devices with their start and end apart: 36 -> 36, of which waited for: 12 -> 12; matrix products, arithmetic and copies ran while one was open for 22% -> 20% of each run, Pallas kernels for 19% -> 26%
where the time goes in v4:
time: 307 us; the launch traced here: 306 us
  Pallas kernels  96.5 us (31%)
  waiting for transfers between devices  75.8 us (25%)
  starting transfers between devices  55.6 us (18%)
  other arithmetic  46 us (15%)
  local copies, waits for them, and re-layouts  28.3 us (9%)
    ppermute x31, waiting for transfers between devices, flipped(): return lax.ppermute(value, axis, [(i, i ^ bit) for i in range(count)])  67.5 us
    ppermute x31, starting transfers between devices, flipped(): return lax.ppermute(value, axis, [(i, i ^ bit) for i in range(count)])  28.9 us
    unnamed x134, local copies, waits for them, and re-layouts  25.3 us
    pallas_call x1, Pallas kernels, recurrence_back(): pl.pallas_call(lambda *refs: backward_kernel(sizes, *refs), out_shape=(ja...  24.2 us
    all_to_all x4, starting transfers between devices, by_channel(): return lax.all_to_all(value, 'seq', 0, 0)  22.5 us
    pallas_call x3, Pallas kernels, products(): pl.pallas_call(lambda *refs: product_kernel(spans, by_batch, *refs), in_s...  16.4 us
    pallas_call x1, Pallas kernels, downward(): pl.pallas_call(downward_kernel, in_specs=[SMEM] + [VMEM] * 8 + [HBM] * 3,...  15.8 us
    pallas_call x1, Pallas kernels, upward(): pl.pallas_call(lambda *refs: upward_kernel(pieces, *refs), in_specs=[SMEM...  14.3 us
  transfers between devices with their start and end apart: 36, of which 12 were waited for; matrix products, arithmetic and copies ran while one was open for 20% of the time, Pallas kernels for 26%

profile of v4, /device:TPU:0, one launch (start us, length us, event | category | flops | bytes accessed | tf_op | source)
XLA Modules:
  0.0 305.6 jit_solution(18295424579522669010)
XLA Ops:
  8.9 6.0 %all-to-all-start = ((f32[16,72,128]{2,1,0:T(8,128)}), f32[16,72,128]{2,1,0:T(8,128)S(1)}, u32[]{:S(2)}, u32[]{:S(2)}) async-start(f32[16,72,128]{2,1,0:T(8,128)} %get-tuple-element.132), calls=%async_computation | async-start | bytes 1179648 | tf_op jit(solution)/shard_map/all_to_all | solution.py:959
  30.6 11.1 %recurrence.1 = (f32[1024,128]{1,0:T(8,128)}, f32[64,64,128]{2,1,0:T(8,128)S(1)}, f32[64,128]{1,0:T(8,128)S(1)}) custom-call(f32[1152,128]{1,0:T(8,128)S(1)} %bitcast.147, f32[64,128]{1,0:T(8,128)S(1)} %get-tuple-element.336.refs_1_.refs_4_, f32[64,128]{1,0:T(8,128)S(1)} %get-tuple-element.337.refs_2_.refs_5_, f32[64,128]{1,0:T(8,128)S(1)} %broadcast_in_dim.6.refs_3_.refs_6_), custom_call_target="tpu_custom_call" | custom-call | flops 16000000000 | tf_op jit(solution)/shard_map/recurrence/pallas_call | solution.py:374
  43.1 4.5 %all-to-all-start.1 = ((f32[16,64,128]{2,1,0:T(8,128)}), f32[16,64,128]{2,1,0:T(8,128)}, u32[]{:S(2)}, u32[]{:S(2)}) async-start(f32[16,64,128]{2,1,0:T(8,128)} %bitcast.9), calls=%async_computation.1 | async-start | bytes 1048576 | tf_op jit(solution)/shard_map/all_to_all | solution.py:959
  47.6 5.4 %subtract_negate_fusion = (f32[1024,64]{1,0:T(8,128)}, f32[1024,64]{1,0:T(8,128)}, f32[1024,64]{1,0:T(8,128)}, f32[1024,64]{1,0:T(8,128)}, f32[1024,64]{1,0:T(8,128)}) fusion(f32[1024,64]{1,0:T(8,128)} %get-tuple-element.328, f32[1024,64]{1,0:T(8,128)} %copy.112, f32[1024,64]{1,0:T(8,128)} %get-tuple-element.327, f32[1024,64]{1,0:T(8,128)} %copy.111, ...), kind=kLoop, calls=%fused_computation.34 | loop fusion | flops 1966080 | bytes 2363392 | tf_op jit(solution)/shard_map/neg | solution.py:925
  53.0 4.8 %multiply_subtract_fusion = (f32[1024,64]{1,0:T(8,128)}, f32[1024,64]{1,0:T(8,128)}, f32[1024,64]{1,0:T(8,128)}) fusion(f32[1024,64]{1,0:T(8,128)} %get-tuple-element.306, f32[1024,64]{1,0:T(8,128)} %get-tuple-element.305, f32[1024,64]{1,0:T(8,128)S(1)} %copy-done.45, f32[1024]{0:T(1024)S(1)} %exp.21, f32[1024,64]{1,0:T(8,128)} %copy.111), kind=kLoop, calls=%fused_computation.36 | loop fusion | flops 720896 | bytes 1839104 | tf_op jit(solution)/shard_map/sub | solution.py:898
  58.8 3.9 %multiply_subtract_fusion.4 = (f32[1024,64]{1,0:T(8,128)}, f32[1024,64]{1,0:T(8,128)}, f32[1024,64]{1,0:T(8,128)}, f32[1024,64]{1,0:T(8,128)}, f32[1024,64]{1,0:T(8,128)}, /*index=5*/f32[1024,64]{1,0:T(8,128)}) fusion(f32[1024,64]{1,0:T(8,128)} %get-tuple-element.308, f32[1024,64]{1,0:T(8,128)} %get-tuple-element.307, f32[1024,64]{1,0:T(8,128)} %copy-done.43, ...), kind=kLoop, calls=%fused_computation.45 | loop fusion | flops 1376256 | bytes 3670016 | tf_op jit(solution)/shard_map/sub | solution.py:898
  62.8 14.3 %upward.1 = (f32[2,128,512]{2,1,0:T(8,128)}, f32[2,2,128,256]{3,2,1,0:T(8,128)}, f32[128,1024]{1,0:T(8,128)}, f32[128,1024]{1,0:T(8,128)}, f32[128,1024]{1,0:T(8...) custom-call(s32[4]{0:T(128)} %pad_add_fusion.refs_0_.place_ref, ...), custom_call_target="tpu_custom_call" | custom-call | flops 14000000000 | tf_op jit(solution)/shard_map/upward/pallas_call | solution.py:701
  79.1 15.8 %downward.1 = (f32[128,4608]{1,0:T(8,128)}, f32[128,4608]{1,0:T(8,128)}, f32[128,2048]{1,0:T(8,128)}, f32[128,2048]{1,0:T(8,128)}, f32[128,1024]{1,0:T(8,128)}, /*index=5*/f32[16,72,128]{2,1,0:T(8,128)}) custom-call(s32[4]{0:T(128)} %pad_add_fusion.refs_0_.place_ref, bf16[128,1024]{1,0:T(8,128)(2,1)} %bitcast.149, ...), custom_call_target="tpu_custom_call" | custom-call | flops 17999998976 | tf_op jit(solution)/shard_map/downward/pallas_call | solution.py:722
  95.0 5.9 %all-to-all-start.2 = ((f32[16,72,128]{2,1,0:T(8,128)}), f32[16,72,128]{2,1,0:T(8,128)S(1)}, u32[]{:S(2)}, u32[]{:S(2)}) async-start(f32[16,72,128]{2,1,0:T(8,128)} %get-tuple-element.158), calls=%async_computation.2 | async-start | bytes 1179648 | tf_op jit(solution)/shard_map/all_to_all | solution.py:959
  111.2 4.5 %products.3 = (f32[4,128,1024]{2,1,0:T(8,128)S(1)}, f32[4,128,1024]{2,1,0:T(8,128)}) custom-call(s32[4]{0:T(128)S(1)} %copy-done.11, f32[128,1024]{1,0:T(8,128)S(1)} %copy-done.37, f32[128,1024]{1,0:T(8,128)S(1)} %copy-done.24, f32[128,1024]{1,0:T(8,128)S(1)} %collective-permute-done.5.refs_3_, f32[128,1024]{1,0:T(8,128)S(1)} %collective-permute-done.6.refs_4_, ...), custom_call_target="tpu_custom_call" | custom-call | flops 4000000000 | tf_op jit(solution)/shard_map/products/pallas_call | solution.py:749
  118.7 24.2 %recurrence_back.1 = (f32[1024,128]{1,0:T(8,128)}, f32[64,128]{1,0:T(8,128)S(1)}, f32[64,128]{1,0:T(8,128)S(1)}, f32[64,128]{1,0:T(8,128)S(1)}, f32[64,128]{1,0:T(8,128)S(1)}) custom-call(f32[1152,128]{1,0:T(8,128)S(1)} %bitcast.148, f32[1152,128]{1,0:T(8,128)S(1)} %bitcast.146, f32[64,64,128]{2,1,0:T(8,128)S(1)} %copy-done.40, ...), custom_call_target="tpu_custom_call" | custom-call | flops 30000001024 | tf_op jit(solution)/shard_map/recurrence_back/pallas_call | solution.py:393
  148.4 16.2 %collective-permute-done.9.refs_2_ = f32[128,4608]{1,0:T(8,128)} collective-permute-done((f32[128,4608]{1,0:T(8,128)}, f32[128,4608]{1,0:T(8,128)}, u32[]{:S(2)}, u32[]{:S(2)}) %collective-permute-start.9) | collective-permute-done | bytes 2359328 | tf_op jit(solution)/shard_map/ppermute | solution.py:846
  169.6 6.0 %all-to-all-start.3 = ((f32[16,64,128]{2,1,0:T(8,128)}), f32[16,64,128]{2,1,0:T(8,128)}, u32[]{:S(2)}, u32[]{:S(2)}) async-start(f32[16,64,128]{2,1,0:T(8,128)} %bitcast.19), calls=%async_computation.3 | async-start | bytes 1048576 | tf_op jit(solution)/shard_map/all_to_all | solution.py:959
  175.6 7.7 %products.4 = (f32[4,64,1024]{2,1,0:T(8,128)S(1)}, f32[4,64,1024]{2,1,0:T(8,128)}, f32[4,64,1024]{2,1,0:T(8,128)S(1)}, f32[4,64,1024]{2,1,0:T(8,128)}) custom-call(s32[4]{0:T(128)S(1)} %copy-done.11, f32[128,4608]{1,0:T(8,128)} %get-tuple-element.169.refs_1_, f32[128,4608]{1,0:T(8,128)} %collective-permute-done.9.refs_2_, ...), custom_call_target="tpu_custom_call" | custom-call | flops 4000000000 | tf_op jit(solution)/shard_map/products/pallas_call | solution.py:749
  184.1 4.2 %products.5 = (f32[4,64,1024]{2,1,0:T(8,128)S(1)}, f32[4,64,1024]{2,1,0:T(8,128)}) custom-call(s32[4]{0:T(128)S(1)} %copy-done.11, f32[128,2048]{1,0:T(8,128)S(1)} %copy-done.12, f32[128,2048]{1,0:T(8,128)} %collective-permute-done.8.refs_2_, f32[128,2048]{1,0:T(8,128)} %collective-permute-done.18.refs_3_, f32[128,2048]{1,0:T(8,128)} %collective-permute-done.19.refs_4_), custom_call_target="tpu_custom_call" | custom-call | flops 4000000000 | tf_op jit(solution)/shard_map/products/pallas_call | solution.py:749
  190.2 9.8 %collective-permute-done.16 = f32[2,128,1024]{2,1,0:T(8,128)} collective-permute-done((f32[2,128,1024]{2,1,0:T(8,128)}, f32[2,128,1024]{2,1,0:T(8,128)}, u32[]{:S(2)}, u32[]{:S(2)}) %collective-permute-start.16) | collective-permute-done | bytes 1048608 | tf_op jit(solution)/shard_map/ppermute | solution.py:846
  207.3 4.2 %all-to-all-start.4 = ((f32[8,72,256]{2,1,0:T(8,128)}), f32[8,72,256]{2,1,0:T(8,128)}, u32[]{:S(2)}, u32[]{:S(2)}) async-start(f32[8,72,256]{2,1,0:T(8,128)} %broadcast_in_dim.8), calls=%async_computation.4 | async-start | bytes 1179648 | tf_op jit(solution)/shard_map/all_to_all | solution.py:1050
  227.4 9.5 %collective-permute-done.17 = f32[1,128,1024]{2,1,0:T(8,128)} collective-permute-done((f32[1,128,1024]{2,1,0:T(8,128)}, f32[1,128,1024]{2,1,0:T(8,128)}, u32[]{:S(2)}, u32[]{:S(2)}) %collective-permute-start.17) | collective-permute-done | bytes 524320 | tf_op jit(solution)/shard_map/ppermute | solution.py:846
  236.9 5.2 %all-to-all-done.4.own_ref = f32[8,72,256]{2,1,0:T(8,128)} async-done(((f32[8,72,256]{2,1,0:T(8,128)}), f32[8,72,256]{2,1,0:T(8,128)}, u32[]{:S(2)}, u32[]{:S(2)}) %all-to-all-start.4) | async-done | bytes 589856 | tf_op jit(solution)/shard_map/all_to_all | solution.py:1050
  242.0 4.7 %collective-permute-done.21 = f32[2,64,1024]{2,1,0:T(8,128)} collective-permute-done((f32[2,64,1024]{2,1,0:T(8,128)}, f32[2,64,1024]{2,1,0:T(8,128)}, u32[]{:S(2)}, u32[]{:S(2)}) %collective-permute-start.21) | collective-permute-done | bytes 524320 | tf_op jit(solution)/shard_map/ppermute | solution.py:846
  258.4 6.0 %pulled.1 = (f32[1024,64]{1,0:T(8,128)S(1)}, f32[1024,64]{1,0:T(8,128)S(1)}, f32[1024,64]{1,0:T(8,128)S(1)}, f32[1024,64]{1,0:T(8,128)S(1)}, f32[1024,64]{1,0:T(...) custom-call(s32[4]{0:T(128)S(1)} %copy-done.11, ...), custom_call_target="tpu_custom_call" | custom-call | flops 4000000000 | tf_op jit(solution)/shard_map/pulled/pallas_call | solution.py:835
  264.4 7.2 %collective-permute-done.23 = f32[1,64,1024]{2,1,0:T(8,128)S(1)} collective-permute-done((f32[1,64,1024]{2,1,0:T(8,128)S(1)}, f32[1,64,1024]{2,1,0:T(8,128)S(1)}, u32[]{:S(2)}, u32[]{:S(2)}) %collective-permute-start.23) | collective-permute-done | bytes 262176 | tf_op jit(solution)/shard_map/ppermute | solution.py:846
  271.6 5.5 %collective-permute-done.24 = f32[1,64,1024]{2,1,0:T(8,128)S(1)} collective-permute-done((f32[1,64,1024]{2,1,0:T(8,128)S(1)}, f32[1,64,1024]{2,1,0:T(8,128)S(1)}, u32[]{:S(2)}, u32[]{:S(2)}) %collective-permute-start.24) | collective-permute-done | bytes 262176 | tf_op jit(solution)/shard_map/ppermute | solution.py:846
  280.6 10.7 %collective-permute-done.27 = f32[1,64,1024]{2,1,0:T(8,128)S(1)} collective-permute-done((f32[1,64,1024]{2,1,0:T(8,128)S(1)}, f32[1,64,1024]{2,1,0:T(8,128)S(1)}, u32[]{:S(2)}, u32[]{:S(2)}) %collective-permute-start.27) | collective-permute-done | bytes 262176 | tf_op jit(solution)/shard_map/ppermute | solution.py:846
  (244 shorter events, 106.9 us)
Async XLA Ops:
  5.9 51.9 %collective-permute-start = (f32[128,1024]{1,0:T(8,128)S(1)}, f32[128,1024]{1,0:T(8,128)S(1)}, u32[]{:S(2)}, u32[]{:S(2)}) collective-permute-start(f32[128,1024]{1,0:T(8,128)S(1)} %get-tuple-element.150.refs_5_), channel_id=1, source_target_pairs={{0,16},{16,0},{1,17},{17,1},{2,18},{18,2},{3,19},{19,3},{4,20},{20... | collective-permute-start | bytes 1572872 | tf_op jit(solution)/shard_map/ppermute | solution.py:846
  8.9 53.8 %collective-permute-start.1 = (f32[128,1024]{1,0:T(8,128)S(1)}, f32[128,1024]{1,0:T(8,128)S(1)}, u32[]{:S(2)}, u32[]{:S(2)}) collective-permute-start(f32[128,1024]{1,0:T(8,128)S(1)} %get-tuple-element.150.refs_5_), channel_id=1, source_target_pairs={{0,1},{1,0},{2,3},{3,2},{4,5},{5,4},{6,7},{7,6},{8,9},{9,8},{10,11... | collective-permute-start | bytes 1572872 | tf_op jit(solution)/shard_map/ppermute | solution.py:846
  8.9 21.6 %all-to-all-start = ((f32[16,72,128]{2,1,0:T(8,128)}), f32[16,72,128]{2,1,0:T(8,128)S(1)}, u32[]{:S(2)}, u32[]{:S(2)}) async-start(f32[16,72,128]{2,1,0:T(8,128)} %get-tuple-element.132), calls=%async_computation | async-start | bytes 1179648 | tf_op jit(solution)/shard_map/all_to_all | solution.py:959
  43.1 19.7 %all-to-all-start.1 = ((f32[16,64,128]{2,1,0:T(8,128)}), f32[16,64,128]{2,1,0:T(8,128)}, u32[]{:S(2)}, u32[]{:S(2)}) async-start(f32[16,64,128]{2,1,0:T(8,128)} %bitcast.9), calls=%async_computation.1 | async-start | bytes 1048576 | tf_op jit(solution)/shard_map/all_to_all | solution.py:959
  77.1 27.1 %collective-permute-start.3 = (f32[128,1024]{1,0:T(8,128)}, f32[128,1024]{1,0:T(8,128)S(1)}, u32[]{:S(2)}, u32[]{:S(2)}) collective-permute-start(f32[128,1024]{1,0:T(8,128)} %get-tuple-element.145), channel_id=1, source_target_pairs={{0,16},{16,0},{1,17},{17,1},{2,18},{18,2},{3,19},{19,3},{4,20},{20... | collective-permute-start | bytes 1572872 | tf_op jit(solution)/shard_map/ppermute | solution.py:846
  77.6 26.5 %collective-permute-start.4 = (f32[128,1024]{1,0:T(8,128)}, f32[128,1024]{1,0:T(8,128)}, u32[]{:S(2)}, u32[]{:S(2)}) collective-permute-start(f32[128,1024]{1,0:T(8,128)} %get-tuple-element.146), channel_id=1, source_target_pairs={{0,16},{16,0},{1,17},{17,1},{2,18},{18,2},{3,19},{19,3},{4,20},{20... | collective-permute-start | bytes 1572872 | tf_op jit(solution)/shard_map/ppermute | solution.py:846
  95.0 22.1 %all-to-all-start.2 = ((f32[16,72,128]{2,1,0:T(8,128)}), f32[16,72,128]{2,1,0:T(8,128)S(1)}, u32[]{:S(2)}, u32[]{:S(2)}) async-start(f32[16,72,128]{2,1,0:T(8,128)} %get-tuple-element.158), calls=%async_computation.2 | async-start | bytes 1179648 | tf_op jit(solution)/shard_map/all_to_all | solution.py:959
  108.6 56.0 %collective-permute-start.9 = (f32[128,4608]{1,0:T(8,128)}, f32[128,4608]{1,0:T(8,128)}, u32[]{:S(2)}, u32[]{:S(2)}) collective-permute-start(f32[128,4608]{1,0:T(8,128)} %get-tuple-element.163), channel_id=1, source_target_pairs={{0,4},{1,5},{2,6},{3,7},{4,0},{5,1},{6,2},{7,3},{8,12},{9,13},{10,... | collective-permute-start | bytes 7077896 | tf_op jit(solution)/shard_map/ppermute | solution.py:846
  110.5 54.1 %collective-permute-start.10 = (f32[128,4608]{1,0:T(8,128)}, f32[128,4608]{1,0:T(8,128)}, u32[]{:S(2)}, u32[]{:S(2)}) collective-permute-start(f32[128,4608]{1,0:T(8,128)} %get-tuple-element.169.refs_1_), channel_id=1, source_target_pairs={{0,1},{1,0},{2,3},{3,2},{4,5},{5,4},{6,7},{7,6},{8,9},{9,8},{10,11... | collective-permute-start | bytes 7077896 | tf_op jit(solution)/shard_map/ppermute | solution.py:846
  110.5 37.8 %collective-permute-start.8 = (f32[128,2048]{1,0:T(8,128)}, f32[128,2048]{1,0:T(8,128)}, u32[]{:S(2)}, u32[]{:S(2)}) collective-permute-start(f32[128,2048]{1,0:T(8,128)} %get-tuple-element.162), channel_id=1, source_target_pairs={{0,16},{16,0},{1,17},{17,1},{2,18},{18,2},{3,19},{19,3},{4,20},{20... | collective-permute-start | bytes 3145736 | tf_op jit(solution)/shard_map/ppermute | solution.py:846
  115.6 49.0 %collective-permute-start.7 = (f32[4,128,1024]{2,1,0:T(8,128)}, f32[4,128,1024]{2,1,0:T(8,128)}, u32[]{:S(2)}, u32[]{:S(2)}) collective-permute-start(f32[4,128,1024]{2,1,0:T(8,128)} %get-tuple-element.157), channel_id=1, source_target_pairs={{0,2},{1,3},{2,0},{3,1},{4,6},{5,7},{6,4},{7,5},{8,10},{9,11},{10,... | collective-permute-start | bytes 6291464 | tf_op jit(solution)/shard_map/ppermute | solution.py:846
  169.6 30.5 %collective-permute-start.16 = (f32[2,128,1024]{2,1,0:T(8,128)}, f32[2,128,1024]{2,1,0:T(8,128)}, u32[]{:S(2)}, u32[]{:S(2)}) collective-permute-start(f32[2,128,1024]{2,1,0:T(8,128)} %get-tuple-element.320), channel_id=1, source_target_pairs={{0,4},{1,5},{2,6},{3,7},{4,0},{5,1},{6,2},{7,3},{8,12},{9,13},{10,... | collective-permute-start | bytes 3145736 | tf_op jit(solution)/shard_map/ppermute | solution.py:846
  169.6 36.8 %all-to-all-start.3 = ((f32[16,64,128]{2,1,0:T(8,128)}), f32[16,64,128]{2,1,0:T(8,128)}, u32[]{:S(2)}, u32[]{:S(2)}) async-start(f32[16,64,128]{2,1,0:T(8,128)} %bitcast.19), calls=%async_computation.3 | async-start | bytes 1048576 | tf_op jit(solution)/shard_map/all_to_all | solution.py:959
  183.4 28.1 %collective-permute-start.14 = (f32[4,64,1024]{2,1,0:T(8,128)}, f32[4,64,1024]{2,1,0:T(8,128)}, u32[]{:S(2)}, u32[]{:S(2)}) collective-permute-start(f32[4,64,1024]{2,1,0:T(8,128)} %get-tuple-element.174), channel_id=1, source_target_pairs={{0,16},{16,0},{1,17},{17,1},{2,18},{18,2},{3,19},{19,3},{4,20},{20... | collective-permute-start | bytes 3145736 | tf_op jit(solution)/shard_map/ppermute | solution.py:846
  188.4 30.7 %collective-permute-start.20 = (f32[4,64,1024]{2,1,0:T(8,128)}, f32[4,64,1024]{2,1,0:T(8,128)}, u32[]{:S(2)}, u32[]{:S(2)}) collective-permute-start(f32[4,64,1024]{2,1,0:T(8,128)} %get-tuple-element.184), channel_id=1, source_target_pairs={{0,2},{1,3},{2,0},{3,1},{4,6},{5,7},{6,4},{7,5},{8,10},{9,11},{10,... | collective-permute-start | bytes 3145736 | tf_op jit(solution)/shard_map/ppermute | solution.py:846
  203.6 33.3 %collective-permute-start.17 = (f32[1,128,1024]{2,1,0:T(8,128)}, f32[1,128,1024]{2,1,0:T(8,128)}, u32[]{:S(2)}, u32[]{:S(2)}) collective-permute-start(f32[1,128,1024]{2,1,0:T(8,128)} %select_bitcast_fusion.5), channel_id=1, source_target_pairs={{0,8},{1,9},{2,10},{3,11},{4,12},{5,13},{6,14},{7,15},{8,0},{9,1},... | collective-permute-start | bytes 1572872 | tf_op jit(solution)/shard_map/ppermute | solution.py:846
  205.4 36.6 %collective-permute-start.13 = (f32[4,64,1024]{2,1,0:T(8,128)}, f32[4,64,1024]{2,1,0:T(8,128)}, u32[]{:S(2)}, u32[]{:S(2)}) collective-permute-start(f32[4,64,1024]{2,1,0:T(8,128)} %get-tuple-element.172), channel_id=1, source_target_pairs={{0,16},{16,0},{1,17},{17,1},{2,18},{18,2},{3,19},{19,3},{4,20},{20... | collective-permute-start | bytes 3145736 | tf_op jit(solution)/shard_map/ppermute | solution.py:846
  207.3 34.7 %all-to-all-start.4 = ((f32[8,72,256]{2,1,0:T(8,128)}), f32[8,72,256]{2,1,0:T(8,128)}, u32[]{:S(2)}, u32[]{:S(2)}) async-start(f32[8,72,256]{2,1,0:T(8,128)} %broadcast_in_dim.8), calls=%async_computation.4 | async-start | bytes 1179648 | tf_op jit(solution)/shard_map/all_to_all | solution.py:1050
  213.9 28.1 %collective-permute-start.15 = (f32[2,64,1024]{2,1,0:T(8,128)}, f32[2,64,1024]{2,1,0:T(8,128)}, u32[]{:S(2)}, u32[]{:S(2)}) collective-permute-start(f32[2,64,1024]{2,1,0:T(8,128)} %get-tuple-element.330), channel_id=1, source_target_pairs={{0,2},{1,3},{2,0},{3,1},{4,6},{5,7},{6,4},{7,5},{8,10},{9,11},{10,... | collective-permute-start | bytes 1572872 | tf_op jit(solution)/shard_map/ppermute | solution.py:846
  221.5 25.3 %collective-permute-start.21 = (f32[2,64,1024]{2,1,0:T(8,128)}, f32[2,64,1024]{2,1,0:T(8,128)}, u32[]{:S(2)}, u32[]{:S(2)}) collective-permute-start(f32[2,64,1024]{2,1,0:T(8,128)} %select_bitcast_fusion.3), channel_id=1, source_target_pairs={{0,4},{1,5},{2,6},{3,7},{4,0},{5,1},{6,2},{7,3},{8,12},{9,13},{10,... | collective-permute-start | bytes 1572872 | tf_op jit(solution)/shard_map/ppermute | solution.py:846
  248.2 28.9 %collective-permute-start.22 = (f32[2,64,1024]{2,1,0:T(8,128)S(1)}, f32[2,64,1024]{2,1,0:T(8,128)S(1)}, u32[]{:S(2)}, u32[]{:S(2)}) collective-permute-start(f32[2,64,1024]{2,1,0:T(8,128)S(1)} %select_bitcast_fusion.2), channel_id=1, source_target_pairs={{0,2},{1,3},{2,0},{3,1},{4,6},{5,7},{6,4},{7,5},{8,10},{9,11},{10,... | collective-permute-start | bytes 1572872 | tf_op jit(solution)/shard_map/ppermute | solution.py:846
  252.4 19.2 %collective-permute-start.23 = (f32[1,64,1024]{2,1,0:T(8,128)S(1)}, f32[1,64,1024]{2,1,0:T(8,128)S(1)}, u32[]{:S(2)}, u32[]{:S(2)}) collective-permute-start(f32[1,64,1024]{2,1,0:T(8,128)S(1)} %select_bitcast_fusion.9), channel_id=1, source_target_pairs={{0,8},{1,9},{2,10},{3,11},{4,12},{5,13},{6,14},{7,15},{8,0},{9,1},... | collective-permute-start | bytes 786440 | tf_op jit(solution)/shard_map/ppermute | solution.py:846
  254.6 22.5 %collective-permute-start.25 = (f32[128,1024]{1,0:T(8,128)S(1)}, f32[128,1024]{1,0:T(8,128)S(1)}, u32[]{:S(2)}, u32[]{:S(2)}) collective-permute-start(f32[128,1024]{1,0:T(8,128)S(1)} %fusion.3.refs_0_), channel_id=1, source_target_pairs={{0,16},{16,0},{1,17},{17,1},{2,18},{18,2},{3,19},{19,3},{4,20},{20... | collective-permute-start | bytes 1572872 | tf_op jit(solution)/shard_map/ppermute | solution.py:846
  256.5 20.6 %collective-permute-start.24 = (f32[1,64,1024]{2,1,0:T(8,128)S(1)}, f32[1,64,1024]{2,1,0:T(8,128)S(1)}, u32[]{:S(2)}, u32[]{:S(2)}) collective-permute-start(f32[1,64,1024]{2,1,0:T(8,128)S(1)} %select_bitcast_fusion.8), channel_id=1, source_target_pairs={{0,8},{1,9},{2,10},{3,11},{4,12},{5,13},{6,14},{7,15},{8,0},{9,1},... | collective-permute-start | bytes 786440 | tf_op jit(solution)/shard_map/ppermute | solution.py:846
  (73 other events, 441.6 us)

commit v5 on v4

--- a/solution.py
+++ b/solution.py
@@ -477,15 +477,26 @@
     out_ref[...] = (hidden_ref[...] + norm_back(grad, unit, recip)).astype(BF16)
 
 
-def fetch(source, target, sems, chunks, rows):
+def pieces_of(source, target, sems, chunks, rows):
     out = []
     wide = source.shape[0 if rows else 1] // chunks
     for i in range(chunks):
         part = (pl.ds(i * wide, wide), slice(None)) if rows else (slice(None), pl.ds(i * wide, wide))
-        copy = pltpu.make_async_copy(source.at[part], target.at[part], sems.at[i])
-        copy.start()
-        out.append(copy)
+        out.append(pltpu.make_async_copy(source.at[part], target.at[part], sems.at[i]))
     return out
+
+
+class Sender:
+    def __init__(self, sems):
+        self.sems, self.copies = sems, []
+
+    def send(self, source, target):
+        self.copies.append(pltpu.make_async_copy(source, target, self.sems.at[len(self.copies)]))
+        self.copies[-1].start()
+
+    def finish(self):
+        for copy in self.copies:
+            copy.wait()
 
 
 def by_core(values, place_ref, out_ref, pieces):
@@ -507,57 +518,63 @@
 
 def upward_kernel(
     pieces, place_ref, mixed_ref, tokens_ref, glu_bias_ref, gain_ref, bias_ref, ffn_bias_ref, glu_ref, ffn_ref,
-    act_ref, z2_ref, keep_here_ref, keep_there_ref, send_here_ref, send_there_ref, pre_ref, hidden_ref, slope1_ref, slope2_ref, low_ref,
-    glu_v, ffn_v, parts_ref, glu_sem, ffn_sem, out_sem,
+    act_ref, z2_ref, keep_here_ref, keep_there_ref, send_here_ref, send_there_ref, pre_ref, hidden_ref,
+    slope1_ref, slope2_ref, low_ref,
+    glu_v, ffn_v, parts_v, act_v, z2_v, pre_v, hidden_v, slope1_v, slope2_v, low_v, glu_sem, ffn_sem, out_sem,
 ):
     rows, features = tokens_ref.shape
-    glu_copies = fetch(glu_ref, glu_v, glu_sem, 4, False)
-    ffn_copies = fetch(ffn_ref, ffn_v, ffn_sem, 8, False)
+    glu_copies = pieces_of(glu_ref, glu_v, glu_sem, 4, False)
+    ffn_copies = pieces_of(ffn_ref, ffn_v, ffn_sem, 8, False)
+    for copy in glu_copies + ffn_copies[:2]:
+        copy.start()
+    sender = Sender(out_sem)
     mixed = mixed_ref[...].T
     share, steep = bell(mixed)
-    slope1_ref[...] = share + steep
+    slope1_v[...] = share + steep
+    sender.send(slope1_v, slope1_ref)
     act = (mixed * share).astype(BF16)
-    by_core(act.astype(F32), place_ref, act_ref, pieces)
+    by_core(act.astype(F32), place_ref, act_v, pieces)
+    sender.send(act_v, act_ref)
     wide = glu_ref.shape[1] // 4
     for i in range(4):
         glu_copies[i].wait()
+        ffn_copies[i + 2].start()
         at = slice(i * wide, (i + 1) * wide)
-        pre_ref[:, at] = (
-            jnp.dot(act, glu_v[:, at], preferred_element_type=F32) + glu_bias_ref[:, at]
-        )
-    hidden = tokens_ref[...].astype(F32) + pre_ref[:, :features] * jax.nn.sigmoid(pre_ref[:, features:])
-    hidden_ref[...] = hidden
+        pre_v[:, at] = jnp.dot(act, glu_v[:, at], preferred_element_type=F32) + glu_bias_ref[:, at]
+    sender.send(pre_v, pre_ref)
+    hidden = tokens_ref[...].astype(F32) + pre_v[:, :features] * jax.nn.sigmoid(pre_v[:, features:])
+    hidden_v[...] = hidden
+    sender.send(hidden_v, hidden_ref)
     unit, _ = normalize(hidden)
     normed = (unit * gain_ref[...] + bias_ref[...]).astype(BF16)
-    by_pair(normed.astype(F32), place_ref, z2_ref, pieces)
+    by_pair(normed.astype(F32), place_ref, z2_v, pieces)
+    sender.send(z2_v, z2_ref)
     wide = ffn_ref.shape[1] // 8
     block = ffn_ref.shape[1] // pieces // 2
     for i in range(8):
         ffn_copies[i].wait()
+        if 6 <= i + 6 < 8:
+            ffn_copies[i + 6].start()
         at = slice(i * wide, (i + 1) * wide)
         ffn_pre = jnp.dot(normed, ffn_v[:, at], preferred_element_type=F32) + ffn_bias_ref[:, at]
         share, steep = bell(ffn_pre)
-        slope2_ref[:, at] = share + steep
+        slope2_v[:, at] = share + steep
         low = (ffn_pre * share).astype(BF16)
-        low_ref[:, at] = low
+        low_v[:, at] = low
+        columns = pl.ds(i * wide, wide)
+        sender.send(slope2_v.at[:, columns], slope2_ref.at[:, columns])
+        sender.send(low_v.at[:, columns], low_ref.at[:, columns])
         wider = low.astype(F32)
         for k in range(wide // block):
             index = (i * wide) // block + k
             piece, half = index // 2, index % 2
-            parts_ref[
+            parts_v[
                 half ^ place_ref[1], (piece % 2) ^ place_ref[0], :,
                 (piece // 2) * block : (piece // 2 + 1) * block,
             ] = wider[:, k * block : (k + 1) * block]
-    copies = []
     for k, ref in enumerate((keep_here_ref, keep_there_ref, send_here_ref, send_there_ref)):
-        copies.append(pltpu.make_async_copy(parts_ref.at[k // 2, k % 2], ref, out_sem.at[k]))
-        copies[-1].start()
-    for copy in copies:
-        copy.wait()
-
-
-def store(ref, columns, value):
-    ref[:, columns] = value
+        sender.send(parts_v.at[k // 2, k % 2], ref)
+    sender.finish()
 
 
 def downward_kernel(
@@ -565,28 +582,35 @@
     out_w_ref, in_w_ref, glu_w_ref,
     in_keep_ref, in_send_ref, glu_keep_ref, glu_send_ref, grad_hidden_ref, turned_ref,
     in_sum_ref, glu_sum_ref, gain_sum_ref, bias_sum_ref, out_sum_ref,
-    out_v, in_v, glu_v, parts_ref, out_sem, in_sem, glu_sem, keep_sem, send_sem,
+    out_v, in_v, glu_v, slope2_v, hidden_v, pre_v, slope1_v, parts_v, halves_v, grad_v,
+    out_sem, in_sem, slope_sem, one_sem, send_sem, half_sem,
 ):
     rows, features = cot_ref.shape
     inner = out_w_ref.shape[0]
     wide = inner // 8
-    out_copies = fetch(out_w_ref, out_v, out_sem, 8, True)
-    in_copies = fetch(in_w_ref, in_v, in_sem, 8, False)
-    glu_copies = fetch(glu_w_ref, glu_v, glu_sem, 1, False)
-    copies = []
-
-    def pass_on(source, target, sem):
-        copies.append(pltpu.make_async_copy(source, target, sem))
-        copies[-1].start()
-
+    out_copies = pieces_of(out_w_ref, out_v, out_sem, 8, True)
+    in_copies = pieces_of(in_w_ref, in_v, in_sem, 8, False)
+    slope_copies = pieces_of(slope2_ref, slope2_v, slope_sem, 8, False)
+    late = [
+        pltpu.make_async_copy(source, target, one_sem.at[k])
+        for k, (source, target) in enumerate(
+            ((hidden_ref, hidden_v), (pre_ref, pre_v), (slope1_ref, slope1_v), (glu_w_ref, glu_v))
+        )
+    ]
+    ahead = 3
+    for i in range(ahead):
+        out_copies[i].start()
+        slope_copies[i].start()
+        in_copies[i].start()
+    sender = Sender(send_sem)
     quarter, half = features // 4, features // 2
     for k in range(2):
-        columns = slice(features + k * half, features + (k + 1) * half)
-        glu_keep_ref[:, columns] = act_ref[k]
-        glu_send_ref[:, columns] = act_ref[k]
+        columns = pl.ds(features + k * half, half)
+        sender.send(act_ref.at[k], glu_keep_ref.at[:, columns])
+        sender.send(act_ref.at[k], glu_send_ref.at[:, columns])
         columns = pl.ds(inner + k * quarter, quarter)
-        pass_on(z2_ref.at[0, k], in_keep_ref.at[:, columns], keep_sem.at[8 + k])
-        pass_on(z2_ref.at[1, k], in_send_ref.at[:, columns], send_sem.at[8 + k])
+        sender.send(z2_ref.at[0, k], in_keep_ref.at[:, columns])
+        sender.send(z2_ref.at[1, k], in_send_ref.at[:, columns])
     cot = cot_ref[...]
     up = cot.astype(F32)
     out_sum_ref[...] = jnp.sum(up, axis=0, keepdims=True)
@@ -594,44 +618,56 @@
     for i in range(8):
         at = slice(i * wide, (i + 1) * wide)
         out_copies[i].wait()
-        grad = lax.dot_general(cot, out_v[at, :], NT, preferred_element_type=F32)
-        low = (grad * slope2_ref[:, at]).astype(BF16)
+        slope_copies[i].wait()
+        in_copies[i].wait()
+        if i + ahead < 8:
+            out_copies[i + ahead].start()
+            slope_copies[i + ahead].start()
+            in_copies[i + ahead].start()
+        elif i + ahead == 8:
+            for copy in late:
+                copy.start()
+        grad = dot(cot, out_v[at, :], NT)
+        low = (grad * slope2_v[:, at]).astype(BF16)
         wider = low.astype(F32)
         in_sum_ref[:, at] = jnp.sum(wider, axis=0, keepdims=True)
-        parts_ref[:, at] = wider
+        parts_v[:, at] = wider
         columns = pl.ds(i * wide, wide)
-        pass_on(parts_ref.at[:, columns], in_keep_ref.at[:, columns], keep_sem.at[i])
-        pass_on(parts_ref.at[:, columns], in_send_ref.at[:, columns], send_sem.at[i])
-        in_copies[i].wait()
-        total = total + lax.dot_general(low, in_v[:, at], NT, preferred_element_type=F32)
-    unit, recip = normalize(hidden_ref[...])
+        sender.send(parts_v.at[:, columns], in_keep_ref.at[:, columns])
+        sender.send(parts_v.at[:, columns], in_send_ref.at[:, columns])
+        total = total + dot(low, in_v[:, at], NT)
+    for copy in late:
+        copy.wait()
+    unit, recip = normalize(hidden_v[...])
     gain_sum_ref[...] = jnp.sum(total * unit, axis=0, keepdims=True)
     bias_sum_ref[...] = jnp.sum(total, axis=0, keepdims=True)
     grad_hidden = up + norm_back(total * gain_ref[...], unit, recip)
-    grad_hidden_ref[...] = grad_hidden
-    gate = jax.nn.sigmoid(pre_ref[:, features:])
+    grad_v[...] = grad_hidden
+    sender.send(grad_v, grad_hidden_ref)
+    gate = jax.nn.sigmoid(pre_v[:, features:])
     first = (grad_hidden * gate).astype(BF16)
-    second = (grad_hidden * pre_ref[:, :features] * (gate * (1.0 - gate))).astype(BF16)
-    glu_copies[0].wait()
+    second = (grad_hidden * pre_v[:, :features] * (gate * (1.0 - gate))).astype(BF16)
     grad_act = None
     for k, part in enumerate((first, second)):
         wider = part.astype(F32)
         at = slice(k * features, (k + 1) * features)
         glu_sum_ref[:, at] = jnp.sum(wider, axis=0, keepdims=True)
+        halves_v[k] = wider
         kept = k ^ place_ref[1] == 0
-        columns = slice(0, features)
-        pl.when(kept)(functools.partial(store, glu_keep_ref, columns, wider))
-        pl.when(jnp.logical_not(kept))(functools.partial(store, glu_send_ref, columns, wider))
-        term = lax.dot_general(part, glu_v[:, at], NT, preferred_element_type=F32)
+        for ref, chosen in ((glu_keep_ref, kept), (glu_send_ref, jnp.logical_not(kept))):
+            copy = pltpu.make_async_copy(halves_v.at[k], ref.at[:, pl.ds(0, features)], half_sem.at[k])
+            pl.when(chosen)(copy.start)
+        term = dot(part, glu_v[:, at], NT)
         grad_act = term if grad_act is None else grad_act + term
     turn = turning(rows)
-    high, low = halves(grad_act * slope1_ref[...])
+    high, low = halves(grad_act * slope1_v[...])
     sent_rows(dot(turn, high, NN) + dot(turn, low, NN), turned_ref, turned_ref.shape[1] - 8)
     share_vectors(
         (in_sum_ref, glu_sum_ref, gain_sum_ref, bias_sum_ref, out_sum_ref), turned_ref, turned_ref.shape[1] - 8
     )
-    for copy in copies:
-        copy.wait()
+    for k in range(2):
+        pltpu.make_async_copy(halves_v.at[k], glu_keep_ref.at[:, pl.ds(0, features)], half_sem.at[k]).wait()
+    sender.finish()
 
 
 def product_kernel(spans, by_batch, place_ref, *refs):
@@ -701,7 +737,7 @@
     return pl.pallas_call(
         lambda *refs: upward_kernel(pieces, *refs),
         in_specs=[SMEM] + [VMEM] * 6 + [HBM] * 2,
-        out_specs=(WHOLE, WHOLE) + (HBM,) * 4 + (WHOLE,) * 5,
+        out_specs=(HBM,) * 11,
         out_shape=(
             shaped(2, rows, features // 2), shaped(2, 2, rows, features // 4),
             *(shaped(rows, inner // 4),) * 4, shaped(rows, 2 * features),
@@ -709,8 +745,11 @@
         ),
         scratch_shapes=[
             pltpu.VMEM(glu_weight.shape, BF16), pltpu.VMEM(ffn_in.shape, BF16),
-            pltpu.VMEM((2, 2, rows, inner // 4), F32),
-            pltpu.SemaphoreType.DMA((4,)), pltpu.SemaphoreType.DMA((8,)), pltpu.SemaphoreType.DMA((4,)),
+            pltpu.VMEM((2, 2, rows, inner // 4), F32), pltpu.VMEM((2, rows, features // 2), F32),
+            pltpu.VMEM((2, 2, rows, features // 4), F32), pltpu.VMEM((rows, 2 * features), F32),
+            pltpu.VMEM((rows, features), F32), pltpu.VMEM((rows, features), F32),
+            pltpu.VMEM((rows, inner), F32), pltpu.VMEM((rows, inner), BF16),
+            pltpu.SemaphoreType.DMA((4,)), pltpu.SemaphoreType.DMA((8,)), pltpu.SemaphoreType.DMA((25,)),
         ],
         compiler_params=params_of(56), cost_estimate=estimate(14), name="upward",
     )(place, mixed, tokens, glu_bias, gain, bias, ffn_bias, glu_weight, ffn_in)
@@ -721,8 +760,8 @@
     inner = ffn_in.shape[1]
     return pl.pallas_call(
         downward_kernel,
-        in_specs=[SMEM] + [VMEM] * 8 + [HBM] * 3,
-        out_specs=(HBM, HBM) + (WHOLE,) * 4,
+        in_specs=[SMEM, VMEM] + [HBM] * 4 + [VMEM] * 3 + [HBM] * 3,
+        out_specs=(HBM,) * 5 + (WHOLE,),
         out_shape=(
             shaped(rows, inner + features // 2), shaped(rows, inner + features // 2),
             shaped(rows, 2 * features), shaped(rows, 2 * features),
@@ -733,9 +772,11 @@
             pltpu.VMEM((1, inner), F32), pltpu.VMEM((1, 2 * features), F32), pltpu.VMEM((1, features), F32),
             pltpu.VMEM((1, features), F32), pltpu.VMEM((1, features), F32),
             pltpu.VMEM(ffn_out.shape, BF16), pltpu.VMEM(ffn_in.shape, BF16), pltpu.VMEM(glu_weight.shape, BF16),
-            pltpu.VMEM((rows, inner), F32),
-            pltpu.SemaphoreType.DMA((8,)), pltpu.SemaphoreType.DMA((8,)), pltpu.SemaphoreType.DMA((1,)),
-            pltpu.SemaphoreType.DMA((10,)), pltpu.SemaphoreType.DMA((10,)),
+            pltpu.VMEM((rows, inner), F32), pltpu.VMEM((rows, features), F32),
+            pltpu.VMEM((rows, 2 * features), F32), pltpu.VMEM((rows, features), F32),
+            pltpu.VMEM((rows, inner), F32), pltpu.VMEM((2, rows, features), F32), pltpu.VMEM((rows, features), F32),
+            pltpu.SemaphoreType.DMA((8,)), pltpu.SemaphoreType.DMA((8,)), pltpu.SemaphoreType.DMA((8,)),
+            pltpu.SemaphoreType.DMA((4,)), pltpu.SemaphoreType.DMA((25,)), pltpu.SemaphoreType.DMA((2,)),
         ],
         compiler_params=params_of(56), cost_estimate=estimate(18), name="downward",
     )(place, cot, slope2, hidden, pre, slope1, gain, act, z2, ffn_out, ffn_in, glu_weight)
@@ -969,18 +1010,12 @@
     )
     recv = by_channel(send)
     _, _, tables, step_size, real_part = mode_tables(params)
-    tables = tuple(packed(*pair) for pair in tables)
-    around = (
-        jnp.broadcast_to(step_size, tables[0].shape),
-        packed(real_part, real_part),
-        packed(decay_freq, decay_freq),
-    )
     recv = recv.reshape(pieces * (channels + 8), rows)
     up_x = over_batch(up)
     ups = [up, up_x, across(up), across(up_x)]
     mixed_rows, enter, lags = recurrence(recv, lam, weight, skip, pieces, docs, FORWARD_UNROLL)
     mixed = by_channel(mixed_rows.reshape(pieces, channels, rows))
-    mixed, *ups = lax.optimization_barrier((mixed, *ups))
+    mixed, tables, *ups = lax.optimization_barrier((mixed, tables, *ups))
     mixed = mixed.reshape(features, rows)
     act_parts, z2_parts, ffn_here, ffn_there, ffn_send_here, ffn_send_there, glu_pre, hidden, slope1, slope2, ffn_low = upward(
         place, mixed, flat, line(glu_bias), line(norm2_gain), line(norm2_bias), line(ffn_in_bias),
@@ -1007,6 +1042,13 @@
         recv, back.reshape(pieces * (channels + 8), rows), enter, lags, lam, weight, skip,
         pieces, docs, BACKWARD_UNROLL,
     )
+    sums, tables, step_size, real_part = lax.optimization_barrier((sums, tables, step_size, real_part))
+    tables = tuple(packed(*pair) for pair in tables)
+    around = (
+        jnp.broadcast_to(step_size, tables[0].shape),
+        packed(real_part, real_part),
+        packed(decay_freq, decay_freq),
+    )
     vectors = jnp.concatenate([lagsum[:, LANES - 1], jnp.sum(bias_part, axis=1)]).reshape(1, -1)
     vectors = jnp.pad(vectors, ((0, 7), (0, LANES - vectors.shape[1])))
     vectors = jnp.concatenate([vectors, shares], axis=1)

time: 307 us -> 301 us (0.980)
  local copies, waits for them, and re-layouts: 28.3 us -> 35.5 us
  waiting for transfers between devices: 75.8 us -> 70.9 us
  Pallas kernels: 96.5 us -> 91.7 us
    unnamed x134 -> x154, local copies, waits for them, and re-layouts: 25.3 us -> 32.5 us
    sub x4 -> x3, other arithmetic: 11.9 us -> 4.77 us  [times_pair(): left[0] * right[0] - left[1] * right[1]]
    ppermute x31, waiting for transfers between devices: 67.5 us -> 61 us  [flipped(): return lax.ppermute(value, axis, [(i, i ^ bit) for i in range(count)])]
    add x2 -> x3, other arithmetic: 1.36 us -> 7.32 us  [times_pair(): left[0] * right[1] + left[1] * right[0]]
    pallas_call x1, Pallas kernels: 14.3 us -> 9.99 us  [upward(): pl.pallas_call(lambda *refs: upward_kernel(pieces, *refs), in_specs=[SMEM...]
    concatenate x5 -> x8, other arithmetic: 7.87 us -> 9.77 us  [packed(): return jnp.concatenate([real, imag], axis=1)]
where the time goes in v5:
time: 301 us; the launch traced here: 300 us
  Pallas kernels  91.7 us (30%)
  waiting for transfers between devices  70.9 us (24%)
  starting transfers between devices  53.7 us (18%)
  other arithmetic  44.4 us (15%)
  local copies, waits for them, and re-layouts  35.5 us (12%)
    ppermute x31, waiting for transfers between devices, flipped(): return lax.ppermute(value, axis, [(i, i ^ bit) for i in range(count)])  61 us
    unnamed x154, local copies, waits for them, and re-layouts  32.5 us
    ppermute x31, starting transfers between devices, flipped(): return lax.ppermute(value, axis, [(i, i ^ bit) for i in range(count)])  28.7 us
    pallas_call x1, Pallas kernels, recurrence_back(): pl.pallas_call(lambda *refs: backward_kernel(sizes, *refs), out_shape=(ja...  24.2 us
    all_to_all x4, starting transfers between devices, by_channel(): return lax.all_to_all(value, 'seq', 0, 0)  20.5 us
    pallas_call x3, Pallas kernels, products(): pl.pallas_call(lambda *refs: product_kernel(spans, by_batch, *refs), in_s...  16 us
    pallas_call x1, Pallas kernels, downward(): pl.pallas_call(downward_kernel, in_specs=[SMEM, VMEM] + [HBM] * 4 + [VMEM...  15.8 us
    pallas_call x1, Pallas kernels, recurrence(): pl.pallas_call(lambda *refs: forward_kernel(sizes, *refs), out_shape=(jax...  11.1 us
  transfers between devices with their start and end apart: 36, of which 12 were waited for; matrix products, arithmetic and copies ran while one was open for 20% of the time, Pallas kernels for 26%

profile of v5, /device:TPU:0, one launch (start us, length us, event | category | flops | bytes accessed | tf_op | source)
XLA Modules:
  0.0 299.6 jit_solution(16346181527807195219)
XLA Ops:
  8.9 5.9 %all-to-all-start = ((f32[16,72,128]{2,1,0:T(8,128)}), f32[16,72,128]{2,1,0:T(8,128)S(1)}, u32[]{:S(2)}, u32[]{:S(2)}) async-start(f32[16,72,128]{2,1,0:T(8,128)} %get-tuple-element.155), calls=%async_computation | async-start | bytes 1179648 | tf_op jit(solution)/shard_map/all_to_all | solution.py:1000
  26.9 3.8 %add_negate_fusion = (f32[1024,64]{1,0:T(8,128)}, f32[1024,64]{1,0:T(8,128)}, f32[1024,64]{1,0:T(8,128)}, f32[1024,64]{1,0:T(8,128)}, f32[1024,64]{1,0:T(8,128)}, /*index=5*/f32[1024,64]{1,0:T(8,128)}) fusion(f32[1024,64]{1,0:T(8,128)S(1)} %get-tuple-element.374, f32[1024,64]{1,0:T(8,128)S(1)} %copy-done.46, f32[1024,64]{1,0:T(8,128)S(1)} %get-tuple-element.373, ...), kind=kLoop, calls=%fused_computation.33 | loop fusion | flops 1966080 | bytes 2625536 | tf_op jit(solution)/shard_map/neg | solution.py:966
  30.8 11.1 %recurrence.1 = (f32[1024,128]{1,0:T(8,128)}, f32[64,64,128]{2,1,0:T(8,128)S(1)}, f32[64,128]{1,0:T(8,128)S(1)}) custom-call(f32[1152,128]{1,0:T(8,128)S(1)} %bitcast.149, f32[64,128]{1,0:T(8,128)S(1)} %get-tuple-element.382.refs_1_.refs_4_, f32[64,128]{1,0:T(8,128)S(1)} %get-tuple-element.383.refs_2_.refs_5_, f32[64,128]{1,0:T(8,128)S(1)} %broadcast_in_dim.10.refs_3_.refs_6_), custom_call_target="tpu_custom_call" | custom-call | flops 16000000000 | tf_op jit(solution)/shard_map/recurrence/pallas_call | solution.py:374
  43.3 6.1 %all-to-all-start.1 = ((f32[16,64,128]{2,1,0:T(8,128)}), f32[16,64,128]{2,1,0:T(8,128)}, u32[]{:S(2)}, u32[]{:S(2)}) async-start(f32[16,64,128]{2,1,0:T(8,128)} %bitcast.9), calls=%async_computation.1 | async-start | bytes 1048576 | tf_op jit(solution)/shard_map/all_to_all | solution.py:1000
  49.4 3.9 %multiply_add_fusion.4 = (f32[1024,64]{1,0:T(8,128)}, f32[1024,64]{1,0:T(8,128)}, f32[1024,64]{1,0:T(8,128)}, f32[1024,64]{1,0:T(8,128)}, f32[1024,64]{1,0:T(8,128)}, /*index=5*/f32[1024,64]{1,0:T(8,128)}) fusion(f32[1024,64]{1,0:T(8,128)} %get-tuple-element.353, f32[1024,64]{1,0:T(8,128)} %get-tuple-element.354, f32[1024,64]{1,0:T(8,128)S(1)} %copy.116, ...), kind=kLoop, calls=%fused_computation.44 | loop fusion | flops 1376256 | bytes 3670016 | tf_op jit(solution)/shard_map/add | solution.py:939
  63.9 10.0 %upward.1 = (f32[2,128,512]{2,1,0:T(8,128)}, f32[2,2,128,256]{3,2,1,0:T(8,128)}, f32[128,1024]{1,0:T(8,128)}, f32[128,1024]{1,0:T(8,128)}, f32[128,1024]{1,0:T(8...) custom-call(s32[4]{0:T(128)} %pad_add_fusion.refs_0_.place_ref, ...), custom_call_target="tpu_custom_call" | custom-call | flops 14000000000 | tf_op jit(solution)/shard_map/upward/pallas_call | solution.py:737
  76.0 15.8 %downward.1 = (f32[128,4608]{1,0:T(8,128)}, f32[128,4608]{1,0:T(8,128)}, f32[128,2048]{1,0:T(8,128)}, f32[128,2048]{1,0:T(8,128)}, f32[128,1024]{1,0:T(8,128)}, /*index=5*/f32[16,72,128]{2,1,0:T(8,128)}) custom-call(s32[4]{0:T(128)} %pad_add_fusion.refs_0_.place_ref, bf16[128,1024]{1,0:T(8,128)(2,1)} %bitcast.151, ...), custom_call_target="tpu_custom_call" | custom-call | flops 17999998976 | tf_op jit(solution)/shard_map/downward/pallas_call | solution.py:761
  91.8 4.1 %all-to-all-start.2 = ((f32[16,72,128]{2,1,0:T(8,128)}), f32[16,72,128]{2,1,0:T(8,128)S(1)}, u32[]{:S(2)}, u32[]{:S(2)}) async-start(f32[16,72,128]{2,1,0:T(8,128)} %get-tuple-element.181), calls=%async_computation.2 | async-start | bytes 1179648 | tf_op jit(solution)/shard_map/all_to_all | solution.py:1000
  109.1 4.5 %products.3 = (f32[4,128,1024]{2,1,0:T(8,128)S(1)}, f32[4,128,1024]{2,1,0:T(8,128)}) custom-call(s32[4]{0:T(128)S(1)} %copy-done.11, f32[128,1024]{1,0:T(8,128)S(1)} %copy-done.37, f32[128,1024]{1,0:T(8,128)S(1)} %copy-done.24, f32[128,1024]{1,0:T(8,128)S(1)} %collective-permute-done.5.refs_3_, f32[128,1024]{1,0:T(8,128)S(1)} %collective-permute-done.6.refs_4_, ...), custom_call_target="tpu_custom_call" | custom-call | flops 4000000000 | tf_op jit(solution)/shard_map/products/pallas_call | solution.py:790
  116.0 24.2 %recurrence_back.1 = (f32[1024,128]{1,0:T(8,128)}, f32[64,128]{1,0:T(8,128)S(1)}, f32[64,128]{1,0:T(8,128)S(1)}, f32[64,128]{1,0:T(8,128)S(1)}, f32[64,128]{1,0:T(8,128)S(1)}) custom-call(f32[1152,128]{1,0:T(8,128)S(1)} %bitcast.150, f32[1152,128]{1,0:T(8,128)S(1)} %bitcast.148, f32[64,64,128]{2,1,0:T(8,128)S(1)} %copy-done.40, ...), custom_call_target="tpu_custom_call" | custom-call | flops 30000001024 | tf_op jit(solution)/shard_map/recurrence_back/pallas_call | solution.py:393
  151.0 8.2 %collective-permute-done.9.refs_2_ = f32[128,4608]{1,0:T(8,128)} collective-permute-done((f32[128,4608]{1,0:T(8,128)}, f32[128,4608]{1,0:T(8,128)}, u32[]{:S(2)}, u32[]{:S(2)}) %collective-permute-start.9) | collective-permute-done | bytes 2359328 | tf_op jit(solution)/shard_map/ppermute | solution.py:887
  166.6 4.4 %all-to-all-start.3 = ((f32[16,64,128]{2,1,0:T(8,128)}), f32[16,64,128]{2,1,0:T(8,128)}, u32[]{:S(2)}, u32[]{:S(2)}) async-start(f32[16,64,128]{2,1,0:T(8,128)} %bitcast.21), calls=%async_computation.3 | async-start | bytes 1048576 | tf_op jit(solution)/shard_map/all_to_all | solution.py:1000
  172.8 7.0 %products.4 = (f32[4,64,1024]{2,1,0:T(8,128)S(1)}, f32[4,64,1024]{2,1,0:T(8,128)}, f32[4,64,1024]{2,1,0:T(8,128)S(1)}, f32[4,64,1024]{2,1,0:T(8,128)}) custom-call(s32[4]{0:T(128)S(1)} %copy-done.11, f32[128,4608]{1,0:T(8,128)S(1)} %copy-done.12, f32[128,4608]{1,0:T(8,128)} %collective-permute-done.9.refs_2_, f32[128,4608]{1,0:T(8,128)} %collective-permute-done.10.refs_3_, ...), custom_call_target="tpu_custom_call" | custom-call | flops 4000000000 | tf_op jit(solution)/shard_map/products/pallas_call | solution.py:790
  181.2 4.6 %products.5 = (f32[4,64,1024]{2,1,0:T(8,128)S(1)}, f32[4,64,1024]{2,1,0:T(8,128)}) custom-call(s32[4]{0:T(128)S(1)} %copy-done.11, f32[128,2048]{1,0:T(8,128)} %get-tuple-element.227.refs_1_, f32[128,2048]{1,0:T(8,128)} %collective-permute-done.8.refs_2_, f32[128,2048]{1,0:T(8,128)} %collective-permute-done.18.refs_3_, ...), custom_call_target="tpu_custom_call" | custom-call | flops 4000000000 | tf_op jit(solution)/shard_map/products/pallas_call | solution.py:790
  187.7 10.4 %collective-permute-done.16 = f32[2,128,1024]{2,1,0:T(8,128)} collective-permute-done((f32[2,128,1024]{2,1,0:T(8,128)}, f32[2,128,1024]{2,1,0:T(8,128)}, u32[]{:S(2)}, u32[]{:S(2)}) %collective-permute-start.16) | collective-permute-done | bytes 1048608 | tf_op jit(solution)/shard_map/ppermute | solution.py:887
  203.9 4.5 %all-to-all-start.4 = ((f32[8,72,256]{2,1,0:T(8,128)}), f32[8,72,256]{2,1,0:T(8,128)}, u32[]{:S(2)}, u32[]{:S(2)}) async-start(f32[8,72,256]{2,1,0:T(8,128)} %broadcast_in_dim.28), calls=%async_computation.4 | async-start | bytes 1179648 | tf_op jit(solution)/shard_map/all_to_all | solution.py:1092
  210.8 5.6 %collective-permute-done.20 = f32[4,64,1024]{2,1,0:T(8,128)} collective-permute-done((f32[4,64,1024]{2,1,0:T(8,128)}, f32[4,64,1024]{2,1,0:T(8,128)}, u32[]{:S(2)}, u32[]{:S(2)}) %collective-permute-start.20) | collective-permute-done | bytes 1048608 | tf_op jit(solution)/shard_map/ppermute | solution.py:887
  226.4 5.0 %collective-permute-done.17 = f32[1,128,1024]{2,1,0:T(8,128)} collective-permute-done((f32[1,128,1024]{2,1,0:T(8,128)}, f32[1,128,1024]{2,1,0:T(8,128)}, u32[]{:S(2)}, u32[]{:S(2)}) %collective-permute-start.17) | collective-permute-done | bytes 524320 | tf_op jit(solution)/shard_map/ppermute | solution.py:887
  231.4 6.4 %all-to-all-done.4.own_ref = f32[8,72,256]{2,1,0:T(8,128)} async-done(((f32[8,72,256]{2,1,0:T(8,128)}), f32[8,72,256]{2,1,0:T(8,128)}, u32[]{:S(2)}, u32[]{:S(2)}) %all-to-all-start.4) | async-done | bytes 589856 | tf_op jit(solution)/shard_map/all_to_all | solution.py:1092
  237.8 5.5 %collective-permute-done.21 = f32[2,64,1024]{2,1,0:T(8,128)} collective-permute-done((f32[2,64,1024]{2,1,0:T(8,128)}, f32[2,64,1024]{2,1,0:T(8,128)}, u32[]{:S(2)}, u32[]{:S(2)}) %collective-permute-start.21) | collective-permute-done | bytes 524320 | tf_op jit(solution)/shard_map/ppermute | solution.py:887
  254.4 6.0 %pulled.1 = (f32[1024,64]{1,0:T(8,128)S(1)}, f32[1024,64]{1,0:T(8,128)S(1)}, f32[1024,64]{1,0:T(8,128)S(1)}, f32[1024,64]{1,0:T(8,128)S(1)}, f32[1024,64]{1,0:T(...) custom-call(s32[4]{0:T(128)S(1)} %copy-done.11, ...), custom_call_target="tpu_custom_call" | custom-call | flops 4000000000 | tf_op jit(solution)/shard_map/pulled/pallas_call | solution.py:876
  260.3 4.0 %collective-permute-done.24 = f32[1,64,1024]{2,1,0:T(8,128)S(1)} collective-permute-done((f32[1,64,1024]{2,1,0:T(8,128)S(1)}, f32[1,64,1024]{2,1,0:T(8,128)S(1)}, u32[]{:S(2)}, u32[]{:S(2)}) %collective-permute-start.24) | collective-permute-done | bytes 262176 | tf_op jit(solution)/shard_map/ppermute | solution.py:887
  264.3 5.5 %collective-permute-done.23 = f32[1,64,1024]{2,1,0:T(8,128)S(1)} collective-permute-done((f32[1,64,1024]{2,1,0:T(8,128)S(1)}, f32[1,64,1024]{2,1,0:T(8,128)S(1)}, u32[]{:S(2)}, u32[]{:S(2)}) %collective-permute-start.23) | collective-permute-done | bytes 262176 | tf_op jit(solution)/shard_map/ppermute | solution.py:887
  272.7 11.7 %collective-permute-done.27 = f32[1,64,1024]{2,1,0:T(8,128)S(1)} collective-permute-done((f32[1,64,1024]{2,1,0:T(8,128)S(1)}, f32[1,64,1024]{2,1,0:T(8,128)S(1)}, u32[]{:S(2)}, u32[]{:S(2)}) %collective-permute-start.27) | collective-permute-done | bytes 262176 | tf_op jit(solution)/shard_map/ppermute | solution.py:887
  (267 shorter events, 120.2 us)
Async XLA Ops:
  5.9 54.4 %collective-permute-start.1 = (f32[128,1024]{1,0:T(8,128)S(1)}, f32[128,1024]{1,0:T(8,128)S(1)}, u32[]{:S(2)}, u32[]{:S(2)}) collective-permute-start(f32[128,1024]{1,0:T(8,128)S(1)} %get-tuple-element.173.refs_5_), channel_id=1, source_target_pairs={{0,1},{1,0},{2,3},{3,2},{4,5},{5,4},{6,7},{7,6},{8,9},{9,8},{10,11... | collective-permute-start | bytes 1572872 | tf_op jit(solution)/shard_map/ppermute | solution.py:887
  6.4 47.0 %collective-permute-start = (f32[128,1024]{1,0:T(8,128)S(1)}, f32[128,1024]{1,0:T(8,128)S(1)}, u32[]{:S(2)}, u32[]{:S(2)}) collective-permute-start(f32[128,1024]{1,0:T(8,128)S(1)} %get-tuple-element.173.refs_5_), channel_id=1, source_target_pairs={{0,16},{16,0},{1,17},{17,1},{2,18},{18,2},{3,19},{19,3},{4,20},{20... | collective-permute-start | bytes 1572872 | tf_op jit(solution)/shard_map/ppermute | solution.py:887
  8.9 21.8 %all-to-all-start = ((f32[16,72,128]{2,1,0:T(8,128)}), f32[16,72,128]{2,1,0:T(8,128)S(1)}, u32[]{:S(2)}, u32[]{:S(2)}) async-start(f32[16,72,128]{2,1,0:T(8,128)} %get-tuple-element.155), calls=%async_computation | async-start | bytes 1179648 | tf_op jit(solution)/shard_map/all_to_all | solution.py:1000
  43.3 20.6 %all-to-all-start.1 = ((f32[16,64,128]{2,1,0:T(8,128)}), f32[16,64,128]{2,1,0:T(8,128)}, u32[]{:S(2)}, u32[]{:S(2)}) async-start(f32[16,64,128]{2,1,0:T(8,128)} %bitcast.9), calls=%async_computation.1 | async-start | bytes 1048576 | tf_op jit(solution)/shard_map/all_to_all | solution.py:1000
  73.9 22.5 %collective-permute-start.3 = (f32[128,1024]{1,0:T(8,128)}, f32[128,1024]{1,0:T(8,128)S(1)}, u32[]{:S(2)}, u32[]{:S(2)}) collective-permute-start(f32[128,1024]{1,0:T(8,128)} %get-tuple-element.168), channel_id=1, source_target_pairs={{0,16},{16,0},{1,17},{17,1},{2,18},{18,2},{3,19},{19,3},{4,20},{20... | collective-permute-start | bytes 1572872 | tf_op jit(solution)/shard_map/ppermute | solution.py:887
  74.5 24.8 %collective-permute-start.4 = (f32[128,1024]{1,0:T(8,128)}, f32[128,1024]{1,0:T(8,128)S(1)}, u32[]{:S(2)}, u32[]{:S(2)}) collective-permute-start(f32[128,1024]{1,0:T(8,128)} %get-tuple-element.169), channel_id=1, source_target_pairs={{0,16},{16,0},{1,17},{17,1},{2,18},{18,2},{3,19},{19,3},{4,20},{20... | collective-permute-start | bytes 1572872 | tf_op jit(solution)/shard_map/ppermute | solution.py:887
  91.8 22.7 %all-to-all-start.2 = ((f32[16,72,128]{2,1,0:T(8,128)}), f32[16,72,128]{2,1,0:T(8,128)S(1)}, u32[]{:S(2)}, u32[]{:S(2)}) async-start(f32[16,72,128]{2,1,0:T(8,128)} %get-tuple-element.181), calls=%async_computation.2 | async-start | bytes 1179648 | tf_op jit(solution)/shard_map/all_to_all | solution.py:1000
  100.3 58.9 %collective-permute-start.9 = (f32[128,4608]{1,0:T(8,128)}, f32[128,4608]{1,0:T(8,128)}, u32[]{:S(2)}, u32[]{:S(2)}) collective-permute-start(f32[128,4608]{1,0:T(8,128)} %get-tuple-element.186), channel_id=1, source_target_pairs={{0,4},{1,5},{2,6},{3,7},{4,0},{5,1},{6,2},{7,3},{8,12},{9,13},{10,... | collective-permute-start | bytes 7077896 | tf_op jit(solution)/shard_map/ppermute | solution.py:887
  102.0 57.1 %collective-permute-start.10 = (f32[128,4608]{1,0:T(8,128)}, f32[128,4608]{1,0:T(8,128)}, u32[]{:S(2)}, u32[]{:S(2)}) collective-permute-start(f32[128,4608]{1,0:T(8,128)} %get-tuple-element.215.refs_1_), channel_id=1, source_target_pairs={{0,1},{1,0},{2,3},{3,2},{4,5},{5,4},{6,7},{7,6},{8,9},{9,8},{10,11... | collective-permute-start | bytes 7077896 | tf_op jit(solution)/shard_map/ppermute | solution.py:887
  102.2 48.7 %collective-permute-start.8 = (f32[128,2048]{1,0:T(8,128)}, f32[128,2048]{1,0:T(8,128)}, u32[]{:S(2)}, u32[]{:S(2)}) collective-permute-start(f32[128,2048]{1,0:T(8,128)} %get-tuple-element.185), channel_id=1, source_target_pairs={{0,16},{16,0},{1,17},{17,1},{2,18},{18,2},{3,19},{19,3},{4,20},{20... | collective-permute-start | bytes 3145736 | tf_op jit(solution)/shard_map/ppermute | solution.py:887
  113.5 47.9 %collective-permute-start.7 = (f32[4,128,1024]{2,1,0:T(8,128)}, f32[4,128,1024]{2,1,0:T(8,128)}, u32[]{:S(2)}, u32[]{:S(2)}) collective-permute-start(f32[4,128,1024]{2,1,0:T(8,128)} %get-tuple-element.180), channel_id=1, source_target_pairs={{0,2},{1,3},{2,0},{3,1},{4,6},{5,7},{6,4},{7,5},{8,10},{9,11},{10,... | collective-permute-start | bytes 6291464 | tf_op jit(solution)/shard_map/ppermute | solution.py:887
  162.4 18.8 %collective-permute-start.18 = (f32[128,2048]{1,0:T(8,128)}, f32[128,2048]{1,0:T(8,128)}, u32[]{:S(2)}, u32[]{:S(2)}) collective-permute-start(f32[128,2048]{1,0:T(8,128)} %get-tuple-element.227.refs_1_), channel_id=1, source_target_pairs={{0,1},{1,0},{2,3},{3,2},{4,5},{5,4},{6,7},{7,6},{8,9},{9,8},{10,11... | collective-permute-start | bytes 3145736 | tf_op jit(solution)/shard_map/ppermute | solution.py:887
  166.4 31.7 %collective-permute-start.16 = (f32[2,128,1024]{2,1,0:T(8,128)}, f32[2,128,1024]{2,1,0:T(8,128)}, u32[]{:S(2)}, u32[]{:S(2)}) collective-permute-start(f32[2,128,1024]{2,1,0:T(8,128)} %get-tuple-element.366), channel_id=1, source_target_pairs={{0,4},{1,5},{2,6},{3,7},{4,0},{5,1},{6,2},{7,3},{8,12},{9,13},{10,... | collective-permute-start | bytes 3145736 | tf_op jit(solution)/shard_map/ppermute | solution.py:887
  166.6 36.4 %all-to-all-start.3 = ((f32[16,64,128]{2,1,0:T(8,128)}), f32[16,64,128]{2,1,0:T(8,128)}, u32[]{:S(2)}, u32[]{:S(2)}) async-start(f32[16,64,128]{2,1,0:T(8,128)} %bitcast.21), calls=%async_computation.3 | async-start | bytes 1048576 | tf_op jit(solution)/shard_map/all_to_all | solution.py:1000
  179.7 28.7 %collective-permute-start.14 = (f32[4,64,1024]{2,1,0:T(8,128)}, f32[4,64,1024]{2,1,0:T(8,128)}, u32[]{:S(2)}, u32[]{:S(2)}) collective-permute-start(f32[4,64,1024]{2,1,0:T(8,128)} %get-tuple-element.220), channel_id=1, source_target_pairs={{0,16},{16,0},{1,17},{17,1},{2,18},{18,2},{3,19},{19,3},{4,20},{20... | collective-permute-start | bytes 3145736 | tf_op jit(solution)/shard_map/ppermute | solution.py:887
  185.8 30.6 %collective-permute-start.20 = (f32[4,64,1024]{2,1,0:T(8,128)}, f32[4,64,1024]{2,1,0:T(8,128)}, u32[]{:S(2)}, u32[]{:S(2)}) collective-permute-start(f32[4,64,1024]{2,1,0:T(8,128)} %get-tuple-element.230), channel_id=1, source_target_pairs={{0,2},{1,3},{2,0},{3,1},{4,6},{5,7},{6,4},{7,5},{8,10},{9,11},{10,... | collective-permute-start | bytes 3145736 | tf_op jit(solution)/shard_map/ppermute | solution.py:887
  201.6 29.8 %collective-permute-start.17 = (f32[1,128,1024]{2,1,0:T(8,128)}, f32[1,128,1024]{2,1,0:T(8,128)}, u32[]{:S(2)}, u32[]{:S(2)}) collective-permute-start(f32[1,128,1024]{2,1,0:T(8,128)} %select_bitcast_fusion.5), channel_id=1, source_target_pairs={{0,8},{1,9},{2,10},{3,11},{4,12},{5,13},{6,14},{7,15},{8,0},{9,1},... | collective-permute-start | bytes 1572872 | tf_op jit(solution)/shard_map/ppermute | solution.py:887
  201.6 36.2 %collective-permute-start.13 = (f32[4,64,1024]{2,1,0:T(8,128)}, f32[4,64,1024]{2,1,0:T(8,128)}, u32[]{:S(2)}, u32[]{:S(2)}) collective-permute-start(f32[4,64,1024]{2,1,0:T(8,128)} %get-tuple-element.218), channel_id=1, source_target_pairs={{0,16},{16,0},{1,17},{17,1},{2,18},{18,2},{3,19},{19,3},{4,20},{20... | collective-permute-start | bytes 3145736 | tf_op jit(solution)/shard_map/ppermute | solution.py:887
  203.9 33.9 %all-to-all-start.4 = ((f32[8,72,256]{2,1,0:T(8,128)}), f32[8,72,256]{2,1,0:T(8,128)}, u32[]{:S(2)}, u32[]{:S(2)}) async-start(f32[8,72,256]{2,1,0:T(8,128)} %broadcast_in_dim.28), calls=%async_computation.4 | async-start | bytes 1179648 | tf_op jit(solution)/shard_map/all_to_all | solution.py:1092
  218.8 24.4 %collective-permute-start.21 = (f32[2,64,1024]{2,1,0:T(8,128)}, f32[2,64,1024]{2,1,0:T(8,128)}, u32[]{:S(2)}, u32[]{:S(2)}) collective-permute-start(f32[2,64,1024]{2,1,0:T(8,128)} %select_bitcast_fusion.3), channel_id=1, source_target_pairs={{0,4},{1,5},{2,6},{3,7},{4,0},{5,1},{6,2},{7,3},{8,12},{9,13},{10,... | collective-permute-start | bytes 1572872 | tf_op jit(solution)/shard_map/ppermute | solution.py:887
  220.5 22.7 %collective-permute-start.15 = (f32[2,64,1024]{2,1,0:T(8,128)}, f32[2,64,1024]{2,1,0:T(8,128)}, u32[]{:S(2)}, u32[]{:S(2)}) collective-permute-start(f32[2,64,1024]{2,1,0:T(8,128)} %get-tuple-element.376), channel_id=1, source_target_pairs={{0,2},{1,3},{2,0},{3,1},{4,6},{5,7},{6,4},{7,5},{8,10},{9,11},{10,... | collective-permute-start | bytes 1572872 | tf_op jit(solution)/shard_map/ppermute | solution.py:887
  245.6 18.8 %collective-permute-start.24 = (f32[1,64,1024]{2,1,0:T(8,128)S(1)}, f32[1,64,1024]{2,1,0:T(8,128)S(1)}, u32[]{:S(2)}, u32[]{:S(2)}) collective-permute-start(f32[1,64,1024]{2,1,0:T(8,128)S(1)} %select_bitcast_fusion.8), channel_id=1, source_target_pairs={{0,8},{1,9},{2,10},{3,11},{4,12},{5,13},{6,14},{7,15},{8,0},{9,1},... | collective-permute-start | bytes 786440 | tf_op jit(solution)/shard_map/ppermute | solution.py:887
  247.4 22.5 %collective-permute-start.22 = (f32[2,64,1024]{2,1,0:T(8,128)S(1)}, f32[2,64,1024]{2,1,0:T(8,128)S(1)}, u32[]{:S(2)}, u32[]{:S(2)}) collective-permute-start(f32[2,64,1024]{2,1,0:T(8,128)S(1)} %select_bitcast_fusion.2), channel_id=1, source_target_pairs={{0,2},{1,3},{2,0},{3,1},{4,6},{5,7},{6,4},{7,5},{8,10},{9,11},{10,... | collective-permute-start | bytes 1572872 | tf_op jit(solution)/shard_map/ppermute | solution.py:887
  249.3 20.5 %collective-permute-start.25 = (f32[128,1024]{1,0:T(8,128)S(1)}, f32[128,1024]{1,0:T(8,128)S(1)}, u32[]{:S(2)}, u32[]{:S(2)}) collective-permute-start(f32[128,1024]{1,0:T(8,128)S(1)} %fusion.3.refs_0_), channel_id=1, source_target_pairs={{0,16},{16,0},{1,17},{17,1},{2,18},{18,2},{3,19},{19,3},{4,20},{20... | collective-permute-start | bytes 1572872 | tf_op jit(solution)/shard_map/ppermute | solution.py:887
  (83 other events, 592.0 us)

commit v6 on v5

--- a/solution.py
+++ b/solution.py
@@ -670,35 +670,38 @@
     sender.finish()
 
 
-def product_kernel(spans, by_batch, place_ref, *refs):
+def product_kernel(spans, place_ref, *refs):
     many = 1 + max(at for span in spans for at, _ in span)
-    values, outs, scratch_ref = refs[:many], refs[many:-1], refs[-1]
-    start = 0
-    for k in range(len(spans[0]) - 1):
-        total = None
-        for span in spans:
-            (left, rows), (right, columns) = span[0], span[k + 1]
-            term = dot(
-                values[left][:, rows].astype(BF16), values[right][:, columns].astype(BF16), TN
+    values, (keep_ref, send_ref) = refs[:many], refs[many : many + 2]
+    left_ref, right_ref, total_ref, in_sem, keep_sem, send_sem = refs[many + 2 :]
+    rows = values[0].shape[0]
+    copies = []
+    for g, span in enumerate(spans):
+        for k, ((at, start), target) in enumerate(zip(span, (left_ref, right_ref))):
+            copies.append(
+                pltpu.make_async_copy(
+                    values[at].at[:, pl.ds(start, target.shape[1])], target.at[pl.ds(g * rows, rows), :],
+                    in_sem.at[2 * g + k],
+                )
             )
-            total = term if total is None else total + term
-        scratch_ref[:, start : start + total.shape[1]] = total
-        start += total.shape[1]
-    blocks, height, _ = outs[0].shape
-    start = 0
-    for k, ref in enumerate(outs):
-        wide = ref.shape[2]
-        for i in range(blocks):
-            if by_batch:
-                half = scratch_ref.shape[1] // 2
-                columns = pl.ds(pl.multiple_of((place_ref[1] ^ (k % 2)) * half + start, LANES), wide)
-                ref[i] = scratch_ref[i * height : (i + 1) * height, columns]
-            else:
-                block = 2 * i + (place_ref[2] ^ (k % 2))
-                ref[i] = scratch_ref[
-                    pl.ds(pl.multiple_of(block * height, 8), height), start : start + wide
-                ]
-        start += k % 2 * wide
+            copies[-1].start()
+    for copy in copies:
+        copy.wait()
+    left = left_ref[...].astype(BF16)
+    right = right_ref[...].astype(BF16)
+    blocks, height, _ = keep_ref.shape
+    copies = []
+    for i in range(blocks):
+        total_ref[2 * i * height : 2 * (i + 1) * height, :] = dot(
+            left[:, 2 * i * height : 2 * (i + 1) * height], right, TN
+        )
+        for k, (ref, sem) in enumerate(((keep_ref, keep_sem), (send_ref, send_sem))):
+            block = 2 * i + (place_ref[2] ^ k)
+            source = total_ref.at[pl.ds(pl.multiple_of(block * height, 8), height), :]
+            copies.append(pltpu.make_async_copy(source, ref.at[i], sem.at[i]))
+            copies[-1].start()
+    for copy in copies:
+        copy.wait()
 
 
 SMEM = pl.BlockSpec(memory_space=pltpu.SMEM)
@@ -736,7 +739,7 @@
     inner = ffn_in.shape[1]
     return pl.pallas_call(
         lambda *refs: upward_kernel(pieces, *refs),
-        in_specs=[SMEM] + [VMEM] * 6 + [HBM] * 2,
+        in_specs=[SMEM] + [WHOLE] * 6 + [HBM] * 2,
         out_specs=(HBM,) * 11,
         out_shape=(
             shaped(2, rows, features // 2), shaped(2, 2, rows, features // 4),
@@ -782,17 +785,20 @@
     )(place, cot, slope2, hidden, pre, slope1, gain, act, z2, ffn_out, ffn_in, glu_weight)
 
 
-def products(place, values, spans, tall, wide, blocks, chunks=1, by_batch=False):
-    if by_batch:
-        out = shaped(blocks, tall // blocks, wide // 2 // chunks)
-    else:
-        out = shaped(blocks // 2, tall // blocks, wide // chunks)
+def products(place, values, spans, tall, wide, blocks):
+    out = shaped(blocks // 2, tall // blocks, wide)
+    tokens = len(spans) * values[0].shape[0]
     return pl.pallas_call(
-        lambda *refs: product_kernel(spans, by_batch, *refs),
-        in_specs=[SMEM] + [VMEM] * len(values),
-        out_shape=(out,) * (2 * chunks),
-        scratch_shapes=[pltpu.VMEM((tall, wide), F32)],
-        compiler_params=params_of(28), cost_estimate=estimate(4), name="products",
+        functools.partial(product_kernel, spans),
+        in_specs=[SMEM] + [HBM] * len(values),
+        out_specs=(HBM, HBM),
+        out_shape=(out, out),
+        scratch_shapes=[
+            pltpu.VMEM((tokens, tall), F32), pltpu.VMEM((tokens, wide), F32), pltpu.VMEM((tall, wide), F32),
+            pltpu.SemaphoreType.DMA((2 * len(spans),)), pltpu.SemaphoreType.DMA((blocks // 2,)),
+            pltpu.SemaphoreType.DMA((blocks // 2,)),
+        ],
+        compiler_params=params_of(60), cost_estimate=estimate(4), name="products",
     )(place, *values)
 
 
@@ -875,11 +881,75 @@
     table = shaped(features, LANES // 2)
     return pl.pallas_call(
         functools.partial(pull_kernel, lengths),
-        in_specs=[SMEM] + [VMEM] * 13,
+        in_specs=[SMEM] + [WHOLE] * 13,
         out_shape=(table,) * 6 + (row,) * 4 + tuple(shaped(1, length) for length in lengths),
         scratch_shapes=[pltpu.VMEM((features, LANES), F32)] * 2,
         compiler_params=params_of(32), cost_estimate=estimate(4), name="pulled",
     )(place, own, other, *tables, gain, bias, skip, step, real, freq)
+
+
+def wide_product_kernel(quarter, place_ref, *refs):
+    values, outs = refs[:4], refs[4:8]
+    left_ref, right_ref, total_ref, left_sem, right_sem, out_sem = refs[8:]
+    rows = values[0].shape[0]
+    parts = right_ref.shape[0]
+    wide = right_ref.shape[2]
+    copies = []
+    for v, value in enumerate(values):
+        at = pl.ds(parts * wide + (quarter if v >= 2 else 0), quarter)
+        copies.append(
+            pltpu.make_async_copy(value.at[:, at], left_ref.at[pl.ds(v * rows, rows), :], left_sem.at[v])
+        )
+    for k in range(parts):
+        for v, value in enumerate(values):
+            copies.append(
+                pltpu.make_async_copy(
+                    value.at[:, pl.ds(k * wide, wide)], right_ref.at[k, pl.ds(v * rows, rows), :],
+                    right_sem.at[4 * k + v],
+                )
+            )
+    for copy in copies:
+        copy.start()
+    for copy in copies[:4]:
+        copy.wait()
+    left = left_ref[...].astype(BF16)
+    blocks, height, _ = outs[0].shape
+    for k in range(parts):
+        for copy in copies[4 + 4 * k : 8 + 4 * k]:
+            copy.wait()
+        total = dot(left, right_ref[k].astype(BF16), TN)
+        total_ref[k] = total.reshape(blocks, height, wide)
+        here = place_ref[1] == k // 2
+        keep, send = outs[2 * (k % 2)], outs[2 * (k % 2) + 1]
+
+        @pl.when(here)
+        def _():
+            pltpu.make_async_copy(total_ref.at[k], keep, out_sem.at[k]).start()
+
+        @pl.when(jnp.logical_not(here))
+        def _():
+            pltpu.make_async_copy(total_ref.at[k], send, out_sem.at[k]).start()
+
+    for k in range(parts):
+        pltpu.make_async_copy(total_ref.at[k], outs[0], out_sem.at[k]).wait()
+
+
+def wide_products(place, values, inner, quarter, blocks):
+    rows = values[0].shape[0]
+    wide = inner // 4
+    out = shaped(blocks, quarter // blocks, wide)
+    return pl.pallas_call(
+        functools.partial(wide_product_kernel, quarter),
+        in_specs=[SMEM] + [HBM] * 4,
+        out_specs=(HBM,) * 4,
+        out_shape=(out,) * 4,
+        scratch_shapes=[
+            pltpu.VMEM((4 * rows, quarter), F32), pltpu.VMEM((4, 4 * rows, wide), F32),
+            pltpu.VMEM((4, blocks, quarter // blocks, wide), F32),
+            pltpu.SemaphoreType.DMA((4,)), pltpu.SemaphoreType.DMA((16,)), pltpu.SemaphoreType.DMA((4,)),
+        ],
+        compiler_params=params_of(60), cost_estimate=estimate(5), name="wide_products",
+    )(place, *values)
 
 
 def flipped(value, axis, bit):
@@ -1030,9 +1100,8 @@
     in_z = across(in_send, 4)
     glu_send, ffn_x, ffn_xo = lax.optimization_barrier((glu_send, ffn_x, ffn_xo))
     glu_x = over_batch(glu_send)
-    every = slice(None)
     values = [ffn_here, ffn_x, across(ffn_there), across(ffn_xo)] + ups
-    spans = [[(i, every), (i + 4, every)] for i in range(4)]
+    spans = [[(i, 0), (i + 4, 0)] for i in range(4)]
     keep_out, send_out = products(place, values, spans, inner // 4, features, pieces // 2)
     back = by_channel(turned)
     lags, send_out = lax.optimization_barrier((lags, send_out))
@@ -1059,22 +1128,17 @@
         [out], grad_rows, glu_x, in_z, in_c, state, tables, around
     )
     out.step()
-    grad_normed = by_channel(grad_rows.reshape(pieces, channels, rows)).reshape(features, rows)
     in_keep, out.keep = lax.optimization_barrier((in_keep, out.keep))
     quarter, half = features // 4, features // 2
     values = [in_keep, in_z, in_c, across(in_z)]
-    low_half, high_half = slice(0, inner // 2), slice(inner // 2, inner)
-    here, there = slice(inner, inner + quarter), slice(inner + quarter, inner + half)
-    spans = [[(i, here if i < 2 else there), (i, low_half), (i, high_half)] for i in range(4)]
-    keep_a, send_a, keep_b, send_b = products(
-        place, values, spans, quarter, inner, pieces // 4, 2, by_batch=True
-    )
+    keep_a, send_a, keep_b, send_b = wide_products(place, values, inner, quarter, pieces // 4)
+    grad_rows, keep_a = lax.optimization_barrier((grad_rows, keep_a))
+    grad_normed = by_channel(grad_rows.reshape(pieces, channels, rows)).reshape(features, rows)
     first = Halving(keep_a, over_batch(send_a), mine, [2] + high_bits)
     second = Halving(keep_b, over_batch(send_b), mine, [2] + high_bits)
     glu_own = glu_keep
     values = [glu_own, glu_x, across(glu_keep), across(glu_x)]
-    here, there = slice(features, features + half), slice(features + half, 2 * features)
-    spans = [[(i, here if i < 2 else there), (i, slice(0, features))] for i in range(4)]
+    spans = [[(i, features if i < 2 else features + half), (i, 0)] for i in range(4)]
     keep_glu, send_glu = products(place, values, spans, half, features, pieces // 2)
     (state,) = tied([out], state)
     out.step()

time: 301 us -> 298 us (0.990)
  waiting for transfers between devices: 70.9 us -> 80.5 us
  local copies, waits for them, and re-layouts: 35.5 us -> 27.8 us
  starting transfers between devices: 53.7 us -> 49.6 us
    unnamed x154 -> x142, local copies, waits for them, and re-layouts: 32.5 us -> 24.7 us
    all_to_all x4, waiting for transfers between devices: 3.55 us -> 10.8 us  [by_channel(): return lax.all_to_all(value, 'seq', 0, 0)]
    ppermute x31, starting transfers between devices: 28.7 us -> 25.3 us  [flipped(): return lax.ppermute(value, axis, [(i, i ^ bit) for i in range(count)])]
  transfers between devices with their start and end apart: 36 -> 36, of which waited for: 12 -> 14; matrix products, arithmetic and copies ran while one was open for 20% -> 19% of each run, Pallas kernels for 26% -> 26%
where the time goes in v6:
time: 298 us; the launch traced here: 295 us
  Pallas kernels  90.6 us (30%)
  waiting for transfers between devices  80.5 us (27%)
  starting transfers between devices  49.6 us (17%)
  other arithmetic  43.2 us (14%)
  local copies, waits for them, and re-layouts  27.8 us (9%)
    ppermute x31, waiting for transfers between devices, flipped(): return lax.ppermute(value, axis, [(i, i ^ bit) for i in range(count)])  63.6 us
    ppermute x31, starting transfers between devices, flipped(): return lax.ppermute(value, axis, [(i, i ^ bit) for i in range(count)])  25.3 us
    unnamed x142, local copies, waits for them, and re-layouts  24.7 us
    pallas_call x1, Pallas kernels, recurrence_back(): pl.pallas_call(lambda *refs: backward_kernel(sizes, *refs), out_shape=(ja...  24.2 us
    all_to_all x4, starting transfers between devices, by_channel(): return lax.all_to_all(value, 'seq', 0, 0)  20.5 us
    pallas_call x1, Pallas kernels, downward(): pl.pallas_call(downward_kernel, in_specs=[SMEM, VMEM] + [HBM] * 4 + [VMEM...  15.8 us
    pallas_call x1, Pallas kernels, recurrence(): pl.pallas_call(lambda *refs: forward_kernel(sizes, *refs), out_shape=(jax...  11 us
    all_to_all x4, waiting for transfers between devices, by_channel(): return lax.all_to_all(value, 'seq', 0, 0)  10.8 us
  transfers between devices with their start and end apart: 36, of which 14 were waited for; matrix products, arithmetic and copies ran while one was open for 19% of the time, Pallas kernels for 26%

profile of v6, /device:TPU:0, one launch (start us, length us, event | category | flops | bytes accessed | tf_op | source)
XLA Modules:
  0.0 295.2 jit_solution(10954167799410609286)
XLA Ops:
  9.0 5.9 %all-to-all-start = ((f32[16,72,128]{2,1,0:T(8,128)}), f32[16,72,128]{2,1,0:T(8,128)S(1)}, u32[]{:S(2)}, u32[]{:S(2)}) async-start(f32[16,72,128]{2,1,0:T(8,128)} %get-tuple-element.157), calls=%async_computation | async-start | bytes 1179648 | tf_op jit(solution)/shard_map/all_to_all | solution.py:1070
  23.9 5.0 %add_negate_fusion = (f32[1024,64]{1,0:T(8,128)}, f32[1024,64]{1,0:T(8,128)}, f32[1024,64]{1,0:T(8,128)}, f32[1024,64]{1,0:T(8,128)}, f32[1024,64]{1,0:T(8,128)}, /*index=5*/f32[1024,64]{1,0:T(8,128)}) fusion(f32[1024,64]{1,0:T(8,128)S(1)} %get-tuple-element.378, f32[1024,64]{1,0:T(8,128)S(1)} %copy.112, f32[1024,64]{1,0:T(8,128)S(1)} %get-tuple-element.377, ...), kind=kLoop, calls=%fused_computation.33 | loop fusion | flops 1966080 | bytes 2625536 | tf_op jit(solution)/shard_map/neg | solution.py:1036
  30.5 11.0 %recurrence.1 = (f32[1024,128]{1,0:T(8,128)}, f32[64,64,128]{2,1,0:T(8,128)S(1)}, f32[64,128]{1,0:T(8,128)S(1)}) custom-call(f32[1152,128]{1,0:T(8,128)S(1)} %bitcast.149, f32[64,128]{1,0:T(8,128)S(1)} %get-tuple-element.386.refs_1_.refs_4_, f32[64,128]{1,0:T(8,128)S(1)} %get-tuple-element.387.refs_2_.refs_5_, f32[64,128]{1,0:T(8,128)S(1)} %broadcast_in_dim.10.refs_3_.refs_6_), custom_call_target="tpu_custom_call" | custom-call | flops 16000000000 | tf_op jit(solution)/shard_map/recurrence/pallas_call | solution.py:374
  43.0 4.6 %all-to-all-start.1 = ((f32[16,64,128]{2,1,0:T(8,128)}), f32[16,64,128]{2,1,0:T(8,128)}, u32[]{:S(2)}, u32[]{:S(2)}) async-start(f32[16,64,128]{2,1,0:T(8,128)} %bitcast.9), calls=%async_computation.1 | async-start | bytes 1048576 | tf_op jit(solution)/shard_map/all_to_all | solution.py:1070
  47.6 3.8 %multiply_add_fusion.4 = (f32[1024,64]{1,0:T(8,128)}, f32[1024,64]{1,0:T(8,128)}, f32[1024,64]{1,0:T(8,128)}, f32[1024,64]{1,0:T(8,128)}, f32[1024,64]{1,0:T(8,128)}, /*index=5*/f32[1024,64]{1,0:T(8,128)}) fusion(f32[1024,64]{1,0:T(8,128)} %get-tuple-element.357, f32[1024,64]{1,0:T(8,128)} %get-tuple-element.358, f32[1024,64]{1,0:T(8,128)S(1)} %copy.116, ...), kind=kLoop, calls=%fused_computation.44 | loop fusion | flops 1376256 | bytes 3670016 | tf_op jit(solution)/shard_map/add | solution.py:1009
  58.2 3.9 %all-to-all-done.1 = f32[16,64,128]{2,1,0:T(8,128)} async-done(((f32[16,64,128]{2,1,0:T(8,128)}), f32[16,64,128]{2,1,0:T(8,128)}, u32[]{:S(2)}, u32[]{:S(2)}) %all-to-all-start.1) | async-done | bytes 524320 | tf_op jit(solution)/shard_map/all_to_all | solution.py:1070
  62.1 10.0 %upward.1 = (f32[2,128,512]{2,1,0:T(8,128)}, f32[2,2,128,256]{3,2,1,0:T(8,128)}, f32[128,1024]{1,0:T(8,128)}, f32[128,1024]{1,0:T(8,128)}, f32[128,1024]{1,0:T(8...) custom-call(s32[4]{0:T(128)} %pad_add_fusion.refs_0_.place_ref, ...), custom_call_target="tpu_custom_call" | custom-call | flops 14000000000 | tf_op jit(solution)/shard_map/upward/pallas_call | solution.py:740
  74.2 15.8 %downward.1 = (f32[128,4608]{1,0:T(8,128)}, f32[128,4608]{1,0:T(8,128)}, f32[128,2048]{1,0:T(8,128)}, f32[128,2048]{1,0:T(8,128)}, f32[128,1024]{1,0:T(8,128)}, /*index=5*/f32[16,72,128]{2,1,0:T(8,128)}) custom-call(s32[4]{0:T(128)} %pad_add_fusion.refs_0_.place_ref, bf16[128,1024]{1,0:T(8,128)(2,1)} %bitcast.152, ...), custom_call_target="tpu_custom_call" | custom-call | flops 17999998976 | tf_op jit(solution)/shard_map/downward/pallas_call | solution.py:764
  89.9 4.1 %all-to-all-start.2 = ((f32[16,72,128]{2,1,0:T(8,128)}), f32[16,72,128]{2,1,0:T(8,128)S(1)}, u32[]{:S(2)}, u32[]{:S(2)}) async-start(f32[16,72,128]{2,1,0:T(8,128)} %get-tuple-element.183), calls=%async_computation.2 | async-start | bytes 1179648 | tf_op jit(solution)/shard_map/all_to_all | solution.py:1070
  101.8 5.4 %products.2 = (f32[4,128,1024]{2,1,0:T(8,128)}, f32[4,128,1024]{2,1,0:T(8,128)}) custom-call(s32[4]{0:T(128)} %pad_add_fusion.refs_0_.place_ref, f32[128,1024]{1,0:T(8,128)} %get-tuple-element.168.refs_0_, f32[128,1024]{1,0:T(8,128)} %copy-done.60, f32[128,1024]{1,0:T(8,128)} %copy-done.62, f32[128,1024]{1,0:T(8,128)} %collective-permute-done.6.refs_3_, ...), custom_call_target="tpu_custom_call" | custom-call | flops 4000000000 | tf_op jit(solution)/shard_map/products/pallas_call | solution.py:791
  111.6 24.2 %recurrence_back.1 = (f32[1024,128]{1,0:T(8,128)}, f32[64,128]{1,0:T(8,128)S(1)}, f32[64,128]{1,0:T(8,128)S(1)}, f32[64,128]{1,0:T(8,128)S(1)}, f32[64,128]{1,0:T(8,128)S(1)}) custom-call(f32[1152,128]{1,0:T(8,128)S(1)} %bitcast.150, f32[1152,128]{1,0:T(8,128)S(1)} %bitcast.148, f32[64,64,128]{2,1,0:T(8,128)S(1)} %copy-done.35, ...), custom_call_target="tpu_custom_call" | custom-call | flops 30000001024 | tf_op jit(solution)/shard_map/recurrence_back/pallas_call | solution.py:393
  142.7 14.6 %collective-permute-done.9.refs_1_ = f32[128,4608]{1,0:T(8,128)} collective-permute-done((f32[128,4608]{1,0:T(8,128)}, f32[128,4608]{1,0:T(8,128)}, u32[]{:S(2)}, u32[]{:S(2)}) %collective-permute-start.9) | collective-permute-done | bytes 2359328 | tf_op jit(solution)/shard_map/ppermute | solution.py:957
  163.4 7.1 %wide_products.1 = (f32[4,64,1024]{2,1,0:T(8,128)}, f32[4,64,1024]{2,1,0:T(8,128)}, f32[4,64,1024]{2,1,0:T(8,128)}, f32[4,64,1024]{2,1,0:T(8,128)}) custom-call(s32[4]{0:T(128)} %pad_add_fusion.refs_0_.place_ref, f32[128,4608]{1,0:T(8,128)} %get-tuple-element.217.refs_0_, f32[128,4608]{1,0:T(8,128)} %collective-permute-done.9.refs_1_, ...), custom_call_target="tpu_custom_call" | custom-call | flops 5000000000 | tf_op jit(solution)/shard_map/wide_products/pallas_call | solution.py:941
  170.5 5.8 %all-to-all-start.3 = ((f32[16,64,128]{2,1,0:T(8,128)}), f32[16,64,128]{2,1,0:T(8,128)S(1)}, u32[]{:S(2)}, u32[]{:S(2)}) async-start(f32[16,64,128]{2,1,0:T(8,128)} %bitcast.21), calls=%async_computation.3 | async-start | bytes 1048576 | tf_op jit(solution)/shard_map/all_to_all | solution.py:1070
  176.9 4.3 %products.3 = (f32[4,64,1024]{2,1,0:T(8,128)}, f32[4,64,1024]{2,1,0:T(8,128)}) custom-call(s32[4]{0:T(128)} %pad_add_fusion.refs_0_.place_ref, f32[128,2048]{1,0:T(8,128)} %get-tuple-element.231.refs_0_, f32[128,2048]{1,0:T(8,128)} %collective-permute-done.8.refs_1_, f32[128,2048]{1,0:T(8,128)} %collective-permute-done.18.refs_2_, ...), custom_call_target="tpu_custom_call" | custom-call | flops 4000000000 | tf_op jit(solution)/shard_map/products/pallas_call | solution.py:791
  183.1 10.4 %collective-permute-done.16 = f32[2,128,1024]{2,1,0:T(8,128)} collective-permute-done((f32[2,128,1024]{2,1,0:T(8,128)}, f32[2,128,1024]{2,1,0:T(8,128)}, u32[]{:S(2)}, u32[]{:S(2)}) %collective-permute-start.16) | collective-permute-done | bytes 1048608 | tf_op jit(solution)/shard_map/ppermute | solution.py:957
  208.1 4.0 %collective-permute-done.20 = f32[4,64,1024]{2,1,0:T(8,128)} collective-permute-done((f32[4,64,1024]{2,1,0:T(8,128)}, f32[4,64,1024]{2,1,0:T(8,128)}, u32[]{:S(2)}, u32[]{:S(2)}) %collective-permute-start.20) | collective-permute-done | bytes 1048608 | tf_op jit(solution)/shard_map/ppermute | solution.py:957
  222.9 5.3 %collective-permute-done.17 = f32[1,128,1024]{2,1,0:T(8,128)} collective-permute-done((f32[1,128,1024]{2,1,0:T(8,128)}, f32[1,128,1024]{2,1,0:T(8,128)}, u32[]{:S(2)}, u32[]{:S(2)}) %collective-permute-start.17) | collective-permute-done | bytes 524320 | tf_op jit(solution)/shard_map/ppermute | solution.py:957
  228.1 6.1 %all-to-all-done.4.own_ref = f32[8,72,256]{2,1,0:T(8,128)S(1)} async-done(((f32[8,72,256]{2,1,0:T(8,128)}), f32[8,72,256]{2,1,0:T(8,128)S(1)}, u32[]{:S(2)}, u32[]{:S(2)}) %all-to-all-start.4) | async-done | bytes 589856 | tf_op jit(solution)/shard_map/all_to_all | solution.py:1156
  234.2 5.3 %collective-permute-done.21 = f32[2,64,1024]{2,1,0:T(8,128)} collective-permute-done((f32[2,64,1024]{2,1,0:T(8,128)}, f32[2,64,1024]{2,1,0:T(8,128)}, u32[]{:S(2)}, u32[]{:S(2)}) %collective-permute-start.21) | collective-permute-done | bytes 524320 | tf_op jit(solution)/shard_map/ppermute | solution.py:957
  251.7 5.4 %pulled.1 = (f32[1024,64]{1,0:T(8,128)S(1)}, f32[1024,64]{1,0:T(8,128)S(1)}, f32[1024,64]{1,0:T(8,128)S(1)}, f32[1024,64]{1,0:T(8,128)S(1)}, f32[1024,64]{1,0:T(...) custom-call(s32[4]{0:T(128)S(1)} %copy-done.17, ...), custom_call_target="tpu_custom_call" | custom-call | flops 4000000000 | tf_op jit(solution)/shard_map/pulled/pallas_call | solution.py:882
  257.2 4.7 %collective-permute-done.24 = f32[1,64,1024]{2,1,0:T(8,128)S(1)} collective-permute-done((f32[1,64,1024]{2,1,0:T(8,128)S(1)}, f32[1,64,1024]{2,1,0:T(8,128)S(1)}, u32[]{:S(2)}, u32[]{:S(2)}) %collective-permute-start.24) | collective-permute-done | bytes 262176 | tf_op jit(solution)/shard_map/ppermute | solution.py:957
  261.8 4.7 %collective-permute-done.23 = f32[1,64,1024]{2,1,0:T(8,128)S(1)} collective-permute-done((f32[1,64,1024]{2,1,0:T(8,128)S(1)}, f32[1,64,1024]{2,1,0:T(8,128)S(1)}, u32[]{:S(2)}, u32[]{:S(2)}) %collective-permute-start.23) | collective-permute-done | bytes 262176 | tf_op jit(solution)/shard_map/ppermute | solution.py:957
  269.4 11.8 %collective-permute-done.27 = f32[1,64,1024]{2,1,0:T(8,128)S(1)} collective-permute-done((f32[1,64,1024]{2,1,0:T(8,128)S(1)}, f32[1,64,1024]{2,1,0:T(8,128)S(1)}, u32[]{:S(2)}, u32[]{:S(2)}) %collective-permute-start.27) | collective-permute-done | bytes 262176 | tf_op jit(solution)/shard_map/ppermute | solution.py:957
  (255 shorter events, 110.7 us)
Async XLA Ops:
  5.9 52.2 %collective-permute-start.1 = (f32[128,1024]{1,0:T(8,128)S(1)}, f32[128,1024]{1,0:T(8,128)}, u32[]{:S(2)}, u32[]{:S(2)}) collective-permute-start(f32[128,1024]{1,0:T(8,128)S(1)} %get-tuple-element.175.refs_4_), channel_id=1, source_target_pairs={{0,1},{1,0},{2,3},{3,2},{4,5},{5,4},{6,7},{7,6},{8,9},{9,8},{10,11... | collective-permute-start | bytes 1572872 | tf_op jit(solution)/shard_map/ppermute | solution.py:957
  6.4 45.0 %collective-permute-start = (f32[128,1024]{1,0:T(8,128)S(1)}, f32[128,1024]{1,0:T(8,128)}, u32[]{:S(2)}, u32[]{:S(2)}) collective-permute-start(f32[128,1024]{1,0:T(8,128)S(1)} %get-tuple-element.175.refs_4_), channel_id=1, source_target_pairs={{0,16},{16,0},{1,17},{17,1},{2,18},{18,2},{3,19},{19,3},{4,20},{20... | collective-permute-start | bytes 1572872 | tf_op jit(solution)/shard_map/ppermute | solution.py:957
  9.0 21.5 %all-to-all-start = ((f32[16,72,128]{2,1,0:T(8,128)}), f32[16,72,128]{2,1,0:T(8,128)S(1)}, u32[]{:S(2)}, u32[]{:S(2)}) async-start(f32[16,72,128]{2,1,0:T(8,128)} %get-tuple-element.157), calls=%async_computation | async-start | bytes 1179648 | tf_op jit(solution)/shard_map/all_to_all | solution.py:1070
  43.0 19.1 %all-to-all-start.1 = ((f32[16,64,128]{2,1,0:T(8,128)}), f32[16,64,128]{2,1,0:T(8,128)}, u32[]{:S(2)}, u32[]{:S(2)}) async-start(f32[16,64,128]{2,1,0:T(8,128)} %bitcast.9), calls=%async_computation.1 | async-start | bytes 1048576 | tf_op jit(solution)/shard_map/all_to_all | solution.py:1070
  72.1 22.5 %collective-permute-start.3 = (f32[128,1024]{1,0:T(8,128)}, f32[128,1024]{1,0:T(8,128)S(1)}, u32[]{:S(2)}, u32[]{:S(2)}) collective-permute-start(f32[128,1024]{1,0:T(8,128)} %get-tuple-element.170), channel_id=1, source_target_pairs={{0,16},{16,0},{1,17},{17,1},{2,18},{18,2},{3,19},{19,3},{4,20},{20... | collective-permute-start | bytes 1572872 | tf_op jit(solution)/shard_map/ppermute | solution.py:957
  72.7 24.9 %collective-permute-start.4 = (f32[128,1024]{1,0:T(8,128)}, f32[128,1024]{1,0:T(8,128)}, u32[]{:S(2)}, u32[]{:S(2)}) collective-permute-start(f32[128,1024]{1,0:T(8,128)} %get-tuple-element.171), channel_id=1, source_target_pairs={{0,16},{16,0},{1,17},{17,1},{2,18},{18,2},{3,19},{19,3},{4,20},{20... | collective-permute-start | bytes 1572872 | tf_op jit(solution)/shard_map/ppermute | solution.py:957
  89.9 20.0 %all-to-all-start.2 = ((f32[16,72,128]{2,1,0:T(8,128)}), f32[16,72,128]{2,1,0:T(8,128)S(1)}, u32[]{:S(2)}, u32[]{:S(2)}) async-start(f32[16,72,128]{2,1,0:T(8,128)} %get-tuple-element.183), calls=%async_computation.2 | async-start | bytes 1179648 | tf_op jit(solution)/shard_map/all_to_all | solution.py:1070
  98.5 58.8 %collective-permute-start.9 = (f32[128,4608]{1,0:T(8,128)}, f32[128,4608]{1,0:T(8,128)}, u32[]{:S(2)}, u32[]{:S(2)}) collective-permute-start(f32[128,4608]{1,0:T(8,128)} %get-tuple-element.188), channel_id=1, source_target_pairs={{0,4},{1,5},{2,6},{3,7},{4,0},{5,1},{6,2},{7,3},{8,12},{9,13},{10,... | collective-permute-start | bytes 7077896 | tf_op jit(solution)/shard_map/ppermute | solution.py:957
  100.3 57.1 %collective-permute-start.10 = (f32[128,4608]{1,0:T(8,128)}, f32[128,4608]{1,0:T(8,128)}, u32[]{:S(2)}, u32[]{:S(2)}) collective-permute-start(f32[128,4608]{1,0:T(8,128)} %get-tuple-element.217.refs_0_), channel_id=1, source_target_pairs={{0,1},{1,0},{2,3},{3,2},{4,5},{5,4},{6,7},{7,6},{8,9},{9,8},{10,11... | collective-permute-start | bytes 7077896 | tf_op jit(solution)/shard_map/ppermute | solution.py:957
  100.5 42.2 %collective-permute-start.8 = (f32[128,2048]{1,0:T(8,128)}, f32[128,2048]{1,0:T(8,128)}, u32[]{:S(2)}, u32[]{:S(2)}) collective-permute-start(f32[128,2048]{1,0:T(8,128)} %get-tuple-element.187), channel_id=1, source_target_pairs={{0,16},{16,0},{1,17},{17,1},{2,18},{18,2},{3,19},{19,3},{4,20},{20... | collective-permute-start | bytes 3145736 | tf_op jit(solution)/shard_map/ppermute | solution.py:957
  107.2 50.1 %collective-permute-start.7 = (f32[4,128,1024]{2,1,0:T(8,128)}, f32[4,128,1024]{2,1,0:T(8,128)}, u32[]{:S(2)}, u32[]{:S(2)}) collective-permute-start(f32[4,128,1024]{2,1,0:T(8,128)} %get-tuple-element.182), channel_id=1, source_target_pairs={{0,2},{1,3},{2,0},{3,1},{4,6},{5,7},{6,4},{7,5},{8,10},{9,11},{10,... | collective-permute-start | bytes 6291464 | tf_op jit(solution)/shard_map/ppermute | solution.py:957
  158.3 18.5 %collective-permute-start.18 = (f32[128,2048]{1,0:T(8,128)}, f32[128,2048]{1,0:T(8,128)}, u32[]{:S(2)}, u32[]{:S(2)}) collective-permute-start(f32[128,2048]{1,0:T(8,128)} %get-tuple-element.231.refs_0_), channel_id=1, source_target_pairs={{0,1},{1,0},{2,3},{3,2},{4,5},{5,4},{6,7},{7,6},{8,9},{9,8},{10,11... | collective-permute-start | bytes 3145736 | tf_op jit(solution)/shard_map/ppermute | solution.py:957
  163.0 30.5 %collective-permute-start.16 = (f32[2,128,1024]{2,1,0:T(8,128)}, f32[2,128,1024]{2,1,0:T(8,128)}, u32[]{:S(2)}, u32[]{:S(2)}) collective-permute-start(f32[2,128,1024]{2,1,0:T(8,128)} %get-tuple-element.370), channel_id=1, source_target_pairs={{0,4},{1,5},{2,6},{3,7},{4,0},{5,1},{6,2},{7,3},{8,12},{9,13},{10,... | collective-permute-start | bytes 3145736 | tf_op jit(solution)/shard_map/ppermute | solution.py:957
  170.5 30.0 %all-to-all-start.3 = ((f32[16,64,128]{2,1,0:T(8,128)}), f32[16,64,128]{2,1,0:T(8,128)S(1)}, u32[]{:S(2)}, u32[]{:S(2)}) async-start(f32[16,64,128]{2,1,0:T(8,128)} %bitcast.21), calls=%async_computation.3 | async-start | bytes 1048576 | tf_op jit(solution)/shard_map/all_to_all | solution.py:1070
  176.4 28.9 %collective-permute-start.14 = (f32[4,64,1024]{2,1,0:T(8,128)}, f32[4,64,1024]{2,1,0:T(8,128)}, u32[]{:S(2)}, u32[]{:S(2)}) collective-permute-start(f32[4,64,1024]{2,1,0:T(8,128)} %get-tuple-element.224), channel_id=1, source_target_pairs={{0,16},{16,0},{1,17},{17,1},{2,18},{18,2},{3,19},{19,3},{4,20},{20... | collective-permute-start | bytes 3145736 | tf_op jit(solution)/shard_map/ppermute | solution.py:957
  181.2 31.0 %collective-permute-start.20 = (f32[4,64,1024]{2,1,0:T(8,128)}, f32[4,64,1024]{2,1,0:T(8,128)}, u32[]{:S(2)}, u32[]{:S(2)}) collective-permute-start(f32[4,64,1024]{2,1,0:T(8,128)} %get-tuple-element.234), channel_id=1, source_target_pairs={{0,2},{1,3},{2,0},{3,1},{4,6},{5,7},{6,4},{7,5},{8,10},{9,11},{10,... | collective-permute-start | bytes 3145736 | tf_op jit(solution)/shard_map/ppermute | solution.py:957
  196.0 32.1 %collective-permute-start.17 = (f32[1,128,1024]{2,1,0:T(8,128)}, f32[1,128,1024]{2,1,0:T(8,128)}, u32[]{:S(2)}, u32[]{:S(2)}) collective-permute-start(f32[1,128,1024]{2,1,0:T(8,128)} %select_bitcast_fusion.5), channel_id=1, source_target_pairs={{0,8},{1,9},{2,10},{3,11},{4,12},{5,13},{6,14},{7,15},{8,0},{9,1},... | collective-permute-start | bytes 1572872 | tf_op jit(solution)/shard_map/ppermute | solution.py:957
  196.3 37.9 %collective-permute-start.13 = (f32[4,64,1024]{2,1,0:T(8,128)}, f32[4,64,1024]{2,1,0:T(8,128)}, u32[]{:S(2)}, u32[]{:S(2)}) collective-permute-start(f32[4,64,1024]{2,1,0:T(8,128)} %get-tuple-element.220), channel_id=1, source_target_pairs={{0,16},{16,0},{1,17},{17,1},{2,18},{18,2},{3,19},{19,3},{4,20},{20... | collective-permute-start | bytes 3145736 | tf_op jit(solution)/shard_map/ppermute | solution.py:957
  201.5 32.7 %all-to-all-start.4 = ((f32[8,72,256]{2,1,0:T(8,128)}), f32[8,72,256]{2,1,0:T(8,128)S(1)}, u32[]{:S(2)}, u32[]{:S(2)}) async-start(f32[8,72,256]{2,1,0:T(8,128)} %broadcast_in_dim.28), calls=%async_computation.4 | async-start | bytes 1179648 | tf_op jit(solution)/shard_map/all_to_all | solution.py:1156
  215.6 23.9 %collective-permute-start.21 = (f32[2,64,1024]{2,1,0:T(8,128)}, f32[2,64,1024]{2,1,0:T(8,128)}, u32[]{:S(2)}, u32[]{:S(2)}) collective-permute-start(f32[2,64,1024]{2,1,0:T(8,128)} %select_bitcast_fusion.3), channel_id=1, source_target_pairs={{0,4},{1,5},{2,6},{3,7},{4,0},{5,1},{6,2},{7,3},{8,12},{9,13},{10,... | collective-permute-start | bytes 1572872 | tf_op jit(solution)/shard_map/ppermute | solution.py:957
  216.9 22.6 %collective-permute-start.15 = (f32[2,64,1024]{2,1,0:T(8,128)}, f32[2,64,1024]{2,1,0:T(8,128)}, u32[]{:S(2)}, u32[]{:S(2)}) collective-permute-start(f32[2,64,1024]{2,1,0:T(8,128)} %get-tuple-element.380), channel_id=1, source_target_pairs={{0,2},{1,3},{2,0},{3,1},{4,6},{5,7},{6,4},{7,5},{8,10},{9,11},{10,... | collective-permute-start | bytes 1572872 | tf_op jit(solution)/shard_map/ppermute | solution.py:957
  242.3 19.5 %collective-permute-start.24 = (f32[1,64,1024]{2,1,0:T(8,128)S(1)}, f32[1,64,1024]{2,1,0:T(8,128)S(1)}, u32[]{:S(2)}, u32[]{:S(2)}) collective-permute-start(f32[1,64,1024]{2,1,0:T(8,128)S(1)} %select_bitcast_fusion.8), channel_id=1, source_target_pairs={{0,8},{1,9},{2,10},{3,11},{4,12},{5,13},{6,14},{7,15},{8,0},{9,1},... | collective-permute-start | bytes 786440 | tf_op jit(solution)/shard_map/ppermute | solution.py:957
  244.9 21.6 %collective-permute-start.22 = (f32[2,64,1024]{2,1,0:T(8,128)S(1)}, f32[2,64,1024]{2,1,0:T(8,128)S(1)}, u32[]{:S(2)}, u32[]{:S(2)}) collective-permute-start(f32[2,64,1024]{2,1,0:T(8,128)S(1)} %select_bitcast_fusion.2), channel_id=1, source_target_pairs={{0,2},{1,3},{2,0},{3,1},{4,6},{5,7},{6,4},{7,5},{8,10},{9,11},{10,... | collective-permute-start | bytes 1572872 | tf_op jit(solution)/shard_map/ppermute | solution.py:957
  247.0 19.5 %collective-permute-start.25 = (f32[128,1024]{1,0:T(8,128)S(1)}, f32[128,1024]{1,0:T(8,128)S(1)}, u32[]{:S(2)}, u32[]{:S(2)}) collective-permute-start(f32[128,1024]{1,0:T(8,128)S(1)} %fusion.3.refs_0_), channel_id=1, source_target_pairs={{0,16},{16,0},{1,17},{17,1},{2,18},{18,2},{3,19},{19,3},{4,20},{20... | collective-permute-start | bytes 1572872 | tf_op jit(solution)/shard_map/ppermute | solution.py:957
  (77 other events, 529.4 us)

commit v7 on v6

--- a/solution.py
+++ b/solution.py
@@ -1155,12 +1155,11 @@
     state = jnp.broadcast_to(state[None], (pieces // 2,) + state.shape)
     state = lax.all_to_all(state, "seq", 0, 0, axis_index_groups=groups)
 
-    grad_normed, ffn_low = tied([first], grad_normed, ffn_low)
+    (grad_normed,) = tied([first], grad_normed)
     first.step()
     ffn_res = jnp.dot(ffn_low, ffn_out, preferred_element_type=F32) + ffn_out_bias
     result = (hidden + ffn_res).astype(BF16).reshape(tokens.shape)
     grad_tokens = last_norm(grad_normed, flat, line(norm1_gain), grad_hidden).reshape(tokens.shape)
-    (first.keep,) = tied([glu], first.keep)
     glu.step()
 
     state, result, grad_tokens = tied([second, first, out, glu], state, result, grad_tokens)

time: 298 us -> 295 us (0.990)
  waiting for transfers between devices: 80.5 us -> 75 us
  matrix products: 2.02 us -> 5.53 us
    ppermute x31, waiting for transfers between devices: 63.6 us -> 56.7 us  [flipped(): return lax.ppermute(value, axis, [(i, i ^ bit) for i in range(count)])]
    all_to_all x1, starting transfers between devices: 3.8 us -> 9.16 us  [on_device(): state = lax.all_to_all(state, 'seq', 0, 0, axis_index_groups=groups)]
    all_to_all x1, waiting for transfers between devices: 6.07 us -> 11.2 us  [on_device(): state = lax.all_to_all(state, 'seq', 0, 0, axis_index_groups=groups)]
    all_to_all x4, waiting for transfers between devices: 10.8 us -> 7.11 us  [by_channel(): return lax.all_to_all(value, 'seq', 0, 0)]
    dot_general x1, matrix products: 2.02 us -> 5.53 us  [on_device(): jnp.dot(ffn_low, ffn_out, preferred_element_type=F32) + ffn_out_bias]
    unnamed x142 -> x140, local copies, waits for them, and re-layouts: 24.7 us -> 22.2 us
  transfers between devices with their start and end apart: 36 -> 36, of which waited for: 14 -> 13; matrix products, arithmetic and copies ran while one was open for 19% -> 20% of each run, Pallas kernels for 26% -> 26%
where the time goes in v7:
time: 295 us; the launch traced here: 294 us
  Pallas kernels  90.6 us (31%)
  waiting for transfers between devices  75 us (25%)
  starting transfers between devices  52.4 us (18%)
  other arithmetic  43.2 us (15%)
  local copies, waits for them, and re-layouts  25.3 us (9%)
  matrix products  5.53 us (2%)
    ppermute x31, waiting for transfers between devices, flipped(): return lax.ppermute(value, axis, [(i, i ^ bit) for i in range(count)])  56.7 us
    ppermute x31, starting transfers between devices, flipped(): return lax.ppermute(value, axis, [(i, i ^ bit) for i in range(count)])  24.8 us
    pallas_call x1, Pallas kernels, recurrence_back(): pl.pallas_call(lambda *refs: backward_kernel(sizes, *refs), out_shape=(ja...  24.2 us
    unnamed x140, local copies, waits for them, and re-layouts  22.2 us
    all_to_all x4, starting transfers between devices, by_channel(): return lax.all_to_all(value, 'seq', 0, 0)  18.5 us
    pallas_call x1, Pallas kernels, downward(): pl.pallas_call(downward_kernel, in_specs=[SMEM, VMEM] + [HBM] * 4 + [VMEM...  15.8 us
    all_to_all x1, waiting for transfers between devices, on_device(): state = lax.all_to_all(state, 'seq', 0, 0, axis_index_groups=groups)  11.2 us
    pallas_call x1, Pallas kernels, recurrence(): pl.pallas_call(lambda *refs: forward_kernel(sizes, *refs), out_shape=(jax...  11 us
  transfers between devices with their start and end apart: 36, of which 13 were waited for; matrix products, arithmetic and copies ran while one was open for 20% of the time, Pallas kernels for 26%

profile of v7, /device:TPU:0, one launch (start us, length us, event | category | flops | bytes accessed | tf_op | source)
XLA Modules:
  0.0 293.5 jit_solution(18180179313829449601)
XLA Ops:
  9.0 5.9 %all-to-all-start = ((f32[16,72,128]{2,1,0:T(8,128)}), f32[16,72,128]{2,1,0:T(8,128)S(1)}, u32[]{:S(2)}, u32[]{:S(2)}) async-start(f32[16,72,128]{2,1,0:T(8,128)} %get-tuple-element.154), calls=%async_computation | async-start | bytes 1179648 | tf_op jit(solution)/shard_map/all_to_all | solution.py:1070
  23.9 5.0 %add_negate_fusion = (f32[1024,64]{1,0:T(8,128)}, f32[1024,64]{1,0:T(8,128)}, f32[1024,64]{1,0:T(8,128)}, f32[1024,64]{1,0:T(8,128)}, f32[1024,64]{1,0:T(8,128)}, /*index=5*/f32[1024,64]{1,0:T(8,128)}) fusion(f32[1024,64]{1,0:T(8,128)S(1)} %get-tuple-element.372, f32[1024,64]{1,0:T(8,128)S(1)} %copy.112, f32[1024,64]{1,0:T(8,128)S(1)} %get-tuple-element.371, ...), kind=kLoop, calls=%fused_computation.33 | loop fusion | flops 1966080 | bytes 2625536 | tf_op jit(solution)/shard_map/neg | solution.py:1036
  30.5 11.0 %recurrence.1 = (f32[1024,128]{1,0:T(8,128)}, f32[64,64,128]{2,1,0:T(8,128)S(1)}, f32[64,128]{1,0:T(8,128)S(1)}) custom-call(f32[1152,128]{1,0:T(8,128)S(1)} %bitcast.151, f32[64,128]{1,0:T(8,128)S(1)} %get-tuple-element.378.refs_1_.refs_4_, f32[64,128]{1,0:T(8,128)S(1)} %get-tuple-element.379.refs_2_.refs_5_, f32[64,128]{1,0:T(8,128)S(1)} %broadcast_in_dim.10.refs_3_.refs_6_), custom_call_target="tpu_custom_call" | custom-call | flops 16000000000 | tf_op jit(solution)/shard_map/recurrence/pallas_call | solution.py:374
  43.0 4.6 %all-to-all-start.1 = ((f32[16,64,128]{2,1,0:T(8,128)}), f32[16,64,128]{2,1,0:T(8,128)}, u32[]{:S(2)}, u32[]{:S(2)}) async-start(f32[16,64,128]{2,1,0:T(8,128)} %bitcast.9), calls=%async_computation.1 | async-start | bytes 1048576 | tf_op jit(solution)/shard_map/all_to_all | solution.py:1070
  47.6 3.8 %multiply_add_fusion.4 = (f32[1024,64]{1,0:T(8,128)}, f32[1024,64]{1,0:T(8,128)}, f32[1024,64]{1,0:T(8,128)}, f32[1024,64]{1,0:T(8,128)}, f32[1024,64]{1,0:T(8,128)}, /*index=5*/f32[1024,64]{1,0:T(8,128)}) fusion(f32[1024,64]{1,0:T(8,128)} %get-tuple-element.351, f32[1024,64]{1,0:T(8,128)} %get-tuple-element.352, f32[1024,64]{1,0:T(8,128)S(1)} %copy.116, ...), kind=kLoop, calls=%fused_computation.44 | loop fusion | flops 1376256 | bytes 3670016 | tf_op jit(solution)/shard_map/add | solution.py:1009
  58.2 3.8 %all-to-all-done.1 = f32[16,64,128]{2,1,0:T(8,128)} async-done(((f32[16,64,128]{2,1,0:T(8,128)}), f32[16,64,128]{2,1,0:T(8,128)}, u32[]{:S(2)}, u32[]{:S(2)}) %all-to-all-start.1) | async-done | bytes 524320 | tf_op jit(solution)/shard_map/all_to_all | solution.py:1070
  62.1 10.0 %upward.1 = (f32[2,128,512]{2,1,0:T(8,128)}, f32[2,2,128,256]{3,2,1,0:T(8,128)}, f32[128,1024]{1,0:T(8,128)}, f32[128,1024]{1,0:T(8,128)}, f32[128,1024]{1,0:T(8...) custom-call(s32[4]{0:T(128)} %pad_add_fusion.refs_0_.place_ref, ...), custom_call_target="tpu_custom_call" | custom-call | flops 14000000000 | tf_op jit(solution)/shard_map/upward/pallas_call | solution.py:740
  74.2 15.8 %downward.1 = (f32[128,4608]{1,0:T(8,128)}, f32[128,4608]{1,0:T(8,128)}, f32[128,2048]{1,0:T(8,128)}, f32[128,2048]{1,0:T(8,128)}, f32[128,1024]{1,0:T(8,128)}, /*index=5*/f32[16,72,128]{2,1,0:T(8,128)}) custom-call(s32[4]{0:T(128)} %pad_add_fusion.refs_0_.place_ref, bf16[128,1024]{1,0:T(8,128)(2,1)} %bitcast.154, ...), custom_call_target="tpu_custom_call" | custom-call | flops 17999998976 | tf_op jit(solution)/shard_map/downward/pallas_call | solution.py:764
  89.9 4.1 %all-to-all-start.2 = ((f32[16,72,128]{2,1,0:T(8,128)}), f32[16,72,128]{2,1,0:T(8,128)S(1)}, u32[]{:S(2)}, u32[]{:S(2)}) async-start(f32[16,72,128]{2,1,0:T(8,128)} %get-tuple-element.180), calls=%async_computation.2 | async-start | bytes 1179648 | tf_op jit(solution)/shard_map/all_to_all | solution.py:1070
  101.8 5.4 %products.2 = (f32[4,128,1024]{2,1,0:T(8,128)}, f32[4,128,1024]{2,1,0:T(8,128)}) custom-call(s32[4]{0:T(128)} %pad_add_fusion.refs_0_.place_ref, f32[128,1024]{1,0:T(8,128)} %get-tuple-element.165.refs_0_, f32[128,1024]{1,0:T(8,128)} %copy-done.61, f32[128,1024]{1,0:T(8,128)} %copy-done.63, f32[128,1024]{1,0:T(8,128)} %collective-permute-done.6.refs_3_, ...), custom_call_target="tpu_custom_call" | custom-call | flops 4000000000 | tf_op jit(solution)/shard_map/products/pallas_call | solution.py:791
  111.6 24.2 %recurrence_back.1 = (f32[1024,128]{1,0:T(8,128)}, f32[64,128]{1,0:T(8,128)S(1)}, f32[64,128]{1,0:T(8,128)S(1)}, f32[64,128]{1,0:T(8,128)S(1)}, f32[64,128]{1,0:T(8,128)S(1)}) custom-call(f32[1152,128]{1,0:T(8,128)S(1)} %bitcast.152, f32[1152,128]{1,0:T(8,128)S(1)} %bitcast.150, f32[64,64,128]{2,1,0:T(8,128)S(1)} %copy-done.35, ...), custom_call_target="tpu_custom_call" | custom-call | flops 30000001024 | tf_op jit(solution)/shard_map/recurrence_back/pallas_call | solution.py:393
  142.6 14.7 %collective-permute-done.9.refs_1_ = f32[128,4608]{1,0:T(8,128)} collective-permute-done((f32[128,4608]{1,0:T(8,128)}, f32[128,4608]{1,0:T(8,128)}, u32[]{:S(2)}, u32[]{:S(2)}) %collective-permute-start.9) | collective-permute-done | bytes 2359328 | tf_op jit(solution)/shard_map/ppermute | solution.py:957
  166.3 4.3 %products.3 = (f32[4,64,1024]{2,1,0:T(8,128)}, f32[4,64,1024]{2,1,0:T(8,128)}) custom-call(s32[4]{0:T(128)} %pad_add_fusion.refs_0_.place_ref, f32[128,2048]{1,0:T(8,128)} %get-tuple-element.227.refs_0_, f32[128,2048]{1,0:T(8,128)} %collective-permute-done.8.refs_1_, f32[128,2048]{1,0:T(8,128)} %collective-permute-done.18.refs_2_, ...), custom_call_target="tpu_custom_call" | custom-call | flops 4000000000 | tf_op jit(solution)/shard_map/products/pallas_call | solution.py:791
  172.1 7.1 %wide_products.1 = (f32[4,64,1024]{2,1,0:T(8,128)}, f32[4,64,1024]{2,1,0:T(8,128)}, f32[4,64,1024]{2,1,0:T(8,128)}, f32[4,64,1024]{2,1,0:T(8,128)}) custom-call(s32[4]{0:T(128)} %pad_add_fusion.refs_0_.place_ref, f32[128,4608]{1,0:T(8,128)} %get-tuple-element.214.refs_0_, f32[128,4608]{1,0:T(8,128)} %collective-permute-done.9.refs_1_, ...), custom_call_target="tpu_custom_call" | custom-call | flops 5000000000 | tf_op jit(solution)/shard_map/wide_products/pallas_call | solution.py:941
  179.7 3.9 %all-to-all-start.3 = ((f32[16,64,128]{2,1,0:T(8,128)}), f32[16,64,128]{2,1,0:T(8,128)S(1)}, u32[]{:S(2)}, u32[]{:S(2)}) async-start(f32[16,64,128]{2,1,0:T(8,128)} %bitcast.21), calls=%async_computation.3 | async-start | bytes 1048576 | tf_op jit(solution)/shard_map/all_to_all | solution.py:1070
  183.6 8.6 %collective-permute-done.16 = f32[2,128,1024]{2,1,0:T(8,128)} collective-permute-done((f32[2,128,1024]{2,1,0:T(8,128)}, f32[2,128,1024]{2,1,0:T(8,128)}, u32[]{:S(2)}, u32[]{:S(2)}) %collective-permute-start.16) | collective-permute-done | bytes 1048608 | tf_op jit(solution)/shard_map/ppermute | solution.py:957
  194.9 6.1 %collective-permute-done.20 = f32[4,64,1024]{2,1,0:T(8,128)} collective-permute-done((f32[4,64,1024]{2,1,0:T(8,128)}, f32[4,64,1024]{2,1,0:T(8,128)}, u32[]{:S(2)}, u32[]{:S(2)}) %collective-permute-start.20) | collective-permute-done | bytes 1048608 | tf_op jit(solution)/shard_map/ppermute | solution.py:957
  205.1 9.2 %all-to-all-start.4 = ((f32[8,72,256]{2,1,0:T(8,128)}), f32[8,72,256]{2,1,0:T(8,128)S(1)}, u32[]{:S(2)}, u32[]{:S(2)}) async-start(f32[8,72,256]{2,1,0:T(8,128)} %broadcast_in_dim.28), calls=%async_computation.4 | async-start | bytes 1179648 | tf_op jit(solution)/shard_map/all_to_all | solution.py:1156
  219.2 5.5 %fusion.1 = bf16[128,1024]{1,0:T(8,128)(2,1)} fusion(f32[128,1024]{1,0:T(8,128)S(1)} %copy-done.54, bf16[128,4096]{1,0:T(8,128)(2,1)S(1)} %copy-done.44, bf16[4096,1024]{1,0:T(8,128)(2,1)} %out_w_ref.1, f32[1024]{0:T(1024)S(1)} %copy-done.59), kind=kOutput, calls=%fused_computation.2 | convolution fusion | flops 1074135040 | bytes 10227712 | tf_op jit(solution)/shard_map/dot_general | solution.py:1160
  225.9 11.2 %all-to-all-done.4.own_ref = f32[8,72,256]{2,1,0:T(8,128)S(1)} async-done(((f32[8,72,256]{2,1,0:T(8,128)}), f32[8,72,256]{2,1,0:T(8,128)S(1)}, u32[]{:S(2)}, u32[]{:S(2)}) %all-to-all-start.4) | async-done | bytes 589856 | tf_op jit(solution)/shard_map/all_to_all | solution.py:1156
  248.7 5.4 %pulled.1 = (f32[1024,64]{1,0:T(8,128)S(1)}, f32[1024,64]{1,0:T(8,128)S(1)}, f32[1024,64]{1,0:T(8,128)S(1)}, f32[1024,64]{1,0:T(8,128)S(1)}, f32[1024,64]{1,0:T(...) custom-call(s32[4]{0:T(128)S(1)} %copy-done.17, ...), custom_call_target="tpu_custom_call" | custom-call | flops 4000000000 | tf_op jit(solution)/shard_map/pulled/pallas_call | solution.py:882
  254.2 6.5 %collective-permute-done.24 = f32[1,64,1024]{2,1,0:T(8,128)S(1)} collective-permute-done((f32[1,64,1024]{2,1,0:T(8,128)S(1)}, f32[1,64,1024]{2,1,0:T(8,128)S(1)}, u32[]{:S(2)}, u32[]{:S(2)}) %collective-permute-start.24) | collective-permute-done | bytes 262176 | tf_op jit(solution)/shard_map/ppermute | solution.py:957
  260.7 3.9 %collective-permute-done.23 = f32[1,64,1024]{2,1,0:T(8,128)S(1)} collective-permute-done((f32[1,64,1024]{2,1,0:T(8,128)S(1)}, f32[1,64,1024]{2,1,0:T(8,128)S(1)}, u32[]{:S(2)}, u32[]{:S(2)}) %collective-permute-start.23) | collective-permute-done | bytes 262176 | tf_op jit(solution)/shard_map/ppermute | solution.py:957
  267.5 11.0 %collective-permute-done.27 = f32[1,64,1024]{2,1,0:T(8,128)S(1)} collective-permute-done((f32[1,64,1024]{2,1,0:T(8,128)S(1)}, f32[1,64,1024]{2,1,0:T(8,128)S(1)}, u32[]{:S(2)}, u32[]{:S(2)}) %collective-permute-start.27) | collective-permute-done | bytes 262176 | tf_op jit(solution)/shard_map/ppermute | solution.py:957
  (252 shorter events, 100.9 us)
Async XLA Ops:
  5.9 52.3 %collective-permute-start.1 = (f32[128,1024]{1,0:T(8,128)S(1)}, f32[128,1024]{1,0:T(8,128)}, u32[]{:S(2)}, u32[]{:S(2)}) collective-permute-start(f32[128,1024]{1,0:T(8,128)S(1)} %get-tuple-element.172.refs_4_), channel_id=1, source_target_pairs={{0,1},{1,0},{2,3},{3,2},{4,5},{5,4},{6,7},{7,6},{8,9},{9,8},{10,11... | collective-permute-start | bytes 1572872 | tf_op jit(solution)/shard_map/ppermute | solution.py:957
  6.4 45.0 %collective-permute-start = (f32[128,1024]{1,0:T(8,128)S(1)}, f32[128,1024]{1,0:T(8,128)}, u32[]{:S(2)}, u32[]{:S(2)}) collective-permute-start(f32[128,1024]{1,0:T(8,128)S(1)} %get-tuple-element.172.refs_4_), channel_id=1, source_target_pairs={{0,16},{16,0},{1,17},{17,1},{2,18},{18,2},{3,19},{19,3},{4,20},{20... | collective-permute-start | bytes 1572872 | tf_op jit(solution)/shard_map/ppermute | solution.py:957
  9.0 21.5 %all-to-all-start = ((f32[16,72,128]{2,1,0:T(8,128)}), f32[16,72,128]{2,1,0:T(8,128)S(1)}, u32[]{:S(2)}, u32[]{:S(2)}) async-start(f32[16,72,128]{2,1,0:T(8,128)} %get-tuple-element.154), calls=%async_computation | async-start | bytes 1179648 | tf_op jit(solution)/shard_map/all_to_all | solution.py:1070
  43.0 19.1 %all-to-all-start.1 = ((f32[16,64,128]{2,1,0:T(8,128)}), f32[16,64,128]{2,1,0:T(8,128)}, u32[]{:S(2)}, u32[]{:S(2)}) async-start(f32[16,64,128]{2,1,0:T(8,128)} %bitcast.9), calls=%async_computation.1 | async-start | bytes 1048576 | tf_op jit(solution)/shard_map/all_to_all | solution.py:1070
  72.1 22.5 %collective-permute-start.3 = (f32[128,1024]{1,0:T(8,128)}, f32[128,1024]{1,0:T(8,128)S(1)}, u32[]{:S(2)}, u32[]{:S(2)}) collective-permute-start(f32[128,1024]{1,0:T(8,128)} %get-tuple-element.167), channel_id=1, source_target_pairs={{0,16},{16,0},{1,17},{17,1},{2,18},{18,2},{3,19},{19,3},{4,20},{20... | collective-permute-start | bytes 1572872 | tf_op jit(solution)/shard_map/ppermute | solution.py:957
  72.7 24.9 %collective-permute-start.4 = (f32[128,1024]{1,0:T(8,128)}, f32[128,1024]{1,0:T(8,128)}, u32[]{:S(2)}, u32[]{:S(2)}) collective-permute-start(f32[128,1024]{1,0:T(8,128)} %get-tuple-element.168), channel_id=1, source_target_pairs={{0,16},{16,0},{1,17},{17,1},{2,18},{18,2},{3,19},{19,3},{4,20},{20... | collective-permute-start | bytes 1572872 | tf_op jit(solution)/shard_map/ppermute | solution.py:957
  89.9 20.0 %all-to-all-start.2 = ((f32[16,72,128]{2,1,0:T(8,128)}), f32[16,72,128]{2,1,0:T(8,128)S(1)}, u32[]{:S(2)}, u32[]{:S(2)}) async-start(f32[16,72,128]{2,1,0:T(8,128)} %get-tuple-element.180), calls=%async_computation.2 | async-start | bytes 1179648 | tf_op jit(solution)/shard_map/all_to_all | solution.py:1070
  98.5 58.8 %collective-permute-start.9 = (f32[128,4608]{1,0:T(8,128)}, f32[128,4608]{1,0:T(8,128)}, u32[]{:S(2)}, u32[]{:S(2)}) collective-permute-start(f32[128,4608]{1,0:T(8,128)} %get-tuple-element.185), channel_id=1, source_target_pairs={{0,4},{1,5},{2,6},{3,7},{4,0},{5,1},{6,2},{7,3},{8,12},{9,13},{10,... | collective-permute-start | bytes 7077896 | tf_op jit(solution)/shard_map/ppermute | solution.py:957
  100.3 57.1 %collective-permute-start.10 = (f32[128,4608]{1,0:T(8,128)}, f32[128,4608]{1,0:T(8,128)}, u32[]{:S(2)}, u32[]{:S(2)}) collective-permute-start(f32[128,4608]{1,0:T(8,128)} %get-tuple-element.214.refs_0_), channel_id=1, source_target_pairs={{0,1},{1,0},{2,3},{3,2},{4,5},{5,4},{6,7},{7,6},{8,9},{9,8},{10,11... | collective-permute-start | bytes 7077896 | tf_op jit(solution)/shard_map/ppermute | solution.py:957
  100.5 42.1 %collective-permute-start.8 = (f32[128,2048]{1,0:T(8,128)}, f32[128,2048]{1,0:T(8,128)}, u32[]{:S(2)}, u32[]{:S(2)}) collective-permute-start(f32[128,2048]{1,0:T(8,128)} %get-tuple-element.184), channel_id=1, source_target_pairs={{0,16},{16,0},{1,17},{17,1},{2,18},{18,2},{3,19},{19,3},{4,20},{20... | collective-permute-start | bytes 3145736 | tf_op jit(solution)/shard_map/ppermute | solution.py:957
  107.2 50.1 %collective-permute-start.7 = (f32[4,128,1024]{2,1,0:T(8,128)}, f32[4,128,1024]{2,1,0:T(8,128)}, u32[]{:S(2)}, u32[]{:S(2)}) collective-permute-start(f32[4,128,1024]{2,1,0:T(8,128)} %get-tuple-element.179), channel_id=1, source_target_pairs={{0,2},{1,3},{2,0},{3,1},{4,6},{5,7},{6,4},{7,5},{8,10},{9,11},{10,... | collective-permute-start | bytes 6291464 | tf_op jit(solution)/shard_map/ppermute | solution.py:957
  163.0 29.3 %collective-permute-start.16 = (f32[2,128,1024]{2,1,0:T(8,128)}, f32[2,128,1024]{2,1,0:T(8,128)}, u32[]{:S(2)}, u32[]{:S(2)}) collective-permute-start(f32[2,128,1024]{2,1,0:T(8,128)} %get-tuple-element.364), channel_id=1, source_target_pairs={{0,4},{1,5},{2,6},{3,7},{4,0},{5,1},{6,2},{7,3},{8,12},{9,13},{10,... | collective-permute-start | bytes 3145736 | tf_op jit(solution)/shard_map/ppermute | solution.py:957
  170.5 30.5 %collective-permute-start.20 = (f32[4,64,1024]{2,1,0:T(8,128)}, f32[4,64,1024]{2,1,0:T(8,128)}, u32[]{:S(2)}, u32[]{:S(2)}) collective-permute-start(f32[4,64,1024]{2,1,0:T(8,128)} %get-tuple-element.230), channel_id=1, source_target_pairs={{0,2},{1,3},{2,0},{3,1},{4,6},{5,7},{6,4},{7,5},{8,10},{9,11},{10,... | collective-permute-start | bytes 3145736 | tf_op jit(solution)/shard_map/ppermute | solution.py:957
  179.2 35.1 %collective-permute-start.14 = (f32[4,64,1024]{2,1,0:T(8,128)}, f32[4,64,1024]{2,1,0:T(8,128)}, u32[]{:S(2)}, u32[]{:S(2)}) collective-permute-start(f32[4,64,1024]{2,1,0:T(8,128)} %get-tuple-element.221), channel_id=1, source_target_pairs={{0,16},{16,0},{1,17},{17,1},{2,18},{18,2},{3,19},{19,3},{4,20},{20... | collective-permute-start | bytes 3145736 | tf_op jit(solution)/shard_map/ppermute | solution.py:957
  179.7 24.4 %all-to-all-start.3 = ((f32[16,64,128]{2,1,0:T(8,128)}), f32[16,64,128]{2,1,0:T(8,128)S(1)}, u32[]{:S(2)}, u32[]{:S(2)}) async-start(f32[16,64,128]{2,1,0:T(8,128)} %bitcast.21), calls=%async_computation.3 | async-start | bytes 1048576 | tf_op jit(solution)/shard_map/all_to_all | solution.py:1070
  194.9 31.0 %collective-permute-start.17 = (f32[1,128,1024]{2,1,0:T(8,128)}, f32[1,128,1024]{2,1,0:T(8,128)}, u32[]{:S(2)}, u32[]{:S(2)}) collective-permute-start(f32[1,128,1024]{2,1,0:T(8,128)} %select_bitcast_fusion.4), channel_id=1, source_target_pairs={{0,8},{1,9},{2,10},{3,11},{4,12},{5,13},{6,14},{7,15},{8,0},{9,1},... | collective-permute-start | bytes 1572872 | tf_op jit(solution)/shard_map/ppermute | solution.py:957
  203.4 33.8 %collective-permute-start.21 = (f32[2,64,1024]{2,1,0:T(8,128)}, f32[2,64,1024]{2,1,0:T(8,128)}, u32[]{:S(2)}, u32[]{:S(2)}) collective-permute-start(f32[2,64,1024]{2,1,0:T(8,128)} %select_bitcast_fusion.3), channel_id=1, source_target_pairs={{0,4},{1,5},{2,6},{3,7},{4,0},{5,1},{6,2},{7,3},{8,12},{9,13},{10,... | collective-permute-start | bytes 1572872 | tf_op jit(solution)/shard_map/ppermute | solution.py:957
  203.8 33.4 %collective-permute-start.13 = (f32[4,64,1024]{2,1,0:T(8,128)}, f32[4,64,1024]{2,1,0:T(8,128)}, u32[]{:S(2)}, u32[]{:S(2)}) collective-permute-start(f32[4,64,1024]{2,1,0:T(8,128)} %get-tuple-element.217), channel_id=1, source_target_pairs={{0,16},{16,0},{1,17},{17,1},{2,18},{18,2},{3,19},{19,3},{4,20},{20... | collective-permute-start | bytes 3145736 | tf_op jit(solution)/shard_map/ppermute | solution.py:957
  205.1 32.0 %all-to-all-start.4 = ((f32[8,72,256]{2,1,0:T(8,128)}), f32[8,72,256]{2,1,0:T(8,128)S(1)}, u32[]{:S(2)}, u32[]{:S(2)}) async-start(f32[8,72,256]{2,1,0:T(8,128)} %broadcast_in_dim.28), calls=%async_computation.4 | async-start | bytes 1179648 | tf_op jit(solution)/shard_map/all_to_all | solution.py:1156
  217.1 20.1 %collective-permute-start.15 = (f32[2,64,1024]{2,1,0:T(8,128)}, f32[2,64,1024]{2,1,0:T(8,128)}, u32[]{:S(2)}, u32[]{:S(2)}) collective-permute-start(f32[2,64,1024]{2,1,0:T(8,128)} %select_bitcast_fusion.5), channel_id=1, source_target_pairs={{0,2},{1,3},{2,0},{3,1},{4,6},{5,7},{6,4},{7,5},{8,10},{9,11},{10,... | collective-permute-start | bytes 1572872 | tf_op jit(solution)/shard_map/ppermute | solution.py:957
  240.2 20.5 %collective-permute-start.24 = (f32[1,64,1024]{2,1,0:T(8,128)S(1)}, f32[1,64,1024]{2,1,0:T(8,128)S(1)}, u32[]{:S(2)}, u32[]{:S(2)}) collective-permute-start(f32[1,64,1024]{2,1,0:T(8,128)S(1)} %select_bitcast_fusion.7), channel_id=1, source_target_pairs={{0,8},{1,9},{2,10},{3,11},{4,12},{5,13},{6,14},{7,15},{8,0},{9,1},... | collective-permute-start | bytes 786440 | tf_op jit(solution)/shard_map/ppermute | solution.py:957
  242.9 21.6 %collective-permute-start.22 = (f32[2,64,1024]{2,1,0:T(8,128)S(1)}, f32[2,64,1024]{2,1,0:T(8,128)S(1)}, u32[]{:S(2)}, u32[]{:S(2)}) collective-permute-start(f32[2,64,1024]{2,1,0:T(8,128)S(1)} %select_bitcast_fusion.2), channel_id=1, source_target_pairs={{0,2},{1,3},{2,0},{3,1},{4,6},{5,7},{6,4},{7,5},{8,10},{9,11},{10,... | collective-permute-start | bytes 1572872 | tf_op jit(solution)/shard_map/ppermute | solution.py:957
  244.4 20.1 %collective-permute-start.25 = (f32[128,1024]{1,0:T(8,128)S(1)}, f32[128,1024]{1,0:T(8,128)S(1)}, u32[]{:S(2)}, u32[]{:S(2)}) collective-permute-start(f32[128,1024]{1,0:T(8,128)S(1)} %fusion.3.refs_0_), channel_id=1, source_target_pairs={{0,16},{16,0},{1,17},{17,1},{2,18},{18,2},{3,19},{19,3},{4,20},{20... | collective-permute-start | bytes 1572872 | tf_op jit(solution)/shard_map/ppermute | solution.py:957
  246.6 18.0 %collective-permute-start.23 = (f32[1,64,1024]{2,1,0:T(8,128)S(1)}, f32[1,64,1024]{2,1,0:T(8,128)S(1)}, u32[]{:S(2)}, u32[]{:S(2)}) collective-permute-start(f32[1,64,1024]{2,1,0:T(8,128)S(1)} %select_bitcast_fusion.8), channel_id=1, source_target_pairs={{0,8},{1,9},{2,10},{3,11},{4,12},{5,13},{6,14},{7,15},{8,0},{9,1},... | collective-permute-start | bytes 786440 | tf_op jit(solution)/shard_map/ppermute | solution.py:957
  (76 other events, 521.1 us)
